TPU v7x, 256 devices: a whole 4x4x8 slice. The times are simulated.
256 devices in a mesh: grp: 4 (over y), wide: 64 (over z, x, core).
Axes of the slice: x: 4, y: 4, z: 8, core: 2. Of those that a mesh axis runs over, the one named last changes fastest.
Arguments:
- coeff: float32 [2048, 6144], P(('grp', 'wide')), may hold values from -6 to 6
- beta_blocks: float32 [96, 128, 128], replicated, may hold values from -0.5 to 0.5
- block_list: int32 [2, 96], replicated, may hold values from 0 to 47
- alpha_blocks: float32 [256, 4, 8, 8], P(('grp', 'wide')), may hold values from -2 to 2
- partner_mask: int32 [256, 4], P(('grp', 'wide')), may hold values 0 or 1
- exc_source: int32 [90, 2048], P(None, 'grp'), may hold values from 0 to 2047
- exc_pair: int32 [90, 2048], P(None, 'grp'), may hold values from 0 to 323
- exc_parity: int32 [90, 2048], P(None, 'grp'), may hold values from 0 to 1
- occupation: int32 [18, 6144], P(None, 'wide'), may hold values 0 or 1
- coulomb: float32 [324, 18], replicated, may hold values from -0.2 to 0.2
Outputs:
- sigma: float32 [2048, 6144], P(('grp', 'wide'))
Inputs may be any that keep to these rules, and one draw needn't show every extreme that they name: `exc_source`: any alpha string.
All inputs are finite; a program needn't handle non-finite values. No bound on the sum of `partner_mask` or of `occupation` on one device may be relied on, other than what follows from the above.
Results may differ from a plain program's by a relative error of at most 0.0003.
Values sent between devices are 32-bit elements; how exact they have to be, the bound alone decides.
No kernel may reach another device: no remote copies, remote signals or barrier semaphores. Data moves between devices by JAX's collectives and lax.ppermute only.
A program may use at most 128 MiB of HBM per device.

v0:
```python
import jax
import jax.numpy as jnp
from jax import lax
from jax.sharding import PartitionSpec as P

HIGH = lax.Precision.HIGHEST


def per_device(
    coeff,
    beta_blocks,
    block_list,
    alpha_blocks,
    partner_mask,
    exc_source,
    exc_pair,
    exc_parity,
    occupation,
    coulomb,
):
    alpha_rows, beta_width = coeff.shape
    block_size = beta_blocks.shape[1]
    block_count = beta_width // block_size
    blocked = coeff.reshape(alpha_rows, block_count, block_size)
    block_ids = jnp.arange(block_count, dtype=jnp.int32)
    choosing = (block_list[0][:, None] == block_ids[None, :]).astype(jnp.float32)
    picked = jnp.einsum("rnk,pn->rpk", blocked, choosing, precision=HIGH)
    applied = jnp.einsum("rpk,pkl->rpl", picked, beta_blocks, precision=HIGH)
    placing = (block_list[1][:, None] == block_ids[None, :]).astype(jnp.float32)
    same_beta = jnp.einsum("rpl,pn->rnl", applied, placing, precision=HIGH).reshape(
        alpha_rows, beta_width
    )
    masked = alpha_blocks[0] * partner_mask[0][:, None, None].astype(jnp.float32)
    group_count = masked.shape[0]
    coupling = masked.transpose(1, 0, 2).reshape(alpha_rows, group_count * alpha_rows)
    same_alpha = jnp.dot(
        coupling,
        lax.all_gather(coeff, "grp", axis=0, tiled=True),
        precision=HIGH,
        preferred_element_type=jnp.float32,
    )
    beta_major = lax.all_to_all(coeff, "wide", split_axis=1, concat_axis=0, tiled=True)
    every_string = lax.all_gather(beta_major, "grp", axis=0, tiled=True)
    group_rows, slice_width = beta_major.shape
    replace_count = exc_source.shape[0]
    weights_local = jnp.dot(
        coulomb, occupation.astype(jnp.float32), precision=HIGH, preferred_element_type=jnp.float32
    )
    phases = 1.0 - 2.0 * exc_parity.astype(jnp.float32)
    row_block = 256
    turns = group_rows // row_block

    def one_block(entry):
        sources, pairs, signs = entry
        fetched = jnp.take(every_string, sources, axis=0)
        factor = jnp.take(weights_local, pairs, axis=0)
        return jnp.sum(signs[:, :, None] * factor * fetched, axis=1)

    mixed_local = lax.map(
        one_block,
        (
            exc_source.T.reshape(turns, row_block, replace_count),
            exc_pair.T.reshape(turns, row_block, replace_count),
            phases.T.reshape(turns, row_block, replace_count),
        ),
    ).reshape(group_rows, slice_width)
    mixed = lax.all_to_all(mixed_local, "wide", split_axis=0, concat_axis=1, tiled=True)
    return same_beta + same_alpha + mixed


def solution(mesh):
    in_specs = (
        P(("grp", "wide"), None),
        P(),
        P(),
        P(("grp", "wide"), None, None, None),
        P(("grp", "wide"), None),
        P(None, "grp"),
        P(None, "grp"),
        P(None, "grp"),
        P(None, "wide"),
        P(),
    )
    out_specs = P(("grp", "wide"), None)
    return jax.shard_map(
        per_device, mesh=mesh, in_specs=in_specs, out_specs=out_specs, check_vma=False
    )
```

profile of v0, /device:TPU:2, one launch (start us, length us, event | category | flops | bytes accessed | tf_op | source)
XLA Modules:
  0.0 411.7 jit_solution(13386952593888487022)
XLA Ops:
  0.0 0.0 copy-start
  0.0 1.1 all_to_all.28
  1.1 0.9 copy.35
  1.9 12.0 %all-to-all-start = ((f32[8,64,96]{2,0,1:T(8,128)}), f32[8,64,96]{2,0,1:T(8,128)S(1)}, u32[]{:S(2)}, u32[]{:S(2)}) async-start(f32[8,64,96]{2,0,1:T(8,128)} %copy.35), calls=%async_computation | async-start | bytes 524288 | tf_op jit(solution)/shard_map/all_to_all | solution.py:42
  14.0 1.0 subtract_bitcast_fusion
  14.9 0.1 copy.32
  15.0 1.1 copy.33
  16.1 1.1 copy.34
  17.2 0.7 convert_bitcast_fusion
  17.8 0.8 fusion.8
  18.6 0.7 reshape.108
  19.3 1.3 slice_bitcast_fusion.1
  20.6 0.0 copy-done
  20.6 1.2 fusion.9
  21.8 1.3 convolution_bitcast_fusion.1
  23.1 8.1 %convolution_bitcast_fusion = f32[8,96,128]{2,0,1:T(8,128)} fusion(f32[96,128,128]{2,1,0:T(8,128)} %param.13, f32[8,96,128]{2,1,0:T(8,128)S(1)} %convolution_bitcast_fusion.1), kind=kOutput, calls=%fused_computation.15 | convolution fusion | flops 150994944 | bytes 7077888 | tf_op jit(solution)/shard_map/rpk,pkl->rpl/dot_general | solution.py:28
  31.2 0.0 all-to-all-done
  31.2 15.6 %all_gather.7 = f32[2048,96]{1,0:T(8,128)S(1)} all-gather(f32[512,96]{1,0:T(8,128)S(1)} %bitcast.80), channel_id=1, replica_groups=mesh['grp'=4,'wide'=64] {'grp'}, dimensions={0}, use_global_device_ids=true | all-gather | bytes 983040 | tf_op jit(solution)/shard_map/all_gather | solution.py:43
  46.8 337.8 %while.10 = (s32[]{:T(128)}, f32[2,256,96]{1,2,0:T(8,128)S(1)}, f32[2,256,90]{2,1,0:T(8,128)S(1)}, s32[2,256,90]{2,1,0:T(8,128)S(1)}, f32[324,96]{1,0:T(8,128)S(...) while((s32[]{:T(128)}, f32[2,256,96]{1,2,0:T(8,128)S(1)}, ...), condition=%wide.region_2.3_spmd, body=%wide.region_0.2_spmd.sunk | while | flops 11496450 | bytes 126005352 | solution.py:59
  46.9 0.1 reshape.144
  47.0 42.9 %gather_fusion = f32[23040,96]{1,0:T(8,128)} fusion(f32[2048,96]{1,0:T(8,128)S(1)} %get-tuple-element.157, s32[23552]{0:T(1024)S(1)} %pad_clamp_fusion.4), kind=kCustom, calls=%fused_computation.1.clone.1 | custom fusion | bytes 17786880 | tf_op jit(solution)/shard_map/while/body/eval_jaxpr/jit(_take)/gather | solution.py:55
  90.0 11.6 %copy.50 = f32[23040,96]{0,1:T(8,128)} copy(f32[23040,96]{1,0:T(8,128)} %gather_fusion) | data formatting | bytes 17694720 | tf_op jit(solution)/shard_map/while/body/eval_jaxpr/jit(_take)/gather | solution.py:55
  101.6 24.6 %reshape.145 = f32[256,90,96]{1,0,2:T(8,128)} reshape(f32[23040,96]{0,1:T(8,128)} %copy.50) | data formatting | bytes 17694720 | tf_op jit(solution)/shard_map/while/body/eval_jaxpr/jit(_take)/gather | solution.py:55
  126.2 0.1 reshape.146
  126.3 42.9 %gather_fusion.1 = f32[23040,96]{1,0:T(8,128)} fusion(f32[324,96]{1,0:T(8,128)S(1)} %get-tuple-element.155, s32[23552]{0:T(1024)S(1)} %pad_clamp_fusion.5), kind=kCustom, calls=%fused_computation.clone.1 | custom fusion | bytes 17786880 | tf_op jit(solution)/shard_map/while/body/eval_jaxpr/jit(_take)/gather | solution.py:56
  169.2 11.6 %copy.51 = f32[23040,96]{0,1:T(8,128)} copy(f32[23040,96]{1,0:T(8,128)} %gather_fusion.1) | data formatting | bytes 17694720 | tf_op jit(solution)/shard_map/while/body/eval_jaxpr/jit(_take)/gather | solution.py:56
  180.8 24.6 %reshape.147 = f32[256,90,96]{1,0,2:T(8,128)} reshape(f32[23040,96]{0,1:T(8,128)} %copy.51) | data formatting | bytes 17694720 | tf_op jit(solution)/shard_map/while/body/eval_jaxpr/jit(_take)/gather | solution.py:56
  205.4 0.1 compare_and_fusion.3
  205.5 10.2 %multiply_reduce_fusion.2 = f32[256,96]{0,1:T(8,128)S(1)} fusion(f32[256,90,96]{1,0,2:T(8,128)} %reshape.145, f32[256,90,96]{1,0,2:T(8,128)} %reshape.147, f32[256,90]{1,0:T(8,128)S(1)} %dynamic-slice_bitcast_fusion.2, pred[256,90]{1,0:T(8,128)(4,1)S(1)} %get-tuple-element.133, pred[256,90]{1,0:T(8,128)(4,1)S(1)} %get-tuple-element.134), kind=kLoop, calls=%fused_computation.2.clone.1 | loop fusion | flops 11034624 | bytes 17931264 | tf_op jit(solution)/shard_map/while/body/eval_jaxpr/reduce_sum | solution.py:57
  215.8 0.1 reshape.144
  216.0 42.9 %gather_fusion = f32[23040,96]{1,0:T(8,128)} fusion(f32[2048,96]{1,0:T(8,128)S(1)} %get-tuple-element.157, s32[23552]{0:T(1024)S(1)} %pad_clamp_fusion.4), kind=kCustom, calls=%fused_computation.1.clone.1 | custom fusion | bytes 17786880 | tf_op jit(solution)/shard_map/while/body/eval_jaxpr/jit(_take)/gather | solution.py:55
  258.9 11.6 %copy.50 = f32[23040,96]{0,1:T(8,128)} copy(f32[23040,96]{1,0:T(8,128)} %gather_fusion) | data formatting | bytes 17694720 | tf_op jit(solution)/shard_map/while/body/eval_jaxpr/jit(_take)/gather | solution.py:55
  270.5 24.6 %reshape.145 = f32[256,90,96]{1,0,2:T(8,128)} reshape(f32[23040,96]{0,1:T(8,128)} %copy.50) | data formatting | bytes 17694720 | tf_op jit(solution)/shard_map/while/body/eval_jaxpr/jit(_take)/gather | solution.py:55
  295.1 0.1 reshape.146
  295.3 42.9 %gather_fusion.1 = f32[23040,96]{1,0:T(8,128)} fusion(f32[324,96]{1,0:T(8,128)S(1)} %get-tuple-element.155, s32[23552]{0:T(1024)S(1)} %pad_clamp_fusion.5), kind=kCustom, calls=%fused_computation.clone.1 | custom fusion | bytes 17786880 | tf_op jit(solution)/shard_map/while/body/eval_jaxpr/jit(_take)/gather | solution.py:56
  338.1 11.6 %copy.51 = f32[23040,96]{0,1:T(8,128)} copy(f32[23040,96]{1,0:T(8,128)} %gather_fusion.1) | data formatting | bytes 17694720 | tf_op jit(solution)/shard_map/while/body/eval_jaxpr/jit(_take)/gather | solution.py:56
  349.8 24.6 %reshape.147 = f32[256,90,96]{1,0,2:T(8,128)} reshape(f32[23040,96]{0,1:T(8,128)} %copy.51) | data formatting | bytes 17694720 | tf_op jit(solution)/shard_map/while/body/eval_jaxpr/jit(_take)/gather | solution.py:56
  374.4 0.1 compare_and_fusion.3
  374.4 10.2 %multiply_reduce_fusion.2 = f32[256,96]{0,1:T(8,128)S(1)} fusion(f32[256,90,96]{1,0,2:T(8,128)} %reshape.145, f32[256,90,96]{1,0,2:T(8,128)} %reshape.147, f32[256,90]{1,0:T(8,128)S(1)} %dynamic-slice_bitcast_fusion.2, pred[256,90]{1,0:T(8,128)(4,1)S(1)} %get-tuple-element.133, pred[256,90]{1,0:T(8,128)(4,1)S(1)} %get-tuple-element.134), kind=kLoop, calls=%fused_computation.2.clone.1 | loop fusion | flops 11034624 | bytes 17931264 | tf_op jit(solution)/shard_map/while/body/eval_jaxpr/reduce_sum | solution.py:57
  384.7 0.0 copy-start.1
  384.7 0.8 copy.37
  385.5 10.3 %all-to-all-start.1 = ((f32[64,8,96]{2,1,0:T(8,128)}), f32[64,8,96]{2,1,0:T(8,128)S(1)}, u32[]{:S(2)}, u32[]{:S(2)}) async-start(f32[64,8,96]{2,1,0:T(8,128)} %bitcast.25), calls=%async_computation.1 | async-start | bytes 524288 | tf_op jit(solution)/shard_map/all_to_all | solution.py:67
  395.8 0.3 convolution_bitcast_fusion.2
  396.2 14.2 %all_gather.6 = f32[32,6144]{1,0:T(8,128)S(1)} all-gather(f32[8,6144]{1,0:T(8,128)S(1)} %copy-done.2), channel_id=1, replica_groups=mesh['grp'=4,'wide'=64] {'grp'}, dimensions={0}, use_global_device_ids=true | all-gather | bytes 983040 | tf_op jit(solution)/shard_map/all_gather | solution.py:38
  410.3 0.0 all-to-all-done.1
  410.3 0.1 copy.38
  410.4 0.2 all_to_all.35
  410.5 1.2 fusion
  (21 shorter events, 0.2 us)
Async XLA Ops:
  0.0 20.6 %copy-start = (f32[324,18]{0,1:T(8,128)S(1)}, f32[324,18]{0,1:T(8,128)}, u32[]{:S(2)}) copy-start(f32[324,18]{0,1:T(8,128)} %param.21) | copy-start | bytes 69988
  1.9 29.3 %all-to-all-start = ((f32[8,64,96]{2,0,1:T(8,128)}), f32[8,64,96]{2,0,1:T(8,128)S(1)}, u32[]{:S(2)}, u32[]{:S(2)}) async-start(f32[8,64,96]{2,0,1:T(8,128)} %copy.35), calls=%async_computation | async-start | bytes 524288 | tf_op jit(solution)/shard_map/all_to_all | solution.py:42
  46.8 349.0 %copy-start.3 = (f32[8,96,128]{2,0,1:T(8,128)S(1)}, f32[8,96,128]{2,0,1:T(8,128)}, u32[]{:S(2)}) copy-start(f32[8,96,128]{2,0,1:T(8,128)} %convolution_bitcast_fusion) | copy-start | bytes 1179652
  46.8 349.0 %copy-start.5 = (s32[96]{0:T(128)S(1)}, s32[96]{0:T(128)}, u32[]{:S(2)}) copy-start(s32[96]{0:T(128)} %get-tuple-element.82) | copy-start | bytes 1156
  46.8 349.3 %copy-start.2 = (f32[8,6144]{1,0:T(8,128)S(1)}, f32[8,6144]{1,0:T(8,128)}, u32[]{:S(2)}) copy-start(f32[8,6144]{1,0:T(8,128)} %param.12) | copy-start | bytes 589828
  46.8 363.7 %copy-start.4 = (f32[8,32]{1,0:T(8,128)S(1)}, f32[8,32]{1,0:T(8,128)}, u32[]{:S(2)}) copy-start(f32[8,32]{1,0:T(8,128)} %reshape.108) | copy-start | bytes 3076
  384.7 27.1 %copy-start.1 = (f32[324,18]{0,1:T(8,128)S(1)}, f32[324,18]{0,1:T(8,128)}, u32[]{:S(2)}) copy-start(f32[324,18]{0,1:T(8,128)} %param.21) | copy-start | bytes 69988
  385.5 24.8 %all-to-all-start.1 = ((f32[64,8,96]{2,1,0:T(8,128)}), f32[64,8,96]{2,1,0:T(8,128)S(1)}, u32[]{:S(2)}, u32[]{:S(2)}) async-start(f32[64,8,96]{2,1,0:T(8,128)} %bitcast.25), calls=%async_computation.1 | async-start | bytes 524288 | tf_op jit(solution)/shard_map/all_to_all | solution.py:67
where the time goes:
time: 414 us; the launch traced here: 412 us
  local copies, waits for them, and re-layouts  324 us (78%)
  blocking collectives  29.7 us (7%)
  other arithmetic  23.1 us (6%)
  starting transfers between devices  22.3 us (5%)
  matrix products  12.1 us (3%)
    gather x6, local copies, waits for them, and re-layouts, one_block(): fetched = jnp.take(every_string, sources, axis=0)  158 us
    gather x6, local copies, waits for them, and re-layouts, one_block(): factor = jnp.take(weights_local, pairs, axis=0)  158 us
    reduce_sum x2, other arithmetic, one_block(): return jnp.sum(signs[:, :, None] * factor * fetched, axis=1)  20.3 us
    all_gather x1, blocking collectives, per_device(): every_string = lax.all_gather(beta_major, 'grp', axis=0, tiled=True)  15.6 us
    all_gather x1, blocking collectives, per_device(): lax.all_gather(coeff, 'grp', axis=0, tiled=True)  14.2 us
    all_to_all x1, starting transfers between devices, per_device(): lax.all_to_all(coeff, 'wide', split_axis=1, concat_axis=0, tiled=True)  12 us
    all_to_all x1, starting transfers between devices, per_device(): lax.all_to_all(mixed_local, 'wide', split_axis=0, concat_axis=1, tiled=True)  10.3 us
  transfers between devices with their start and end apart: 2, of which 0 were waited for; matrix products, arithmetic and copies ran while one was open for 4% of the time, Pallas kernels for 0%

commit v1 on v0

v1 whole, which is shorter than its diff:
```python
import functools

import jax
import jax.numpy as jnp
from jax import lax
from jax.experimental import pallas as pl
from jax.experimental.pallas import tpu as pltpu
from jax.sharding import Mesh
from jax.sharding import PartitionSpec as P

HIGH = lax.Precision.HIGHEST
RA = 8
LANES = 128
N_GRP = 4
NZ, NX, NC = 8, 4, 2
NQ = NZ * NX
COLS = 192
PAD = 8

SMEM = pl.BlockSpec(memory_space=pltpu.SMEM)
VMEM = pl.BlockSpec(memory_space=pltpu.VMEM)
ANY = pl.BlockSpec(memory_space=pl.ANY)


def pack_kernel(x_ref, o_ref):
    zeros = jnp.zeros((RA, LANES - COLS + LANES), jnp.float32)
    for j in range(NQ):
        o_ref[j, 0] = x_ref[:, COLS * j : COLS * j + LANES]
        o_ref[j, 1] = jnp.concatenate(
            [x_ref[:, COLS * j + LANES : COLS * (j + 1)], zeros], axis=1
        )


def pack(coeff):
    return pl.pallas_call(
        pack_kernel,
        out_shape=jax.ShapeDtypeStruct((NQ, 2, RA, LANES), jnp.float32),
        in_specs=[VMEM],
        out_specs=VMEM,
        name="pack",
    )(coeff)


def mixed_kernel(n_exc, row_count, c_ref, cidx_ref, widx_ref, w_ref, *rest):
    parts = rest[: 2 * N_GRP]
    o_ref, table, sem = rest[2 * N_GRP :]
    part_rows = NQ * 2 * RA
    copies = []
    for i, part in enumerate(parts):
        copy = pltpu.make_async_copy(
            part, table.at[pl.ds(i * part_rows, part_rows)], sem.at[i]
        )
        copy.start()
        copies.append(copy)
    for copy in copies:
        copy.wait()
    core = c_ref[0]
    span = row_count - 2 * RA + 1

    def block(q, carry):
        start = q * (2 * RA) + core * RA
        for a in range(RA):
            acc = None
            for e in range(n_exc):
                base = e * row_count + a
                ci = cidx_ref.at[pl.ds(base, span + RA)][start]
                wi = widx_ref.at[pl.ds(base, span + RA)][start]
                term = (
                    table[pl.ds(ci, 2, stride=RA), :]
                    * w_ref[pl.ds(wi, 2, stride=RA), :]
                )
                acc = term if acc is None else acc + term
            o_ref[pl.ds(q * (2 * RA) + a, 2, stride=RA), :] = acc
        return carry

    lax.fori_loop(0, NQ, block, 0)


def mixed_call(core, cidx, widx, wtab, parts, n_exc, row_count):
    part_rows = NQ * 2 * RA
    return pl.pallas_call(
        functools.partial(mixed_kernel, n_exc, row_count),
        out_shape=jax.ShapeDtypeStruct((part_rows, LANES), jnp.float32),
        in_specs=[SMEM, SMEM, SMEM, VMEM] + [ANY] * len(parts),
        out_specs=VMEM,
        scratch_shapes=[
            pltpu.VMEM((2 * N_GRP * part_rows, LANES), jnp.float32),
            pltpu.SemaphoreType.DMA((2 * N_GRP,)),
        ],
        compiler_params=pltpu.CompilerParams(vmem_limit_bytes=32 << 20),
        cost_estimate=pl.CostEstimate(
            flops=2 * n_exc * row_count * COLS // 2,
            bytes_accessed=8 << 20,
            transcendentals=0,
        ),
        name="mixed",
    )(core, cidx, widx, wtab, *parts)


def final_kernel(m_ref, b_ref, k_ref, x0, x1, x2, x3, o_ref):
    k = k_ref[...]
    xs = (x0, x1, x2, x3)
    for j in range(NQ):
        lo = COLS * j
        a = m_ref[j, 0]
        b = m_ref[j, 1][:, : COLS - LANES]
        o_ref[:, lo : lo + COLS] = jnp.concatenate([a, b], axis=1)
    width = 1024
    for t in range(b_ref.shape[1] // width):
        cols = slice(t * width, (t + 1) * width)
        stacked = jnp.concatenate([x[:, cols] for x in xs], axis=0)
        alpha = jnp.dot(k, stacked, precision=HIGH, preferred_element_type=jnp.float32)
        o_ref[:, cols] = o_ref[:, cols] + b_ref[:, cols] + alpha


def final_call(mixed, same_beta, coupling, xs):
    return pl.pallas_call(
        final_kernel,
        out_shape=jax.ShapeDtypeStruct(same_beta.shape, jnp.float32),
        in_specs=[VMEM] * (3 + len(xs)),
        out_specs=VMEM,
        name="final",
    )(mixed, same_beta, coupling, *xs)


def per_device(
    coeff,
    beta_blocks,
    block_list,
    alpha_blocks,
    partner_mask,
    exc_source,
    exc_pair,
    exc_parity,
    occupation,
    coulomb,
):
    g = lax.axis_index("grp")
    c = lax.axis_index("c")
    alpha_rows, beta_width = coeff.shape
    n_exc, row_count = exc_source.shape
    n_pair = coulomb.shape[0]

    def shift(value, k):
        return lax.ppermute(
            value, "grp", [(i, (i - k) % N_GRP) for i in range(N_GRP)]
        )

    def swap(value):
        return lax.ppermute(value, "c", [(0, 1), (1, 0)])

    packed = pack(coeff)
    own = lax.all_to_all(packed, ("z", "x"), split_axis=0, concat_axis=0, tiled=True)
    own = own.reshape(NQ * 2 * RA, LANES)
    near = [own] + [shift(own, k) for k in range(1, N_GRP)]
    parts = near + [swap(v) for v in near]

    other_occ = swap(occupation)
    first = jnp.where(c == 0, occupation, other_occ)
    second = jnp.where(c == 0, other_occ, occupation)
    occ = jnp.concatenate([first, second], axis=1).astype(jnp.float32)
    weights = jnp.dot(coulomb, occ, precision=HIGH, preferred_element_type=jnp.float32)
    signed = jnp.concatenate([weights, -weights], axis=0)
    signed = jnp.pad(signed, ((0, 0), (0, 2 * LANES - COLS)))
    wtab = (
        signed.reshape(2 * n_pair // RA, RA, 2, LANES)
        .transpose(0, 2, 1, 3)
        .reshape(4 * n_pair, LANES)
    )

    rel_g = ((exc_source >> 9) - g) & (N_GRP - 1)
    rel_c = ((exc_source >> 3) & 1) ^ c
    pos = (rel_c * N_GRP + rel_g) * NQ + ((exc_source >> 4) & (NQ - 1))
    cidx = (pos * (2 * RA) + (exc_source & (RA - 1))).reshape(-1)
    pair = exc_pair + n_pair * exc_parity
    widx = ((pair >> 3) * (2 * RA) + (pair & (RA - 1))).reshape(-1)

    mixed_local = mixed_call(
        c.reshape(1).astype(jnp.int32), cidx, widx, wtab, parts, n_exc, row_count
    )
    mixed = lax.all_to_all(
        mixed_local.reshape(NQ, 2, RA, LANES),
        ("z", "x"),
        split_axis=0,
        concat_axis=0,
        tiled=True,
    )

    block_size = beta_blocks.shape[1]
    block_count = beta_width // block_size
    blocked = coeff.reshape(alpha_rows, block_count, block_size)
    block_ids = jnp.arange(block_count, dtype=jnp.int32)
    choosing = (block_list[0][:, None] == block_ids[None, :]).astype(jnp.float32)
    picked = jnp.einsum("rnk,pn->rpk", blocked, choosing, precision=HIGH)
    applied = jnp.einsum("rpk,pkl->rpl", picked, beta_blocks, precision=HIGH)
    placing = (block_list[1][:, None] == block_ids[None, :]).astype(jnp.float32)
    same_beta = jnp.einsum("rpl,pn->rnl", applied, placing, precision=HIGH).reshape(
        alpha_rows, beta_width
    )

    masked = alpha_blocks[0] * partner_mask[0][:, None, None].astype(jnp.float32)
    masked = jnp.roll(masked, -g, axis=0)
    coupling = masked.transpose(1, 0, 2).reshape(alpha_rows, N_GRP * alpha_rows)
    rows = [coeff] + [shift(coeff, k) for k in range(1, N_GRP)]
    return final_call(mixed, same_beta, coupling, rows)


def solution(mesh):
    fine = Mesh(mesh.devices.reshape(N_GRP, NZ, NX, NC), ("grp", "z", "x", "c"))
    wide = ("z", "x", "c")
    every = ("grp",) + wide
    in_specs = (
        P(every, None),
        P(),
        P(),
        P(every, None, None, None),
        P(every, None),
        P(None, "grp"),
        P(None, "grp"),
        P(None, "grp"),
        P(None, wide),
        P(),
    )
    return jax.shard_map(
        per_device,
        mesh=fine,
        in_specs=in_specs,
        out_specs=P(every, None),
        check_vma=False,
    )
```

time: 414 us -> 107 us (0.26)
  local copies, waits for them, and re-layouts: 324 us -> 4.28 us
  Pallas kernels: 0 us -> 36.7 us
  blocking collectives: 29.7 us -> 0 us
  waiting for transfers between devices: 0.01 us -> 21.1 us
  other arithmetic: 23.1 us -> 2.29 us
  starting transfers between devices: 22.3 us -> 28.9 us
    gather x12 -> x0, local copies, waits for them, and re-layouts: 316 us -> none  [the longest x6 158 us: one_block(): fetched = jnp.take(every_string, sources, axis=0)]
    pallas_call x0 -> x3, Pallas kernels: none -> 36.7 us  [the longest x1 32.3 us: mixed_call(): pl.pallas_call(functools.partial(mixed_kernel, n_exc, row_count), out_sha...]
    all_gather x2 -> x0, blocking collectives: 29.7 us -> none  [the longest x1 15.6 us: per_device(): every_string = lax.all_gather(beta_major, 'grp', axis=0, tiled=True)]
    reduce_sum x2 -> x0, other arithmetic: 20.3 us -> none  [one_block(): return jnp.sum(signs[:, :, None] * factor * fetched, axis=1)]
    ppermute x0 -> x11, waiting for transfers between devices: none -> 12.9 us  [the longest x6 12.9 us: shift(): lax.ppermute(value, 'grp', [(i, (i - k) % N_GRP) for i in range(N_GRP)])]
    all_to_all x2, waiting for transfers between devices: 0.01 us -> 8.13 us  [the longest x1 7.92 us: per_device(): lax.all_to_all(mixed_local.reshape(NQ, 2, RA, LANES), ('z', 'x'), split_a...]
    ppermute x0 -> x11, starting transfers between devices: none -> 7.49 us  [the longest x6 7.28 us: shift(): lax.ppermute(value, 'grp', [(i, (i - k) % N_GRP) for i in range(N_GRP)])]
  transfers between devices with their start and end apart: 2 -> 13, of which waited for: 0 -> 5; matrix products, arithmetic and copies ran while one was open for 4% -> 16% of each run, Pallas kernels for 0% -> 33%
where the time goes in v1:
time: 107 us; the launch traced here: 105 us
  Pallas kernels  36.7 us (34%)
  starting transfers between devices  28.9 us (27%)
  waiting for transfers between devices  21.1 us (20%)
  matrix products  11.3 us (11%)
  local copies, waits for them, and re-layouts  4.28 us (4%)
  other arithmetic  2.29 us (2%)
    pallas_call x1, Pallas kernels, mixed_call(): pl.pallas_call(functools.partial(mixed_kernel, n_exc, row_count), out_sha...  32.3 us
    ppermute x6, waiting for transfers between devices, shift(): lax.ppermute(value, 'grp', [(i, (i - k) % N_GRP) for i in range(N_GRP)])  12.9 us
    all_to_all x1, starting transfers between devices, per_device(): lax.all_to_all(packed, ('z', 'x'), split_axis=0, concat_axis=0, tiled=True)  11.6 us
    all_to_all x1, starting transfers between devices, per_device(): lax.all_to_all(mixed_local.reshape(NQ, 2, RA, LANES), ('z', 'x'), split_a...  9.79 us
    dot_general x1, matrix products, per_device(): applied = jnp.einsum('rpk,pkl->rpl', picked, beta_blocks, precision=HIGH)  8.19 us
    all_to_all x1, waiting for transfers between devices, per_device(): lax.all_to_all(mixed_local.reshape(NQ, 2, RA, LANES), ('z', 'x'), split_a...  7.92 us
    ppermute x6, starting transfers between devices, shift(): lax.ppermute(value, 'grp', [(i, (i - k) % N_GRP) for i in range(N_GRP)])  7.28 us
    unnamed x20, local copies, waits for them, and re-layouts  2.76 us
  transfers between devices with their start and end apart: 13, of which 5 were waited for; matrix products, arithmetic and copies ran while one was open for 16% of the time, Pallas kernels for 33%

profile of v1, /device:TPU:2, one launch (start us, length us, event | category | flops | bytes accessed | tf_op | source)
XLA Modules:
  0.0 104.7 jit_solution(18433360467953238797)
XLA Ops:
  0.0 0.0 copy-start
  0.0 0.1 collective-permute-start
  0.1 3.1 %collective-permute-start.8 = (f32[8,6144]{1,0:T(8,128)}, f32[8,6144]{1,0:T(8,128)}, u32[]{:S(2)}, u32[]{:S(2)}) collective-permute-start(f32[8,6144]{1,0:T(8,128)} %x0.1), channel_id=1, source_target_pairs={{0,192},{64,0},{128,64},{192,128},{1,193},{65,1},{129,65},{193,129... | collective-permute-start | bytes 589832 | tf_op jit(solution)/shard_map/ppermute | solution.py:145
  3.2 1.8 %pack.1 = f32[32,2,8,128]{3,2,1,0:T(8,128)} custom-call(f32[8,6144]{1,0:T(8,128)} %x0.1), custom_call_target="tpu_custom_call" | custom-call | tf_op jit(solution)/shard_map/pack/pallas_call | solution.py:35
  5.0 11.6 %all-to-all-start = ((f32[32,2,8,128]{3,2,1,0:T(8,128)}), f32[32,2,8,128]{3,2,1,0:T(8,128)S(1)}, u32[]{:S(2)}, u32[]{:S(2)}) async-start(f32[32,2,8,128]{3,2,1,0:T(8,128)} %pack.1), calls=%async_computation | async-start | bytes 524288 | tf_op jit(solution)/shard_map/all_to_all | solution.py:153
  16.6 0.8 slice_bitcast_fusion.1
  17.4 1.3 %fusion.5 = f32[96,8,128]{2,0,1:T(8,128)S(1)} fusion(f32[8,48,128]{2,0,1:T(8,128)} %bitcast.47, s32[96]{0:T(128)S(1)} %get-tuple-element.8), kind=kOutput, calls=%fused_computation.9 | convolution fusion | flops 56627712 | bytes 590208 | tf_op jit(solution)/shard_map/rnk,pn->rpk/dot_general | solution.py:194
  18.6 1.1 %and_add_fusion = s32[90,512]{1,0:T(8,128)S(1)} fusion(s32[90,512]{1,0:T(8,128)} %param.16, s32[90,512]{1,0:T(8,128)} %param.17), kind=kLoop, calls=%fused_computation.11 | loop fusion | flops 276480 | bytes 552960 | tf_op jit(solution)/shard_map/add | solution.py:176
  19.7 0.0 copy-start.1
  19.7 8.2 %fusion.1 = f32[96,8,128]{2,1,0:T(8,128)} fusion(f32[96,128,128]{2,1,0:T(8,128)} %param.11, f32[96,8,128]{2,0,1:T(8,128)S(1)} %fusion.5), kind=kOutput, calls=%fused_computation.4 | convolution fusion | flops 150994944 | bytes 7077888 | tf_op jit(solution)/shard_map/rpk,pkl->rpl/dot_general | solution.py:195
  27.9 0.2 all-to-all-done
  28.1 0.7 collective-permute-start.1
  28.9 0.3 collective-permute-start.2
  29.2 1.0 collective-permute-start.3
  30.2 0.0 copy-done.3
  30.2 0.1 and_add_fusion.1
  30.3 0.0 collective-permute-done
  30.4 0.0 copy-done.7
  30.4 0.1 collective-permute-start.4
  30.5 6.9 %collective-permute-done.1.rest_1_ = f32[512,128]{1,0:T(8,128)S(1)} collective-permute-done((f32[512,128]{1,0:T(8,128)S(1)}, f32[512,128]{1,0:T(8,128)S(1)}, u32[]{:S(2)}, u32[]{:S(2)}) %collective-permute-start.1) | collective-permute-done | bytes 262176 | tf_op jit(solution)/shard_map/ppermute | solution.py:145
  37.4 0.0 collective-permute-start.5
  37.4 2.3 %collective-permute-done.2.rest_2_ = f32[512,128]{1,0:T(8,128)S(1)} collective-permute-done((f32[512,128]{1,0:T(8,128)S(1)}, f32[512,128]{1,0:T(8,128)S(1)}, u32[]{:S(2)}, u32[]{:S(2)}) %collective-permute-start.2) | collective-permute-done | bytes 262176 | tf_op jit(solution)/shard_map/ppermute | solution.py:145
  39.7 0.0 collective-permute-start.6
  39.7 3.7 %collective-permute-done.3.rest_3_ = f32[512,128]{1,0:T(8,128)S(1)} collective-permute-done((f32[512,128]{1,0:T(8,128)S(1)}, f32[512,128]{1,0:T(8,128)S(1)}, u32[]{:S(2)}, u32[]{:S(2)}) %collective-permute-start.3) | collective-permute-done | bytes 262176 | tf_op jit(solution)/shard_map/ppermute | solution.py:145
  43.4 0.0 collective-permute-start.7
  43.4 0.5 fusion.18
  44.0 1.0 pad_maximum_fusion
  45.0 1.3 %copy.18 = f32[648,192]{1,0:T(8,128)S(1)} copy(f32[648,192]{0,1:T(8,128)} %pad_maximum_fusion) | data formatting | bytes 995328
  46.3 0.0 collective-permute-done.4.rest_4_
  46.4 0.4 collective-permute-start.9
  46.8 0.0 collective-permute-done.5.rest_5_
  46.8 1.7 %collective-permute-start.10 = (f32[8,6144]{1,0:T(8,128)S(1)}, f32[8,6144]{1,0:T(8,128)S(1)}, u32[]{:S(2)}, u32[]{:S(2)}) collective-permute-start(f32[8,6144]{1,0:T(8,128)S(1)} %copy-done.1), channel_id=1, source_target_pairs={{0,64},{64,128},{128,192},{192,0},{1,65},{65,129},{129,193},{193,1... | collective-permute-start | bytes 589832 | tf_op jit(solution)/shard_map/ppermute | solution.py:145
  48.5 0.0 collective-permute-done.6.rest_6_
  48.5 0.0 collective-permute-done.7.rest_7_
  48.5 32.3 %mixed.1 = f32[512,128]{1,0:T(8,128)} custom-call(s32[1]{0:T(128)} %bitcast.c_ref, s32[46080]{0:T(1024)S(1)} %reshape.41.cidx_ref, s32[46080]{0:T(1024)S(1)} %reshape.42.widx_ref, f32[1296,128]{1,0:T(8,128)S(1)} %bitcast.41, f32[512,128]{1,0:T(8,128)S(1)} %bitcast.46, f32[512,128]{1,0:T(8,128)S(1)} %collective-permute-done.1.rest_1_, ...), custom_call_target="tpu_custom_call" | custom-call | flops 8847360 | bytes 8388608 | tf_op jit(solution)/shard_map/mixed/pallas_call | solution.py:81
  80.8 9.8 %all-to-all-start.1 = ((f32[32,2,8,128]{3,2,1,0:T(8,128)}), f32[32,2,8,128]{3,2,1,0:T(8,128)S(1)}, u32[]{:S(2)}, u32[]{:S(2)}) async-start(f32[32,2,8,128]{3,2,1,0:T(8,128)} %bitcast.6), calls=%async_computation.1 | async-start | bytes 524288 | tf_op jit(solution)/shard_map/all_to_all | solution.py:181
  90.6 0.0 copy-done.6
  90.6 0.1 bitcast_multiply_fusion
  90.7 1.3 %convolution_bitcast_fusion.1 = f32[1,8,48,128]{3,2,1,0:T(8,128)S(1)} fusion(f32[96,8,128]{2,1,0:T(8,128)} %fusion.1, s32[96]{0:T(128)S(1)} %get-tuple-element.7), kind=kOutput, calls=%fused_computation.1 | convolution fusion | flops 56627712 | bytes 590208 | tf_op jit(solution)/shard_map/rpl,pn->rnl/dot_general | solution.py:197
  92.0 0.7 copy.31
  92.8 0.7 reshape.49.k_ref
  93.5 0.0 collective-permute-done.8.x1
  93.5 0.0 collective-permute-done.9.x2
  93.5 0.0 collective-permute-done.10.x3
  93.5 0.0 copy-start.5
  93.5 7.9 %all-to-all-done.1.m_ref = f32[32,2,8,128]{3,2,1,0:T(8,128)S(1)} async-done(((f32[32,2,8,128]{3,2,1,0:T(8,128)}), f32[32,2,8,128]{3,2,1,0:T(8,128)S(1)}, u32[]{:S(2)}, u32[]{:S(2)}) %all-to-all-start.1) | async-done | bytes 262176 | tf_op jit(solution)/shard_map/all_to_all | solution.py:181
  101.4 0.7 copy-done.2
  102.1 2.6 %final.1 = f32[8,6144]{1,0:T(8,128)} custom-call(f32[32,2,8,128]{3,2,1,0:T(8,128)} %copy-done.2, f32[8,6144]{1,0:T(8,128)} %bitcast.48, f32[8,32]{1,0:T(8,128)} %reshape.49.k_ref, f32[8,6144]{1,0:T(8,128)} %x0.1, f32[8,6144]{1,0:T(8,128)} %collective-permute-done.8.x1, f32[8,6144]{1,0:T(8,128)} %copy-done.4, f32[8,6144]{1,0:T(8,128)} %copy-done.5), custom_call_target="tpu_custom_call" | custom-call | tf_op jit(solution)/shard_map/final/pallas_call | solution.py:117
  (18 shorter events, 0.1 us)
Async XLA Ops:
  0.0 43.4 %copy-start = (f32[324,18]{0,1:T(8,128)S(1)}, f32[324,18]{0,1:T(8,128)}, u32[]{:S(2)}) copy-start(f32[324,18]{0,1:T(8,128)} %param.19) | copy-start | bytes 69988
  0.0 30.4 %copy-start.7 = (s32[18,96]{1,0:T(8,128)S(1)}, s32[18,96]{1,0:T(8,128)}, u32[]{:S(2)}) copy-start(s32[18,96]{1,0:T(8,128)} %param.18) | copy-start | bytes 20740
  0.0 30.2 %copy-start.3 = (s32[90,512]{1,0:T(8,128)S(1)}, s32[90,512]{1,0:T(8,128)}, u32[]{:S(2)}) copy-start(s32[90,512]{1,0:T(8,128)} %param.15) | copy-start | bytes 552964
  0.0 30.3 %collective-permute-start = (s32[18,96]{1,0:T(8,128)}, s32[18,96]{1,0:T(8,128)S(1)}, u32[]{:S(2)}, u32[]{:S(2)}) collective-permute-start(s32[18,96]{1,0:T(8,128)} %param.18), channel_id=1, source_target_pairs={{0,1},{1,0},{2,3},{3,2},{4,5},{5,4},{6,7},{7,6},{8,9},{9,8},{10,11... | collective-permute-start | bytes 20744 | tf_op jit(solution)/shard_map/ppermute | solution.py:150
  0.1 93.4 %collective-permute-start.8 = (f32[8,6144]{1,0:T(8,128)}, f32[8,6144]{1,0:T(8,128)}, u32[]{:S(2)}, u32[]{:S(2)}) collective-permute-start(f32[8,6144]{1,0:T(8,128)} %x0.1), channel_id=1, source_target_pairs={{0,192},{64,0},{128,64},{192,128},{1,193},{65,1},{129,65},{193,129... | collective-permute-start | bytes 589832 | tf_op jit(solution)/shard_map/ppermute | solution.py:145
  5.0 23.2 %all-to-all-start = ((f32[32,2,8,128]{3,2,1,0:T(8,128)}), f32[32,2,8,128]{3,2,1,0:T(8,128)S(1)}, u32[]{:S(2)}, u32[]{:S(2)}) async-start(f32[32,2,8,128]{3,2,1,0:T(8,128)} %pack.1), calls=%async_computation | async-start | bytes 524288 | tf_op jit(solution)/shard_map/all_to_all | solution.py:153
  19.7 26.6 %copy-start.1 = (f32[8,6144]{1,0:T(8,128)S(1)}, f32[8,6144]{1,0:T(8,128)}, u32[]{:S(2)}) copy-start(f32[8,6144]{1,0:T(8,128)} %x0.1) | copy-start | bytes 589828
  27.9 62.7 %copy-start.8 = (s32[1,4]{1,0:T(1,128)S(1)}, s32[1,4]{1,0:T(1,128)}, u32[]{:S(2)}) copy-start(s32[1,4]{1,0:T(1,128)} %param.14) | copy-start | bytes 52
  27.9 62.7 %copy-start.6 = (f32[1,4,8,8]{3,2,1,0:T(8,128)S(1)}, f32[1,4,8,8]{3,2,1,0:T(8,128)}, u32[]{:S(2)}) copy-start(f32[1,4,8,8]{3,2,1,0:T(8,128)} %param.13) | copy-start | bytes 3076
  28.1 9.2 %collective-permute-start.1 = (f32[512,128]{1,0:T(8,128)S(1)}, f32[512,128]{1,0:T(8,128)S(1)}, u32[]{:S(2)}, u32[]{:S(2)}) collective-permute-start(f32[512,128]{1,0:T(8,128)S(1)} %bitcast.42), channel_id=1, source_target_pairs={{0,192},{64,0},{128,64},{192,128},{1,193},{65,1},{129,65},{193,129... | collective-permute-start | bytes 786440 | tf_op jit(solution)/shard_map/ppermute | solution.py:145
  28.9 10.8 %collective-permute-start.2 = (f32[512,128]{1,0:T(8,128)S(1)}, f32[512,128]{1,0:T(8,128)S(1)}, u32[]{:S(2)}, u32[]{:S(2)}) collective-permute-start(f32[512,128]{1,0:T(8,128)S(1)} %bitcast.43), channel_id=1, source_target_pairs={{0,128},{64,192},{128,0},{192,64},{1,129},{65,193},{129,1},{193,65... | collective-permute-start | bytes 786440 | tf_op jit(solution)/shard_map/ppermute | solution.py:145
  29.2 14.2 %collective-permute-start.3 = (f32[512,128]{1,0:T(8,128)S(1)}, f32[512,128]{1,0:T(8,128)S(1)}, u32[]{:S(2)}, u32[]{:S(2)}) collective-permute-start(f32[512,128]{1,0:T(8,128)S(1)} %bitcast.44), channel_id=1, source_target_pairs={{0,64},{64,128},{128,192},{192,0},{1,65},{65,129},{129,193},{193,1... | collective-permute-start | bytes 786440 | tf_op jit(solution)/shard_map/ppermute | solution.py:145
  30.4 16.0 %collective-permute-start.4 = (f32[512,128]{1,0:T(8,128)S(1)}, f32[512,128]{1,0:T(8,128)S(1)}, u32[]{:S(2)}, u32[]{:S(2)}) collective-permute-start(f32[512,128]{1,0:T(8,128)S(1)} %bitcast.45), channel_id=1, source_target_pairs={{0,1},{1,0},{2,3},{3,2},{4,5},{5,4},{6,7},{7,6},{8,9},{9,8},{10,11... | collective-permute-start | bytes 786440 | tf_op jit(solution)/shard_map/ppermute | solution.py:150
  37.4 9.4 %collective-permute-start.5 = (f32[512,128]{1,0:T(8,128)S(1)}, f32[512,128]{1,0:T(8,128)S(1)}, u32[]{:S(2)}, u32[]{:S(2)}) collective-permute-start(f32[512,128]{1,0:T(8,128)S(1)} %collective-permute-done.1.rest_1_), channel_id=1, source_target_pairs={{0,1},{1,0},{2,3},{3,2},{4,5},{5,4},{6,7},{7,6},{8,9},{9,8},{10,11... | collective-permute-start | bytes 786440 | tf_op jit(solution)/shard_map/ppermute | solution.py:150
  39.7 8.8 %collective-permute-start.6 = (f32[512,128]{1,0:T(8,128)S(1)}, f32[512,128]{1,0:T(8,128)S(1)}, u32[]{:S(2)}, u32[]{:S(2)}) collective-permute-start(f32[512,128]{1,0:T(8,128)S(1)} %collective-permute-done.2.rest_2_), channel_id=1, source_target_pairs={{0,1},{1,0},{2,3},{3,2},{4,5},{5,4},{6,7},{7,6},{8,9},{9,8},{10,11... | collective-permute-start | bytes 786440 | tf_op jit(solution)/shard_map/ppermute | solution.py:150
  43.4 5.1 %collective-permute-start.7 = (f32[512,128]{1,0:T(8,128)S(1)}, f32[512,128]{1,0:T(8,128)S(1)}, u32[]{:S(2)}, u32[]{:S(2)}) collective-permute-start(f32[512,128]{1,0:T(8,128)S(1)} %collective-permute-done.3.rest_3_), channel_id=1, source_target_pairs={{0,1},{1,0},{2,3},{3,2},{4,5},{5,4},{6,7},{7,6},{8,9},{9,8},{10,11... | collective-permute-start | bytes 786440 | tf_op jit(solution)/shard_map/ppermute | solution.py:150
  46.4 47.1 %collective-permute-start.9 = (f32[8,6144]{1,0:T(8,128)S(1)}, f32[8,6144]{1,0:T(8,128)S(1)}, u32[]{:S(2)}, u32[]{:S(2)}) collective-permute-start(f32[8,6144]{1,0:T(8,128)S(1)} %copy-done.1), channel_id=1, source_target_pairs={{0,128},{64,192},{128,0},{192,64},{1,129},{65,193},{129,1},{193,65... | collective-permute-start | bytes 589832 | tf_op jit(solution)/shard_map/ppermute | solution.py:145
  46.8 46.7 %collective-permute-start.10 = (f32[8,6144]{1,0:T(8,128)S(1)}, f32[8,6144]{1,0:T(8,128)S(1)}, u32[]{:S(2)}, u32[]{:S(2)}) collective-permute-start(f32[8,6144]{1,0:T(8,128)S(1)} %copy-done.1), channel_id=1, source_target_pairs={{0,64},{64,128},{128,192},{192,0},{1,65},{65,129},{129,193},{193,1... | collective-permute-start | bytes 589832 | tf_op jit(solution)/shard_map/ppermute | solution.py:145
  80.8 20.6 %all-to-all-start.1 = ((f32[32,2,8,128]{3,2,1,0:T(8,128)}), f32[32,2,8,128]{3,2,1,0:T(8,128)S(1)}, u32[]{:S(2)}, u32[]{:S(2)}) async-start(f32[32,2,8,128]{3,2,1,0:T(8,128)} %bitcast.6), calls=%async_computation.1 | async-start | bytes 524288 | tf_op jit(solution)/shard_map/all_to_all | solution.py:181
  93.5 8.0 %copy-start.4 = (f32[8,6144]{1,0:T(8,128)}, f32[8,6144]{1,0:T(8,128)S(1)}, u32[]{:S(2)}) copy-start(f32[8,6144]{1,0:T(8,128)S(1)} %collective-permute-done.9.x2) | copy-start | bytes 589828
  93.5 7.9 %copy-start.5 = (f32[8,6144]{1,0:T(8,128)}, f32[8,6144]{1,0:T(8,128)S(1)}, u32[]{:S(2)}) copy-start(f32[8,6144]{1,0:T(8,128)S(1)} %collective-permute-done.10.x3) | copy-start | bytes 589828
  101.4 0.7 copy-start.2

commit v2 on v1

v2 whole, which is shorter than its diff:
```python
import functools

import jax
import jax.numpy as jnp
from jax import lax
from jax.experimental import pallas as pl
from jax.experimental.pallas import tpu as pltpu
from jax.sharding import Mesh
from jax.sharding import PartitionSpec as P

HIGH = lax.Precision.HIGHEST
RA = 8
LANES = 128
N_GRP = 4
NZ, NX, NC = 8, 4, 2
NQ = NZ * NX
COLS = 192
PAD = 8

SMEM = pl.BlockSpec(memory_space=pltpu.SMEM)
VMEM = pl.BlockSpec(memory_space=pltpu.VMEM)
ANY = pl.BlockSpec(memory_space=pl.ANY)


def pack_kernel(g_ref, mask_ref, x_ref, alpha_ref, o_ref):
    tail = COLS - LANES
    pieces = [jnp.zeros((RA, tail), jnp.float32)]
    for rel in range(N_GRP):
        h = (g_ref[0] + rel) & (N_GRP - 1)
        pieces.append(alpha_ref[0, h] * mask_ref[0, h].astype(jnp.float32))
    pieces.append(jnp.zeros((RA, LANES - tail - N_GRP * RA), jnp.float32))
    coupling = jnp.concatenate(pieces, axis=1)
    for j in range(NQ):
        lo = COLS * j
        o_ref[j, 0] = x_ref[:, lo : lo + LANES]
        o_ref[j, 1] = jnp.concatenate(
            [x_ref[:, lo + LANES : lo + COLS], coupling[:, tail:]], axis=1
        )


def pack(group, mask, coeff, alpha_blocks):
    return pl.pallas_call(
        pack_kernel,
        out_shape=jax.ShapeDtypeStruct((NQ, 2, RA, LANES), jnp.float32),
        in_specs=[SMEM, SMEM, VMEM, VMEM],
        out_specs=VMEM,
        name="pack",
    )(group, mask, coeff, alpha_blocks)


def mixed_kernel(n_exc, row_count, chunks, c_ref, cidx_hbm, widx_hbm, w_ref, *rest):
    parts = rest[: 2 * N_GRP]
    o_ref, table, cidx, widx, part_sem, idx_sem = rest[2 * N_GRP :]
    part_rows = NQ * 2 * RA
    per = n_exc // chunks
    length = per * row_count

    def index_copies(k):
        at = pl.ds(k * length, length)
        return (
            pltpu.make_async_copy(cidx_hbm.at[at], cidx.at[at], idx_sem.at[0, k]),
            pltpu.make_async_copy(widx_hbm.at[at], widx.at[at], idx_sem.at[1, k]),
        )

    for copy in index_copies(0):
        copy.start()
    copies = [
        pltpu.make_async_copy(
            part, table.at[pl.ds(i * part_rows, part_rows)], part_sem.at[i]
        )
        for i, part in enumerate(parts)
    ]
    for copy in copies:
        copy.start()
    for k in range(1, chunks):
        for copy in index_copies(k):
            copy.start()
    for copy in copies:
        copy.wait()
    core = c_ref[0]
    span = row_count - RA + 1

    def gather(q, offset, a, acc):
        start = q * (2 * RA) + core * RA + offset
        size = span + (n_exc - per) * row_count
        for e in range(per):
            base = e * row_count + a
            ci = cidx.at[pl.ds(base, size)][start]
            wi = widx.at[pl.ds(base, size)][start]
            term = (
                table[pl.ds(ci, 2, stride=RA), :] * w_ref[pl.ds(wi, 2, stride=RA), :]
            )
            acc = term if acc is None else acc + term
        return acc

    def first_block(q, carry):
        for a in range(RA):
            rows = pl.ds(q * (2 * RA) + a, 2, stride=RA)
            o_ref[rows, :] = gather(q, 0, a, None)
        at = q * (2 * RA)
        mix = table[pl.ds(pl.multiple_of(at + RA, RA), RA), :]
        mix = mix[:, COLS - LANES : COLS - LANES + N_GRP * RA]
        for half in range(2):
            rows = [
                table[pl.ds(pl.multiple_of(at + h * part_rows + half * RA, RA), RA), :]
                for h in range(N_GRP)
            ]
            alpha = jnp.dot(
                mix,
                jnp.concatenate(rows, axis=0),
                precision=HIGH,
                preferred_element_type=jnp.float32,
            )
            target = pl.ds(pl.multiple_of(at + half * RA, RA), RA)
            o_ref[target, :] = o_ref[target, :] + alpha
        return carry

    def later_chunk(k, carry):
        for copy in index_copies(k):
            copy.wait()

        def block(q, inner):
            for a in range(RA):
                rows = pl.ds(q * (2 * RA) + a, 2, stride=RA)
                o_ref[rows, :] = gather(q, k * length, a, o_ref[rows, :])
            return inner

        return lax.fori_loop(0, NQ, block, carry)

    for copy in index_copies(0):
        copy.wait()
    lax.fori_loop(0, NQ, first_block, 0)
    lax.fori_loop(1, chunks, later_chunk, 0)


def mixed_call(core, cidx, widx, wtab, parts, n_exc, row_count, chunks=3):
    part_rows = NQ * 2 * RA
    return pl.pallas_call(
        functools.partial(mixed_kernel, n_exc, row_count, chunks),
        out_shape=jax.ShapeDtypeStruct((part_rows, LANES), jnp.float32),
        in_specs=[SMEM, ANY, ANY, VMEM] + [ANY] * len(parts),
        out_specs=VMEM,
        scratch_shapes=[
            pltpu.VMEM((2 * N_GRP * part_rows, LANES), jnp.float32),
            pltpu.SMEM((n_exc * row_count,), jnp.int32),
            pltpu.SMEM((n_exc * row_count,), jnp.int32),
            pltpu.SemaphoreType.DMA((2 * N_GRP,)),
            pltpu.SemaphoreType.DMA((2, chunks)),
        ],
        compiler_params=pltpu.CompilerParams(vmem_limit_bytes=16 << 20),
        cost_estimate=pl.CostEstimate(
            flops=n_exc * row_count * COLS, bytes_accessed=8 << 20, transcendentals=0
        ),
        name="mixed",
    )(core, cidx, widx, wtab, *parts)


def final_kernel(m_ref, b_ref, o_ref):
    for j in range(NQ):
        lo = COLS * j
        o_ref[:, lo : lo + LANES] = m_ref[j, 0] + b_ref[:, lo : lo + LANES]
        o_ref[:, lo + LANES : lo + COLS] = (
            m_ref[j, 1, :, : COLS - LANES] + b_ref[:, lo + LANES : lo + COLS]
        )


def final_call(mixed, same_beta):
    return pl.pallas_call(
        final_kernel,
        out_shape=jax.ShapeDtypeStruct(same_beta.shape, jnp.float32),
        in_specs=[VMEM] * 2,
        out_specs=VMEM,
        name="final",
    )(mixed, same_beta)


def per_device(
    coeff,
    beta_blocks,
    block_list,
    alpha_blocks,
    partner_mask,
    exc_source,
    exc_pair,
    exc_parity,
    occupation,
    coulomb,
):
    g = lax.axis_index("grp")
    c = lax.axis_index("c")
    alpha_rows, beta_width = coeff.shape
    n_exc, row_count = exc_source.shape
    n_pair = coulomb.shape[0]

    def shift(value, k):
        return lax.ppermute(
            value, "grp", [(i, (i - k) % N_GRP) for i in range(N_GRP)]
        )

    def swap(value):
        return lax.ppermute(value, "c", [(0, 1), (1, 0)])

    packed = pack(g.reshape(1), partner_mask, coeff, alpha_blocks)
    own = lax.all_to_all(packed, ("z", "x"), split_axis=0, concat_axis=0, tiled=True)
    own = own.reshape(NQ * 2 * RA, LANES)

    other_occ = swap(occupation)
    first = jnp.where(c == 0, occupation, other_occ)
    second = jnp.where(c == 0, other_occ, occupation)
    occ = jnp.concatenate([first, second], axis=1).astype(jnp.float32)
    weights = jnp.dot(coulomb, occ, precision=HIGH, preferred_element_type=jnp.float32)
    signed = jnp.concatenate([weights, -weights], axis=0)
    signed = jnp.pad(signed, ((0, 0), (0, 2 * LANES - COLS)))
    wtab = (
        signed.reshape(2 * n_pair // RA, RA, 2, LANES)
        .transpose(0, 2, 1, 3)
        .reshape(4 * n_pair, LANES)
    )

    rel_g = ((exc_source >> 9) - g) & (N_GRP - 1)
    rel_c = ((exc_source >> 3) & 1) ^ c
    pos = (rel_c * N_GRP + rel_g) * NQ + ((exc_source >> 4) & (NQ - 1))
    cidx = (pos * (2 * RA) + (exc_source & (RA - 1))).reshape(-1)
    pair = exc_pair + n_pair * exc_parity
    widx = ((pair >> 3) * (2 * RA) + (pair & (RA - 1))).reshape(-1)

    own, wtab, cidx, widx, late = lax.optimization_barrier(
        (own, wtab, cidx, widx, coeff)
    )
    near = [own] + [shift(own, k) for k in range(1, N_GRP)]
    parts = near + [swap(v) for v in near]
    mixed_local = mixed_call(
        c.reshape(1).astype(jnp.int32), cidx, widx, wtab, parts, n_exc, row_count
    )
    mixed = lax.all_to_all(
        mixed_local.reshape(NQ, 2, RA, LANES),
        ("z", "x"),
        split_axis=0,
        concat_axis=0,
        tiled=True,
    )

    block_size = beta_blocks.shape[1]
    block_count = beta_width // block_size
    blocked = late.reshape(alpha_rows, block_count, block_size)
    block_ids = jnp.arange(block_count, dtype=jnp.int32)
    choosing = (block_list[0][:, None] == block_ids[None, :]).astype(jnp.float32)
    picked = jnp.einsum("rnk,pn->rpk", blocked, choosing, precision=HIGH)
    applied = jnp.einsum("rpk,pkl->rpl", picked, beta_blocks, precision=HIGH)
    placing = (block_list[1][:, None] == block_ids[None, :]).astype(jnp.float32)
    same_beta = jnp.einsum("rpl,pn->rnl", applied, placing, precision=HIGH).reshape(
        alpha_rows, beta_width
    )

    return final_call(mixed, same_beta)


def solution(mesh):
    fine = Mesh(mesh.devices.reshape(N_GRP, NZ, NX, NC), ("grp", "z", "x", "c"))
    wide = ("z", "x", "c")
    every = ("grp",) + wide
    in_specs = (
        P(every, None),
        P(),
        P(),
        P(every, None, None, None),
        P(every, None),
        P(None, "grp"),
        P(None, "grp"),
        P(None, "grp"),
        P(None, wide),
        P(),
    )
    return jax.shard_map(
        per_device,
        mesh=fine,
        in_specs=in_specs,
        out_specs=P(every, None),
        check_vma=False,
    )
```

time: 107 us -> 96.7 us (0.904); the launches traced: 105 us -> 95.7 us
  starting transfers between devices: 28.9 us -> 22.3 us
  waiting for transfers between devices: 21.1 us -> 24.4 us
  matrix products: 11.3 us -> 8.64 us
  local copies, waits for them, and re-layouts: 4.28 us -> 1.77 us
  Pallas kernels: 36.7 us -> 35.5 us
    all_to_all x1, waiting for transfers between devices: 0.21 us -> 7.97 us  [per_device(): lax.all_to_all(packed, ('z', 'x'), split_axis=0, concat_axis=0, tiled=True)]
    all_to_all x1, waiting for transfers between devices: 7.92 us -> 3 us  [per_device(): lax.all_to_all(mixed_local.reshape(NQ, 2, RA, LANES), ('z', 'x'), split_a...]
    all_to_all x1, starting transfers between devices: 9.79 us -> 5.56 us  [per_device(): lax.all_to_all(mixed_local.reshape(NQ, 2, RA, LANES), ('z', 'x'), split_a...]
    ppermute x6 -> x3, starting transfers between devices: 7.28 us -> 4.61 us  [shift(): lax.ppermute(value, 'grp', [(i, (i - k) % N_GRP) for i in range(N_GRP)])]
    ppermute x5, waiting for transfers between devices: 0.01 us -> 1.13 us  [swap(): return lax.ppermute(value, 'c', [(0, 1), (1, 0)])]
    unnamed x20 -> x10, local copies, waits for them, and re-layouts: 2.76 us -> 1.69 us
    ppermute x6 -> x3, waiting for transfers between devices: 12.9 us -> 12.3 us  [shift(): lax.ppermute(value, 'grp', [(i, (i - k) % N_GRP) for i in range(N_GRP)])]
  transfers between devices with their start and end apart: 13 -> 10, of which waited for: 5 -> 6; matrix products, arithmetic and copies ran while one was open for 16% -> 13% of each run, Pallas kernels for 33% -> 2%
where the time goes in v2:
time: 96.7 us; the launch traced here: 95.7 us
  Pallas kernels  35.5 us (37%)
  waiting for transfers between devices  24.4 us (25%)
  starting transfers between devices  22.3 us (23%)
  matrix products  8.64 us (9%)
  other arithmetic  2.98 us (3%)
  local copies, waits for them, and re-layouts  1.77 us (2%)
    pallas_call x1, Pallas kernels, mixed_call(): pl.pallas_call(functools.partial(mixed_kernel, n_exc, row_count, chunks),...  31.8 us
    ppermute x3, waiting for transfers between devices, shift(): lax.ppermute(value, 'grp', [(i, (i - k) % N_GRP) for i in range(N_GRP)])  12.3 us
    all_to_all x1, starting transfers between devices, per_device(): lax.all_to_all(packed, ('z', 'x'), split_axis=0, concat_axis=0, tiled=True)  11.6 us
    all_to_all x1, waiting for transfers between devices, per_device(): lax.all_to_all(packed, ('z', 'x'), split_axis=0, concat_axis=0, tiled=True)  7.97 us
    dot_general x1, matrix products, per_device(): applied = jnp.einsum('rpk,pkl->rpl', picked, beta_blocks, precision=HIGH)  7.46 us
    all_to_all x1, starting transfers between devices, per_device(): lax.all_to_all(mixed_local.reshape(NQ, 2, RA, LANES), ('z', 'x'), split_a...  5.56 us
    ppermute x3, starting transfers between devices, shift(): lax.ppermute(value, 'grp', [(i, (i - k) % N_GRP) for i in range(N_GRP)])  4.61 us
    all_to_all x1, waiting for transfers between devices, per_device(): lax.all_to_all(mixed_local.reshape(NQ, 2, RA, LANES), ('z', 'x'), split_a...  3 us
  transfers between devices with their start and end apart: 10, of which 6 were waited for; matrix products, arithmetic and copies ran while one was open for 13% of the time, Pallas kernels for 2%

profile of v2, /device:TPU:2, one launch (start us, length us, event | category | flops | bytes accessed | tf_op | source)
XLA Modules:
  0.0 95.7 jit_solution(13825508813504295497)
XLA Ops:
  0.0 0.0 copy-start
  0.0 0.0 copy-start.2
  0.0 0.0 copy-start.3
  0.0 0.1 collective-permute-start
  0.1 1.8 %pack.1 = f32[32,2,8,128]{3,2,1,0:T(8,128)} custom-call(s32[1]{0:T(128)} %bitcast.1.g_ref, s32[1,4]{1,0:T(1,128)} %mask_ref.1, f32[8,6144]{1,0:T(8,128)} %x_ref.1, f32[1,4,8,8]{3,2,1,0:T(8,128)} %alpha_ref.1), custom_call_target="tpu_custom_call" | custom-call | tf_op jit(solution)/shard_map/pack/pallas_call | solution.py:42
  1.9 11.6 %all-to-all-start = ((f32[32,2,8,128]{3,2,1,0:T(8,128)}), f32[32,2,8,128]{3,2,1,0:T(8,128)S(1)}, u32[]{:S(2)}, u32[]{:S(2)}) async-start(f32[32,2,8,128]{3,2,1,0:T(8,128)} %pack.1), calls=%async_computation | async-start | bytes 524288 | tf_op jit(solution)/shard_map/all_to_all | solution.py:204
  13.5 1.1 %and_add_fusion = s32[90,512]{1,0:T(8,128)S(1)} fusion(s32[90,512]{1,0:T(8,128)} %param.16, s32[90,512]{1,0:T(8,128)} %param.17), kind=kLoop, calls=%fused_computation.11 | loop fusion | flops 276480 | bytes 552960 | tf_op jit(solution)/shard_map/add | solution.py:225
  14.6 1.0 %and_add_fusion.1 = s32[90,512]{1,0:T(8,128)S(1)} fusion(s32[90,512]{1,0:T(8,128)} %param.15, s32[]{:T(128)} %axis_index.25, s32[]{:T(128)} %axis_index.22), kind=kLoop, calls=%fused_computation.12 | loop fusion | flops 691200 | bytes 368648 | tf_op jit(solution)/shard_map/add | solution.py:223
  15.7 0.0 collective-permute-done
  15.7 0.7 broadcast_select_fusion.1
  16.4 0.0 copy-done
  16.4 0.5 fusion.16
  16.9 0.2 pad_maximum_fusion
  17.1 0.2 copy.16
  17.4 8.0 %all-to-all-done = f32[32,2,8,128]{3,2,1,0:T(8,128)S(1)} async-done(((f32[32,2,8,128]{3,2,1,0:T(8,128)}), f32[32,2,8,128]{3,2,1,0:T(8,128)S(1)}, u32[]{:S(2)}, u32[]{:S(2)}) %all-to-all-start) | async-done | bytes 262176 | tf_op jit(solution)/shard_map/all_to_all | solution.py:204
  25.4 3.0 %collective-permute-start.1 = (f32[512,128]{1,0:T(8,128)S(1)}, f32[512,128]{1,0:T(8,128)S(1)}, u32[]{:S(2)}, u32[]{:S(2)}) collective-permute-start(f32[512,128]{1,0:T(8,128)S(1)} %bitcast.37), channel_id=1, source_target_pairs={{0,192},{64,0},{128,64},{192,128},{1,193},{65,1},{129,65},{193,129... | collective-permute-start | bytes 786440 | tf_op jit(solution)/shard_map/ppermute | solution.py:196
  28.4 0.6 collective-permute-start.2
  29.0 1.0 %collective-permute-start.3 = (f32[512,128]{1,0:T(8,128)S(1)}, f32[512,128]{1,0:T(8,128)S(1)}, u32[]{:S(2)}, u32[]{:S(2)}) collective-permute-start(f32[512,128]{1,0:T(8,128)S(1)} %bitcast.39), channel_id=1, source_target_pairs={{0,64},{64,128},{128,192},{192,0},{1,65},{65,129},{129,193},{193,1... | collective-permute-start | bytes 786440 | tf_op jit(solution)/shard_map/ppermute | solution.py:196
  30.0 0.0 collective-permute-start.4
  30.0 9.0 %collective-permute-done.1.rest_1_ = f32[512,128]{1,0:T(8,128)S(1)} collective-permute-done((f32[512,128]{1,0:T(8,128)S(1)}, f32[512,128]{1,0:T(8,128)S(1)}, u32[]{:S(2)}, u32[]{:S(2)}) %collective-permute-start.1) | collective-permute-done | bytes 262176 | tf_op jit(solution)/shard_map/ppermute | solution.py:196
  39.0 0.0 collective-permute-start.5
  39.0 0.1 collective-permute-done.2.rest_2_
  39.1 0.4 collective-permute-start.6
  39.5 3.2 %collective-permute-done.3.rest_3_ = f32[512,128]{1,0:T(8,128)S(1)} collective-permute-done((f32[512,128]{1,0:T(8,128)S(1)}, f32[512,128]{1,0:T(8,128)S(1)}, u32[]{:S(2)}, u32[]{:S(2)}) %collective-permute-start.3) | collective-permute-done | bytes 262176 | tf_op jit(solution)/shard_map/ppermute | solution.py:196
  42.7 0.0 collective-permute-start.7
  42.7 0.0 copy-done.3
  42.7 0.0 copy-done.2
  42.7 0.4 fusion.5
  43.1 0.0 collective-permute-done.4.rest_4_
  43.1 0.0 collective-permute-done.5.rest_5_
  43.1 0.0 collective-permute-done.6.rest_6_
  43.1 1.1 %collective-permute-done.7.rest_7_ = f32[512,128]{1,0:T(8,128)S(1)} collective-permute-done((f32[512,128]{1,0:T(8,128)S(1)}, f32[512,128]{1,0:T(8,128)S(1)}, u32[]{:S(2)}, u32[]{:S(2)}) %collective-permute-start.7) | collective-permute-done | bytes 262176 | tf_op jit(solution)/shard_map/ppermute | solution.py:201
  44.2 31.8 %mixed.1 = f32[512,128]{1,0:T(8,128)} custom-call(s32[1]{0:T(128)} %bitcast.c_ref, s32[46080]{0:T(1024)S(1)} %reshape.37.cidx_hbm, s32[46080]{0:T(1024)S(1)} %reshape.38.widx_hbm, f32[1296,128]{1,0:T(8,128)S(1)} %bitcast.36, f32[512,128]{1,0:T(8,128)S(1)} %bitcast.41, f32[512,128]{1,0:T(8,128)S(1)} %collective-permute-done.1.rest_1_, ...), custom_call_target="tpu_custom_call" | custom-call | flops 8847360 | bytes 8388608 | tf_op jit(solution)/shard_map/mixed/pallas_call | solution.py:138
  76.1 5.6 %all-to-all-start.1 = ((f32[32,2,8,128]{3,2,1,0:T(8,128)}), f32[32,2,8,128]{3,2,1,0:T(8,128)S(1)}, u32[]{:S(2)}, u32[]{:S(2)}) async-start(f32[32,2,8,128]{3,2,1,0:T(8,128)} %bitcast.7), calls=%async_computation.1 | async-start | bytes 524288 | tf_op jit(solution)/shard_map/all_to_all | solution.py:235
  81.6 7.5 %fusion.1 = f32[96,8,128]{2,1,0:T(8,128)S(1)} fusion(f32[96,128,128]{2,1,0:T(8,128)} %param.11, f32[96,8,128]{2,0,1:T(8,128)S(1)} %fusion.5), kind=kOutput, calls=%fused_computation.4 | convolution fusion | flops 150994944 | bytes 7077888 | tf_op jit(solution)/shard_map/rpk,pkl->rpl/dot_general | solution.py:249
  89.1 0.3 convolution_bitcast_fusion.1
  89.4 0.7 copy.29
  90.1 3.0 %all-to-all-done.1.m_ref = f32[32,2,8,128]{3,2,1,0:T(8,128)S(1)} async-done(((f32[32,2,8,128]{3,2,1,0:T(8,128)}), f32[32,2,8,128]{3,2,1,0:T(8,128)S(1)}, u32[]{:S(2)}, u32[]{:S(2)}) %all-to-all-start.1) | async-done | bytes 262176 | tf_op jit(solution)/shard_map/all_to_all | solution.py:235
  93.1 0.0 copy-start.1
  93.1 0.7 copy-done.1
  93.9 1.9 %final.1 = f32[8,6144]{1,0:T(8,128)} custom-call(f32[32,2,8,128]{3,2,1,0:T(8,128)} %copy-done.1, f32[8,6144]{1,0:T(8,128)} %bitcast.42), custom_call_target="tpu_custom_call" | custom-call | tf_op jit(solution)/shard_map/final/pallas_call | solution.py:168
  (4 shorter events, 0.1 us)
Async XLA Ops:
  0.0 16.4 %copy-start = (f32[324,18]{0,1:T(8,128)S(1)}, f32[324,18]{0,1:T(8,128)}, u32[]{:S(2)}) copy-start(f32[324,18]{0,1:T(8,128)} %param.19) | copy-start | bytes 69988
  0.0 42.7 %copy-start.2 = (f32[8,6144]{1,0:T(8,128)S(1)}, f32[8,6144]{1,0:T(8,128)}, u32[]{:S(2)}) copy-start(f32[8,6144]{1,0:T(8,128)} %x_ref.1) | copy-start | bytes 589828
  0.0 42.7 %copy-start.3 = (s32[2,96]{1,0:T(2,128)S(1)}, s32[2,96]{1,0:T(2,128)}, u32[]{:S(2)}) copy-start(s32[2,96]{1,0:T(2,128)} %param.12) | copy-start | bytes 2308
  0.0 15.7 %collective-permute-start = (s32[18,96]{1,0:T(8,128)}, s32[18,96]{1,0:T(8,128)S(1)}, u32[]{:S(2)}, u32[]{:S(2)}) collective-permute-start(s32[18,96]{1,0:T(8,128)} %param.18), channel_id=1, source_target_pairs={{0,1},{1,0},{2,3},{3,2},{4,5},{5,4},{6,7},{7,6},{8,9},{9,8},{10,11... | collective-permute-start | bytes 20744 | tf_op jit(solution)/shard_map/ppermute | solution.py:201
  1.9 23.5 %all-to-all-start = ((f32[32,2,8,128]{3,2,1,0:T(8,128)}), f32[32,2,8,128]{3,2,1,0:T(8,128)S(1)}, u32[]{:S(2)}, u32[]{:S(2)}) async-start(f32[32,2,8,128]{3,2,1,0:T(8,128)} %pack.1), calls=%async_computation | async-start | bytes 524288 | tf_op jit(solution)/shard_map/all_to_all | solution.py:204
  25.4 13.6 %collective-permute-start.1 = (f32[512,128]{1,0:T(8,128)S(1)}, f32[512,128]{1,0:T(8,128)S(1)}, u32[]{:S(2)}, u32[]{:S(2)}) collective-permute-start(f32[512,128]{1,0:T(8,128)S(1)} %bitcast.37), channel_id=1, source_target_pairs={{0,192},{64,0},{128,64},{192,128},{1,193},{65,1},{129,65},{193,129... | collective-permute-start | bytes 786440 | tf_op jit(solution)/shard_map/ppermute | solution.py:196
  28.4 10.7 %collective-permute-start.2 = (f32[512,128]{1,0:T(8,128)S(1)}, f32[512,128]{1,0:T(8,128)S(1)}, u32[]{:S(2)}, u32[]{:S(2)}) collective-permute-start(f32[512,128]{1,0:T(8,128)S(1)} %bitcast.38), channel_id=1, source_target_pairs={{0,128},{64,192},{128,0},{192,64},{1,129},{65,193},{129,1},{193,65... | collective-permute-start | bytes 786440 | tf_op jit(solution)/shard_map/ppermute | solution.py:196
  29.0 13.7 %collective-permute-start.3 = (f32[512,128]{1,0:T(8,128)S(1)}, f32[512,128]{1,0:T(8,128)S(1)}, u32[]{:S(2)}, u32[]{:S(2)}) collective-permute-start(f32[512,128]{1,0:T(8,128)S(1)} %bitcast.39), channel_id=1, source_target_pairs={{0,64},{64,128},{128,192},{192,0},{1,65},{65,129},{129,193},{193,1... | collective-permute-start | bytes 786440 | tf_op jit(solution)/shard_map/ppermute | solution.py:196
  30.0 13.1 %collective-permute-start.4 = (f32[512,128]{1,0:T(8,128)S(1)}, f32[512,128]{1,0:T(8,128)S(1)}, u32[]{:S(2)}, u32[]{:S(2)}) collective-permute-start(f32[512,128]{1,0:T(8,128)S(1)} %bitcast.40), channel_id=1, source_target_pairs={{0,1},{1,0},{2,3},{3,2},{4,5},{5,4},{6,7},{7,6},{8,9},{9,8},{10,11... | collective-permute-start | bytes 786440 | tf_op jit(solution)/shard_map/ppermute | solution.py:201
  39.0 4.1 %collective-permute-start.5 = (f32[512,128]{1,0:T(8,128)S(1)}, f32[512,128]{1,0:T(8,128)S(1)}, u32[]{:S(2)}, u32[]{:S(2)}) collective-permute-start(f32[512,128]{1,0:T(8,128)S(1)} %collective-permute-done.1.rest_1_), channel_id=1, source_target_pairs={{0,1},{1,0},{2,3},{3,2},{4,5},{5,4},{6,7},{7,6},{8,9},{9,8},{10,11... | collective-permute-start | bytes 786440 | tf_op jit(solution)/shard_map/ppermute | solution.py:201
  39.1 4.0 %collective-permute-start.6 = (f32[512,128]{1,0:T(8,128)S(1)}, f32[512,128]{1,0:T(8,128)S(1)}, u32[]{:S(2)}, u32[]{:S(2)}) collective-permute-start(f32[512,128]{1,0:T(8,128)S(1)} %collective-permute-done.2.rest_2_), channel_id=1, source_target_pairs={{0,1},{1,0},{2,3},{3,2},{4,5},{5,4},{6,7},{7,6},{8,9},{9,8},{10,11... | collective-permute-start | bytes 786440 | tf_op jit(solution)/shard_map/ppermute | solution.py:201
  42.7 1.5 %collective-permute-start.7 = (f32[512,128]{1,0:T(8,128)S(1)}, f32[512,128]{1,0:T(8,128)S(1)}, u32[]{:S(2)}, u32[]{:S(2)}) collective-permute-start(f32[512,128]{1,0:T(8,128)S(1)} %collective-permute-done.3.rest_3_), channel_id=1, source_target_pairs={{0,1},{1,0},{2,3},{3,2},{4,5},{5,4},{6,7},{7,6},{8,9},{9,8},{10,11... | collective-permute-start | bytes 786440 | tf_op jit(solution)/shard_map/ppermute | solution.py:201
  76.1 17.1 %all-to-all-start.1 = ((f32[32,2,8,128]{3,2,1,0:T(8,128)}), f32[32,2,8,128]{3,2,1,0:T(8,128)S(1)}, u32[]{:S(2)}, u32[]{:S(2)}) async-start(f32[32,2,8,128]{3,2,1,0:T(8,128)} %bitcast.7), calls=%async_computation.1 | async-start | bytes 524288 | tf_op jit(solution)/shard_map/all_to_all | solution.py:235
  93.1 0.7 copy-start.1

commit v3 on v2

v3 whole, which is shorter than its diff:
```python
import functools

import jax
import jax.numpy as jnp
from jax import lax
from jax.experimental import pallas as pl
from jax.experimental.pallas import tpu as pltpu
from jax.sharding import Mesh
from jax.sharding import PartitionSpec as P

HIGH = lax.Precision.HIGHEST
RA = 8
LANES = 128
N_GRP = 4
NZ, NXH, NXL, NC = 8, 2, 2, 2
NQ = NZ * NXH
NS = NXL * NC
NT = 3
PART = NQ * NT * RA

SMEM = pl.BlockSpec(memory_space=pltpu.SMEM)
VMEM = pl.BlockSpec(memory_space=pltpu.VMEM)
ANY = pl.BlockSpec(memory_space=pl.ANY)


def pack_kernel(g_ref, mask_ref, x_ref, alpha_ref, o_ref):
    pieces = []
    for rel in range(N_GRP):
        h = (g_ref[0] + rel) & (N_GRP - 1)
        pieces.append(alpha_ref[0, h] * mask_ref[0, h].astype(jnp.float32))
    pieces.append(jnp.zeros((RA, LANES - N_GRP * RA), jnp.float32))
    coupling = jnp.concatenate(pieces, axis=1)
    for j in range(NQ):
        for t in range(NT):
            lo = (j * NT + t) * LANES
            o_ref[j, t] = x_ref[:, lo : lo + LANES]
        o_ref[j, NT] = coupling


def pack(group, mask, coeff, alpha_blocks):
    return pl.pallas_call(
        pack_kernel,
        out_shape=jax.ShapeDtypeStruct((NQ, NT + 1, RA, LANES), jnp.float32),
        in_specs=[SMEM, SMEM, VMEM, VMEM],
        out_specs=VMEM,
        name="pack",
    )(group, mask, coeff, alpha_blocks)


def mixed_kernel(
    n_exc, row_count, chunks, sel_ref, cidx_hbm, widx_hbm, w_ref, mix_ref, *rest
):
    count = N_GRP * NS
    parts = rest[:count]
    o_ref, table, cidx, widx, part_sem, idx_sem = rest[count:]
    per = n_exc // chunks
    length = per * row_count

    def index_copies(k):
        at = pl.ds(k * length, length)
        return (
            pltpu.make_async_copy(cidx_hbm.at[at], cidx.at[at], idx_sem.at[0, k]),
            pltpu.make_async_copy(widx_hbm.at[at], widx.at[at], idx_sem.at[1, k]),
        )

    for copy in index_copies(0):
        copy.start()
    copies = [
        pltpu.make_async_copy(part, table.at[pl.ds(i * PART, PART)], part_sem.at[i])
        for i, part in enumerate(parts)
    ]
    for copy in copies:
        copy.start()
    for k in range(1, chunks):
        for copy in index_copies(k):
            copy.start()
    for copy in copies:
        copy.wait()
    shift = sel_ref[0] * RA
    size = row_count - RA + 1 + (n_exc - per) * row_count

    def gather(q, offset, a, acc):
        start = q * (NS * RA) + shift + offset
        for e in range(per):
            base = e * row_count + a
            ci = cidx.at[pl.ds(base, size)][start]
            wi = widx.at[pl.ds(base, size)][start]
            term = (
                table[pl.ds(ci, NT, stride=RA), :] * w_ref[pl.ds(wi, NT, stride=RA), :]
            )
            acc = term if acc is None else acc + term
        return acc

    def first_block(q, carry):
        for a in range(RA):
            rows = pl.ds(q * (NT * RA) + a, NT, stride=RA)
            o_ref[rows, :] = gather(q, 0, a, None)
        mix = mix_ref[q, NT][:, : N_GRP * RA]
        for t in range(NT):
            at = q * (NT * RA) + t * RA
            rows = [
                table[pl.ds(pl.multiple_of(at + h * PART, RA), RA), :]
                for h in range(N_GRP)
            ]
            alpha = jnp.dot(
                mix,
                jnp.concatenate(rows, axis=0),
                precision=HIGH,
                preferred_element_type=jnp.float32,
            )
            target = pl.ds(pl.multiple_of(at, RA), RA)
            o_ref[target, :] = o_ref[target, :] + alpha
        return carry

    def later_chunk(k, carry):
        for copy in index_copies(k):
            copy.wait()

        def block(q, inner):
            for a in range(RA):
                rows = pl.ds(q * (NT * RA) + a, NT, stride=RA)
                o_ref[rows, :] = gather(q, k * length, a, o_ref[rows, :])
            return inner

        return lax.fori_loop(0, NQ, block, carry)

    for copy in index_copies(0):
        copy.wait()
    lax.fori_loop(0, NQ, first_block, 0)
    lax.fori_loop(1, chunks, later_chunk, 0)


def mixed_call(sel, cidx, widx, wtab, mix, parts, n_exc, row_count, chunks=3):
    count = N_GRP * NS
    return pl.pallas_call(
        functools.partial(mixed_kernel, n_exc, row_count, chunks),
        out_shape=jax.ShapeDtypeStruct((PART, LANES), jnp.float32),
        in_specs=[SMEM, ANY, ANY, VMEM, VMEM] + [ANY] * count,
        out_specs=VMEM,
        scratch_shapes=[
            pltpu.VMEM((count * PART, LANES), jnp.float32),
            pltpu.SMEM((n_exc * row_count,), jnp.int32),
            pltpu.SMEM((n_exc * row_count,), jnp.int32),
            pltpu.SemaphoreType.DMA((count,)),
            pltpu.SemaphoreType.DMA((2, chunks)),
        ],
        compiler_params=pltpu.CompilerParams(vmem_limit_bytes=16 << 20),
        cost_estimate=pl.CostEstimate(
            flops=n_exc * row_count * NT * LANES // 2,
            bytes_accessed=8 << 20,
            transcendentals=0,
        ),
        name="mixed",
    )(sel, cidx, widx, wtab, mix, *parts)


def per_device(
    coeff,
    beta_blocks,
    block_list,
    alpha_blocks,
    partner_mask,
    exc_source,
    exc_pair,
    exc_parity,
    occupation,
    coulomb,
):
    g = lax.axis_index("grp")
    xl = lax.axis_index("xl")
    c = lax.axis_index("c")
    alpha_rows, beta_width = coeff.shape
    n_exc, row_count = exc_source.shape
    n_pair = coulomb.shape[0]

    def shift(value, k):
        return lax.ppermute(
            value, "grp", [(i, (i - k) % N_GRP) for i in range(N_GRP)]
        )

    def swap(value, axis):
        return lax.ppermute(value, axis, [(0, 1), (1, 0)])

    packed = pack(g.reshape(1), partner_mask, coeff, alpha_blocks)
    arrived = lax.all_to_all(
        packed, ("z", "xh"), split_axis=0, concat_axis=0, tiled=True
    )

    sel = xl * NC + c
    pieces = [
        lax.ppermute(occupation, ("xl", "c"), [(i, i ^ k) for i in range(NS)])
        for k in range(1, NS)
    ]
    pieces = jnp.stack([occupation] + pieces)
    ordered = [
        lax.dynamic_index_in_dim(pieces, sel ^ k, 0, keepdims=False) for k in range(NS)
    ]
    occ = jnp.concatenate(ordered, axis=1).astype(jnp.float32)
    weights = jnp.dot(coulomb, occ, precision=HIGH, preferred_element_type=jnp.float32)
    signed = jnp.concatenate([weights, -weights], axis=0)
    wtab = (
        signed.reshape(2 * n_pair // RA, RA, NT, LANES)
        .transpose(0, 2, 1, 3)
        .reshape(2 * n_pair * NT, LANES)
    )

    rel_g = ((exc_source >> 9) - g) & (N_GRP - 1)
    rel_s = ((exc_source >> 3) & (NS - 1)) ^ sel
    pos = (rel_s * N_GRP + rel_g) * NQ + ((exc_source >> 5) & (NQ - 1))
    cidx = (pos * (NT * RA) + (exc_source & (RA - 1))).reshape(-1)
    pair = exc_pair + n_pair * exc_parity
    widx = ((pair >> 3) * (NT * RA) + (pair & (RA - 1))).reshape(-1)

    arrived, wtab, cidx, widx, late = lax.optimization_barrier(
        (arrived, wtab, cidx, widx, coeff)
    )
    own = arrived[:, :NT].reshape(PART, LANES)
    near = [own] + [shift(own, k) for k in range(1, N_GRP)]
    across = [swap(near[0], "xl"), swap(near[1], "xl"), None, swap(near[3], "xl")]
    across[2] = shift(across[0], 2)
    parts = (
        near
        + [swap(v, "c") for v in near]
        + across
        + [swap(v, "c") for v in across]
    )
    mixed_local = mixed_call(
        sel.reshape(1).astype(jnp.int32),
        cidx,
        widx,
        wtab,
        arrived,
        parts,
        n_exc,
        row_count,
    )
    mixed = lax.all_to_all(
        mixed_local.reshape(NQ, NT, RA, LANES),
        ("z", "xh"),
        split_axis=0,
        concat_axis=0,
        tiled=True,
    )
    mixed = (
        mixed.reshape(NQ * NT, RA, LANES).transpose(1, 0, 2).reshape(alpha_rows, -1)
    )

    block_size = beta_blocks.shape[1]
    block_count = beta_width // block_size
    blocked = late.reshape(alpha_rows, block_count, block_size)
    block_ids = jnp.arange(block_count, dtype=jnp.int32)
    choosing = (block_list[0][:, None] == block_ids[None, :]).astype(jnp.float32)
    picked = jnp.einsum("rnk,pn->rpk", blocked, choosing, precision=HIGH)
    applied = jnp.einsum("rpk,pkl->rpl", picked, beta_blocks, precision=HIGH)
    placing = (block_list[1][:, None] == block_ids[None, :]).astype(jnp.float32)
    same_beta = jnp.einsum("rpl,pn->rnl", applied, placing, precision=HIGH).reshape(
        alpha_rows, beta_width
    )

    return mixed + same_beta


def solution(mesh):
    wide = ("z", "xh", "xl", "c")
    fine = Mesh(mesh.devices.reshape(N_GRP, NZ, NXH, NXL, NC), ("grp",) + wide)
    every = ("grp",) + wide
    in_specs = (
        P(every, None),
        P(),
        P(),
        P(every, None, None, None),
        P(every, None),
        P(None, "grp"),
        P(None, "grp"),
        P(None, "grp"),
        P(None, wide),
        P(),
    )
    return jax.shard_map(
        per_device,
        mesh=fine,
        in_specs=in_specs,
        out_specs=P(every, None),
        check_vma=False,
    )
```

time: 96.7 us -> 97.1 us (level)
  Pallas kernels: 35.5 us -> 21.5 us
  waiting for transfers between devices: 24.4 us -> 34.4 us
  starting transfers between devices: 22.3 us -> 28.1 us
    pallas_call x1, Pallas kernels: 31.8 us -> 19.7 us  [mixed_call(): pl.pallas_call(functools.partial(mixed_kernel, n_exc, row_count, chunks),...]
    ppermute x5 -> x14, waiting for transfers between devices: 1.13 us -> 8.09 us  [the longest x11 8.08 us: swap(): return lax.ppermute(value, axis, [(0, 1), (1, 0)])]
    ppermute x5 -> x14, starting transfers between devices: 0.49 us -> 7.34 us  [the longest x11 4.93 us: swap(): return lax.ppermute(value, axis, [(0, 1), (1, 0)])]
    all_to_all x2, waiting for transfers between devices: 11 us -> 16 us  [the longest x1 10.2 us: per_device(): lax.all_to_all(packed, ('z', 'xh'), split_axis=0, concat_axis=0, tiled=True)]
    all_to_all x2, starting transfers between devices: 17.2 us -> 13.2 us  [the longest x1 9.7 us: per_device(): lax.all_to_all(packed, ('z', 'xh'), split_axis=0, concat_axis=0, tiled=True)]
    ppermute x3 -> x4, starting transfers between devices: 4.61 us -> 7.5 us  [shift(): lax.ppermute(value, 'grp', [(i, (i - k) % N_GRP) for i in range(N_GRP)])]
    ppermute x3 -> x4, waiting for transfers between devices: 12.3 us -> 10.3 us  [shift(): lax.ppermute(value, 'grp', [(i, (i - k) % N_GRP) for i in range(N_GRP)])]
    pallas_call x2 -> x1, Pallas kernels: 3.67 us -> 1.72 us  [pack(): pl.pallas_call(pack_kernel, out_shape=jax.ShapeDtypeStruct((NQ, NT + 1, R...]
  transfers between devices with their start and end apart: 10 -> 20, of which waited for: 6 -> 9; matrix products, arithmetic and copies ran while one was open for 13% -> 12% of each run, Pallas kernels for 2% -> 2%
where the time goes in v3:
time: 97.1 us; the launch traced here: 96.7 us
  waiting for transfers between devices  34.4 us (35%)
  starting transfers between devices  28.1 us (29%)
  Pallas kernels  21.5 us (22%)
  matrix products  8.88 us (9%)
  other arithmetic  2.89 us (3%)
    pallas_call x1, Pallas kernels, mixed_call(): pl.pallas_call(functools.partial(mixed_kernel, n_exc, row_count, chunks),...  19.7 us
    ppermute x4, waiting for transfers between devices, shift(): lax.ppermute(value, 'grp', [(i, (i - k) % N_GRP) for i in range(N_GRP)])  10.3 us
    all_to_all x1, waiting for transfers between devices, per_device(): lax.all_to_all(packed, ('z', 'xh'), split_axis=0, concat_axis=0, tiled=True)  10.2 us
    all_to_all x1, starting transfers between devices, per_device(): lax.all_to_all(packed, ('z', 'xh'), split_axis=0, concat_axis=0, tiled=True)  9.7 us
    ppermute x11, waiting for transfers between devices, swap(): return lax.ppermute(value, axis, [(0, 1), (1, 0)])  8.08 us
    ppermute x4, starting transfers between devices, shift(): lax.ppermute(value, 'grp', [(i, (i - k) % N_GRP) for i in range(N_GRP)])  7.5 us
    dot_general x1, matrix products, per_device(): applied = jnp.einsum('rpk,pkl->rpl', picked, beta_blocks, precision=HIGH)  7.46 us
    all_to_all x1, waiting for transfers between devices, per_device(): lax.all_to_all(mixed_local.reshape(NQ, NT, RA, LANES), ('z', 'xh'), split...  5.8 us
  transfers between devices with their start and end apart: 20, of which 9 were waited for; matrix products, arithmetic and copies ran while one was open for 12% of the time, Pallas kernels for 2%

profile of v3, /device:TPU:2, one launch (start us, length us, event | category | flops | bytes accessed | tf_op | source)
XLA Modules:
  0.0 96.7 jit_solution(4536182048866698678)
XLA Ops:
  0.0 0.1 collective-permute-start
  0.1 2.3 %collective-permute-start.1 = (s32[18,96]{1,0:T(8,128)}, s32[18,96]{1,0:T(8,128)S(1)}, u32[]{:S(2)}, u32[]{:S(2)}) collective-permute-start(s32[18,96]{1,0:T(8,128)} %param.18), channel_id=1, source_target_pairs={{0,2},{1,3},{2,0},{3,1},{4,6},{5,7},{6,4},{7,5},{8,10},{9,11},{10,... | collective-permute-start | bytes 20744 | tf_op jit(solution)/shard_map/ppermute | solution.py:191
  2.4 0.1 collective-permute-start.2
  2.4 1.7 %pack.1 = f32[16,4,8,128]{3,2,1,0:T(8,128)} custom-call(s32[1]{0:T(128)} %bitcast.1.g_ref, s32[1,4]{1,0:T(1,128)} %mask_ref.1, f32[8,6144]{1,0:T(8,128)} %x_ref.1, f32[1,4,8,8]{3,2,1,0:T(8,128)} %alpha_ref.1), custom_call_target="tpu_custom_call" | custom-call | tf_op jit(solution)/shard_map/pack/pallas_call | solution.py:41
  4.1 9.7 %all-to-all-start = ((f32[16,4,8,128]{3,2,1,0:T(8,128)}), f32[16,4,8,128]{3,2,1,0:T(8,128)S(1)}, u32[]{:S(2)}, u32[]{:S(2)}) async-start(f32[16,4,8,128]{3,2,1,0:T(8,128)} %pack.1), calls=%async_computation | async-start | bytes 524288 | tf_op jit(solution)/shard_map/all_to_all | solution.py:185
  13.9 1.1 %and_add_fusion = s32[90,512]{1,0:T(8,128)S(1)} fusion(s32[90,512]{1,0:T(8,128)} %param.16, s32[90,512]{1,0:T(8,128)} %param.17), kind=kLoop, calls=%fused_computation.13 | loop fusion | flops 276480 | bytes 552960 | tf_op jit(solution)/shard_map/add | solution.py:212
  14.9 1.0 %and_add_fusion.1 = s32[90,512]{1,0:T(8,128)S(1)} fusion(s32[90,512]{1,0:T(8,128)} %param.15, s32[]{:T(128)} %axis_index.38, s32[]{:T(128)} %add.40), kind=kLoop, calls=%fused_computation.14 | loop fusion | flops 691200 | bytes 368648 | tf_op jit(solution)/shard_map/add | solution.py:210
  16.0 0.0 collective-permute-done
  16.1 0.0 collective-permute-done.1
  16.1 0.0 collective-permute-done.2
  16.1 0.7 pad_add_fusion
  16.8 0.8 fusion.26
  17.6 0.1 pad_maximum_fusion
  17.7 10.2 %all-to-all-done.mix_ref = f32[16,4,8,128]{3,2,1,0:T(8,128)S(1)} async-done(((f32[16,4,8,128]{3,2,1,0:T(8,128)}), f32[16,4,8,128]{3,2,1,0:T(8,128)S(1)}, u32[]{:S(2)}, u32[]{:S(2)}) %all-to-all-start) | async-done | bytes 262176 | tf_op jit(solution)/shard_map/all_to_all | solution.py:185
  27.8 1.5 %collective-permute-start.10 = (f32[384,128]{1,0:T(8,128)S(1)}, f32[384,128]{1,0:T(8,128)S(1)}, u32[]{:S(2)}, u32[]{:S(2)}) collective-permute-start(f32[384,128]{1,0:T(8,128)S(1)} %bitcast.54), channel_id=1, source_target_pairs={{0,2},{2,0},{1,3},{3,1},{4,6},{6,4},{5,7},{7,5},{8,10},{10,8},{9,1... | collective-permute-start | bytes 589832 | tf_op jit(solution)/shard_map/ppermute | solution.py:182
  29.4 3.0 %collective-permute-start.3 = (f32[384,128]{1,0:T(8,128)S(1)}, f32[384,128]{1,0:T(8,128)S(1)}, u32[]{:S(2)}, u32[]{:S(2)}) collective-permute-start(f32[384,128]{1,0:T(8,128)S(1)} %bitcast.55), channel_id=1, source_target_pairs={{0,192},{64,0},{128,64},{192,128},{1,193},{65,1},{129,65},{193,129... | collective-permute-start | bytes 589832 | tf_op jit(solution)/shard_map/ppermute | solution.py:177
  32.4 0.0 collective-permute-start.5
  32.4 2.2 %collective-permute-start.4 = (f32[384,128]{1,0:T(8,128)S(1)}, f32[384,128]{1,0:T(8,128)S(1)}, u32[]{:S(2)}, u32[]{:S(2)}) collective-permute-start(f32[384,128]{1,0:T(8,128)S(1)} %bitcast.57), channel_id=1, source_target_pairs={{0,128},{64,192},{128,0},{192,64},{1,129},{65,193},{129,1},{193,65... | collective-permute-start | bytes 589832 | tf_op jit(solution)/shard_map/ppermute | solution.py:177
  34.6 0.0 collective-permute-start.6
  34.6 0.0 collective-permute-done.10.rest_8_
  34.6 2.3 %collective-permute-start.12 = (f32[384,128]{1,0:T(8,128)S(1)}, f32[384,128]{1,0:T(8,128)S(1)}, u32[]{:S(2)}, u32[]{:S(2)}) collective-permute-start(f32[384,128]{1,0:T(8,128)S(1)} %collective-permute-done.10.rest_8_), channel_id=1, source_target_pairs={{0,128},{64,192},{128,0},{192,64},{1,129},{65,193},{129,1},{193,65... | collective-permute-start | bytes 589832 | tf_op jit(solution)/shard_map/ppermute | solution.py:177
  36.9 7.2 %collective-permute-done.3.rest_1_ = f32[384,128]{1,0:T(8,128)S(1)} collective-permute-done((f32[384,128]{1,0:T(8,128)S(1)}, f32[384,128]{1,0:T(8,128)S(1)}, u32[]{:S(2)}, u32[]{:S(2)}) %collective-permute-start.3) | collective-permute-done | bytes 196640 | tf_op jit(solution)/shard_map/ppermute | solution.py:177
  44.0 0.0 collective-permute-start.14
  44.0 3.2 %collective-permute-done.5.rest_3_ = f32[384,128]{1,0:T(8,128)S(1)} collective-permute-done((f32[384,128]{1,0:T(8,128)S(1)}, f32[384,128]{1,0:T(8,128)S(1)}, u32[]{:S(2)}, u32[]{:S(2)}) %collective-permute-start.5) | collective-permute-done | bytes 196640 | tf_op jit(solution)/shard_map/ppermute | solution.py:177
  47.2 0.6 collective-permute-start.11
  47.8 0.0 collective-permute-done.4.rest_2_
  47.8 0.0 collective-permute-start.7
  47.8 0.0 collective-permute-done.6.rest_4_
  47.8 1.5 %collective-permute-start.13 = (f32[384,128]{1,0:T(8,128)S(1)}, f32[384,128]{1,0:T(8,128)S(1)}, u32[]{:S(2)}, u32[]{:S(2)}) collective-permute-start(f32[384,128]{1,0:T(8,128)S(1)} %collective-permute-done.5.rest_3_), channel_id=1, source_target_pairs={{0,2},{2,0},{1,3},{3,1},{4,6},{6,4},{5,7},{7,5},{8,10},{10,8},{9,1... | collective-permute-start | bytes 589832 | tf_op jit(solution)/shard_map/ppermute | solution.py:182
  49.3 5.5 %collective-permute-done.11.rest_9_ = f32[384,128]{1,0:T(8,128)S(1)} collective-permute-done((f32[384,128]{1,0:T(8,128)S(1)}, f32[384,128]{1,0:T(8,128)S(1)}, u32[]{:S(2)}, u32[]{:S(2)}) %collective-permute-start.11) | collective-permute-done | bytes 196640 | tf_op jit(solution)/shard_map/ppermute | solution.py:182
  54.8 0.0 collective-permute-start.9
  54.8 0.0 collective-permute-done.12.rest_10_
  54.8 0.5 collective-permute-start.8
  55.3 1.8 %collective-permute-done.13.rest_11_ = f32[384,128]{1,0:T(8,128)S(1)} collective-permute-done((f32[384,128]{1,0:T(8,128)S(1)}, f32[384,128]{1,0:T(8,128)S(1)}, u32[]{:S(2)}, u32[]{:S(2)}) %collective-permute-start.13) | collective-permute-done | bytes 196640 | tf_op jit(solution)/shard_map/ppermute | solution.py:182
  57.1 0.0 collective-permute-start.15
  57.1 0.5 collective-permute-start.16
  57.6 0.3 collective-permute-start.17
  57.9 0.3 fusion.6
  58.2 0.0 collective-permute-done.9.rest_7_
  58.3 0.3 collective-permute-done.15.rest_13_
  58.5 0.3 collective-permute-done.16.rest_14_
  58.8 0.3 collective-permute-done.17.rest_15_
  59.1 19.7 %mixed.1 = f32[384,128]{1,0:T(8,128)} custom-call(s32[1]{0:T(128)} %bitcast.sel_ref, s32[46080]{0:T(1024)S(1)} %reshape.39.cidx_hbm, s32[46080]{0:T(1024)S(1)} %reshape.40.widx_hbm, f32[1944,128]{1,0:T(8,128)S(1)} %bitcast.53, f32[16,4,8,128]{3,2,1,0:T(8,128)S(1)} %all-to-all-done.mix_ref, f32[384,128]{1,0:T(8,128)S(1)} %bitcast.59, ...), custom_call_target="tpu_custom_call" | custom-call | flops 8847360 | bytes 8388608 | tf_op jit(solution)/shard_map/mixed/pallas_call | solution.py:135
  78.8 3.5 %all-to-all-start.1 = ((f32[16,3,8,128]{3,2,1,0:T(8,128)}), f32[16,3,8,128]{3,2,1,0:T(8,128)S(1)}, u32[]{:S(2)}, u32[]{:S(2)}) async-start(f32[16,3,8,128]{3,2,1,0:T(8,128)} %bitcast.15), calls=%async_computation.1 | async-start | bytes 393216 | tf_op jit(solution)/shard_map/all_to_all | solution.py:237
  82.4 7.5 %fusion.2 = f32[96,8,128]{2,1,0:T(8,128)S(1)} fusion(f32[96,128,128]{2,1,0:T(8,128)} %param.11, f32[96,8,128]{2,0,1:T(8,128)S(1)} %fusion.6), kind=kOutput, calls=%fused_computation.4 | convolution fusion | flops 150994944 | bytes 7077888 | tf_op jit(solution)/shard_map/rpk,pkl->rpl/dot_general | solution.py:254
  89.8 5.8 %all-to-all-done.1 = f32[16,3,8,128]{3,2,1,0:T(8,128)S(1)} async-done(((f32[16,3,8,128]{3,2,1,0:T(8,128)}), f32[16,3,8,128]{3,2,1,0:T(8,128)S(1)}, u32[]{:S(2)}, u32[]{:S(2)}) %all-to-all-start.1) | async-done | bytes 196640 | tf_op jit(solution)/shard_map/all_to_all | solution.py:237
  95.6 0.3 fusion.8
  96.0 0.7 copy.33
  (14 shorter events, 0.1 us)
Async XLA Ops:
  0.0 16.8 %copy-start = (f32[324,18]{0,1:T(8,128)S(1)}, f32[324,18]{0,1:T(8,128)}, u32[]{:S(2)}) copy-start(f32[324,18]{0,1:T(8,128)} %param.19) | copy-start | bytes 69988
  0.0 57.9 %copy-start.1 = (f32[8,6144]{1,0:T(8,128)S(1)}, f32[8,6144]{1,0:T(8,128)}, u32[]{:S(2)}) copy-start(f32[8,6144]{1,0:T(8,128)} %x_ref.1) | copy-start | bytes 589828
  0.0 49.3 %copy-start.2 = (s32[2,96]{1,0:T(2,128)S(1)}, s32[2,96]{1,0:T(2,128)}, u32[]{:S(2)}) copy-start(s32[2,96]{1,0:T(2,128)} %param.12) | copy-start | bytes 2308
  0.0 16.0 %collective-permute-start = (s32[18,96]{1,0:T(8,128)}, s32[18,96]{1,0:T(8,128)S(1)}, u32[]{:S(2)}, u32[]{:S(2)}) collective-permute-start(s32[18,96]{1,0:T(8,128)} %param.18), channel_id=1, source_target_pairs={{0,1},{1,0},{2,3},{3,2},{4,5},{5,4},{6,7},{7,6},{8,9},{9,8},{10,11... | collective-permute-start | bytes 20744 | tf_op jit(solution)/shard_map/ppermute | solution.py:191
  0.1 15.9 %collective-permute-start.1 = (s32[18,96]{1,0:T(8,128)}, s32[18,96]{1,0:T(8,128)S(1)}, u32[]{:S(2)}, u32[]{:S(2)}) collective-permute-start(s32[18,96]{1,0:T(8,128)} %param.18), channel_id=1, source_target_pairs={{0,2},{1,3},{2,0},{3,1},{4,6},{5,7},{6,4},{7,5},{8,10},{9,11},{10,... | collective-permute-start | bytes 20744 | tf_op jit(solution)/shard_map/ppermute | solution.py:191
  2.4 13.7 %collective-permute-start.2 = (s32[18,96]{1,0:T(8,128)}, s32[18,96]{1,0:T(8,128)S(1)}, u32[]{:S(2)}, u32[]{:S(2)}) collective-permute-start(s32[18,96]{1,0:T(8,128)} %param.18), channel_id=1, source_target_pairs={{0,3},{1,2},{2,1},{3,0},{4,7},{5,6},{6,5},{7,4},{8,11},{9,10},{10,... | collective-permute-start | bytes 20744 | tf_op jit(solution)/shard_map/ppermute | solution.py:191
  4.1 23.7 %all-to-all-start = ((f32[16,4,8,128]{3,2,1,0:T(8,128)}), f32[16,4,8,128]{3,2,1,0:T(8,128)S(1)}, u32[]{:S(2)}, u32[]{:S(2)}) async-start(f32[16,4,8,128]{3,2,1,0:T(8,128)} %pack.1), calls=%async_computation | async-start | bytes 524288 | tf_op jit(solution)/shard_map/all_to_all | solution.py:185
  27.8 6.7 %collective-permute-start.10 = (f32[384,128]{1,0:T(8,128)S(1)}, f32[384,128]{1,0:T(8,128)S(1)}, u32[]{:S(2)}, u32[]{:S(2)}) collective-permute-start(f32[384,128]{1,0:T(8,128)S(1)} %bitcast.54), channel_id=1, source_target_pairs={{0,2},{2,0},{1,3},{3,1},{4,6},{6,4},{5,7},{7,5},{8,10},{10,8},{9,1... | collective-permute-start | bytes 589832 | tf_op jit(solution)/shard_map/ppermute | solution.py:182
  29.4 14.7 %collective-permute-start.3 = (f32[384,128]{1,0:T(8,128)S(1)}, f32[384,128]{1,0:T(8,128)S(1)}, u32[]{:S(2)}, u32[]{:S(2)}) collective-permute-start(f32[384,128]{1,0:T(8,128)S(1)} %bitcast.55), channel_id=1, source_target_pairs={{0,192},{64,0},{128,64},{192,128},{1,193},{65,1},{129,65},{193,129... | collective-permute-start | bytes 589832 | tf_op jit(solution)/shard_map/ppermute | solution.py:177
  32.4 14.8 %collective-permute-start.5 = (f32[384,128]{1,0:T(8,128)S(1)}, f32[384,128]{1,0:T(8,128)S(1)}, u32[]{:S(2)}, u32[]{:S(2)}) collective-permute-start(f32[384,128]{1,0:T(8,128)S(1)} %bitcast.56), channel_id=1, source_target_pairs={{0,64},{64,128},{128,192},{192,0},{1,65},{65,129},{129,193},{193,1... | collective-permute-start | bytes 589832 | tf_op jit(solution)/shard_map/ppermute | solution.py:177
  32.4 15.4 %collective-permute-start.4 = (f32[384,128]{1,0:T(8,128)S(1)}, f32[384,128]{1,0:T(8,128)S(1)}, u32[]{:S(2)}, u32[]{:S(2)}) collective-permute-start(f32[384,128]{1,0:T(8,128)S(1)} %bitcast.57), channel_id=1, source_target_pairs={{0,128},{64,192},{128,0},{192,64},{1,129},{65,193},{129,1},{193,65... | collective-permute-start | bytes 589832 | tf_op jit(solution)/shard_map/ppermute | solution.py:177
  34.6 13.2 %collective-permute-start.6 = (f32[384,128]{1,0:T(8,128)S(1)}, f32[384,128]{1,0:T(8,128)S(1)}, u32[]{:S(2)}, u32[]{:S(2)}) collective-permute-start(f32[384,128]{1,0:T(8,128)S(1)} %bitcast.58), channel_id=1, source_target_pairs={{0,1},{1,0},{2,3},{3,2},{4,5},{5,4},{6,7},{7,6},{8,9},{9,8},{10,11... | collective-permute-start | bytes 589832 | tf_op jit(solution)/shard_map/ppermute | solution.py:182
  34.6 20.2 %collective-permute-start.12 = (f32[384,128]{1,0:T(8,128)S(1)}, f32[384,128]{1,0:T(8,128)S(1)}, u32[]{:S(2)}, u32[]{:S(2)}) collective-permute-start(f32[384,128]{1,0:T(8,128)S(1)} %collective-permute-done.10.rest_8_), channel_id=1, source_target_pairs={{0,128},{64,192},{128,0},{192,64},{1,129},{65,193},{129,1},{193,65... | collective-permute-start | bytes 589832 | tf_op jit(solution)/shard_map/ppermute | solution.py:177
  44.0 13.1 %collective-permute-start.14 = (f32[384,128]{1,0:T(8,128)S(1)}, f32[384,128]{1,0:T(8,128)S(1)}, u32[]{:S(2)}, u32[]{:S(2)}) collective-permute-start(f32[384,128]{1,0:T(8,128)S(1)} %collective-permute-done.10.rest_8_), channel_id=1, source_target_pairs={{0,1},{1,0},{2,3},{3,2},{4,5},{5,4},{6,7},{7,6},{8,9},{9,8},{10,11... | collective-permute-start | bytes 589832 | tf_op jit(solution)/shard_map/ppermute | solution.py:182
  47.2 7.6 %collective-permute-start.11 = (f32[384,128]{1,0:T(8,128)S(1)}, f32[384,128]{1,0:T(8,128)S(1)}, u32[]{:S(2)}, u32[]{:S(2)}) collective-permute-start(f32[384,128]{1,0:T(8,128)S(1)} %collective-permute-done.3.rest_1_), channel_id=1, source_target_pairs={{0,2},{2,0},{1,3},{3,1},{4,6},{6,4},{5,7},{7,5},{8,10},{10,8},{9,1... | collective-permute-start | bytes 589832 | tf_op jit(solution)/shard_map/ppermute | solution.py:182
  47.8 9.8 %collective-permute-start.7 = (f32[384,128]{1,0:T(8,128)S(1)}, f32[384,128]{1,0:T(8,128)S(1)}, u32[]{:S(2)}, u32[]{:S(2)}) collective-permute-start(f32[384,128]{1,0:T(8,128)S(1)} %collective-permute-done.3.rest_1_), channel_id=1, source_target_pairs={{0,1},{1,0},{2,3},{3,2},{4,5},{5,4},{6,7},{7,6},{8,9},{9,8},{10,11... | collective-permute-start | bytes 589832 | tf_op jit(solution)/shard_map/ppermute | solution.py:182
  47.8 9.3 %collective-permute-start.13 = (f32[384,128]{1,0:T(8,128)S(1)}, f32[384,128]{1,0:T(8,128)S(1)}, u32[]{:S(2)}, u32[]{:S(2)}) collective-permute-start(f32[384,128]{1,0:T(8,128)S(1)} %collective-permute-done.5.rest_3_), channel_id=1, source_target_pairs={{0,2},{2,0},{1,3},{3,1},{4,6},{6,4},{5,7},{7,5},{8,10},{10,8},{9,1... | collective-permute-start | bytes 589832 | tf_op jit(solution)/shard_map/ppermute | solution.py:182
  54.8 3.4 %collective-permute-start.9 = (f32[384,128]{1,0:T(8,128)S(1)}, f32[384,128]{1,0:T(8,128)S(1)}, u32[]{:S(2)}, u32[]{:S(2)}) collective-permute-start(f32[384,128]{1,0:T(8,128)S(1)} %collective-permute-done.5.rest_3_), channel_id=1, source_target_pairs={{0,1},{1,0},{2,3},{3,2},{4,5},{5,4},{6,7},{7,6},{8,9},{9,8},{10,11... | collective-permute-start | bytes 589832 | tf_op jit(solution)/shard_map/ppermute | solution.py:182
  54.8 3.4 %collective-permute-start.8 = (f32[384,128]{1,0:T(8,128)S(1)}, f32[384,128]{1,0:T(8,128)S(1)}, u32[]{:S(2)}, u32[]{:S(2)}) collective-permute-start(f32[384,128]{1,0:T(8,128)S(1)} %collective-permute-done.4.rest_2_), channel_id=1, source_target_pairs={{0,1},{1,0},{2,3},{3,2},{4,5},{5,4},{6,7},{7,6},{8,9},{9,8},{10,11... | collective-permute-start | bytes 589832 | tf_op jit(solution)/shard_map/ppermute | solution.py:182
  57.1 1.4 %collective-permute-start.15 = (f32[384,128]{1,0:T(8,128)S(1)}, f32[384,128]{1,0:T(8,128)S(1)}, u32[]{:S(2)}, u32[]{:S(2)}) collective-permute-start(f32[384,128]{1,0:T(8,128)S(1)} %collective-permute-done.11.rest_9_), channel_id=1, source_target_pairs={{0,1},{1,0},{2,3},{3,2},{4,5},{5,4},{6,7},{7,6},{8,9},{9,8},{10,11... | collective-permute-start | bytes 589832 | tf_op jit(solution)/shard_map/ppermute | solution.py:182
  57.1 1.7 %collective-permute-start.16 = (f32[384,128]{1,0:T(8,128)S(1)}, f32[384,128]{1,0:T(8,128)S(1)}, u32[]{:S(2)}, u32[]{:S(2)}) collective-permute-start(f32[384,128]{1,0:T(8,128)S(1)} %collective-permute-done.12.rest_10_), channel_id=1, source_target_pairs={{0,1},{1,0},{2,3},{3,2},{4,5},{5,4},{6,7},{7,6},{8,9},{9,8},{10,11... | collective-permute-start | bytes 589832 | tf_op jit(solution)/shard_map/ppermute | solution.py:182
  57.6 1.5 %collective-permute-start.17 = (f32[384,128]{1,0:T(8,128)S(1)}, f32[384,128]{1,0:T(8,128)S(1)}, u32[]{:S(2)}, u32[]{:S(2)}) collective-permute-start(f32[384,128]{1,0:T(8,128)S(1)} %collective-permute-done.13.rest_11_), channel_id=1, source_target_pairs={{0,1},{1,0},{2,3},{3,2},{4,5},{5,4},{6,7},{7,6},{8,9},{9,8},{10,11... | collective-permute-start | bytes 589832 | tf_op jit(solution)/shard_map/ppermute | solution.py:182
  78.8 16.8 %all-to-all-start.1 = ((f32[16,3,8,128]{3,2,1,0:T(8,128)}), f32[16,3,8,128]{3,2,1,0:T(8,128)S(1)}, u32[]{:S(2)}, u32[]{:S(2)}) async-start(f32[16,3,8,128]{3,2,1,0:T(8,128)} %bitcast.15), calls=%async_computation.1 | async-start | bytes 393216 | tf_op jit(solution)/shard_map/all_to_all | solution.py:237

commit v4 on v3

--- a/solution.py
+++ b/solution.py
@@ -17,6 +17,8 @@
 NS = NXL * NC
 NT = 3
 PART = NQ * NT * RA
+EPAD = 96
+CHUNK = 32
 
 SMEM = pl.BlockSpec(memory_space=pltpu.SMEM)
 VMEM = pl.BlockSpec(memory_space=pltpu.VMEM)
@@ -47,14 +49,51 @@
     )(group, mask, coeff, alpha_blocks)
 
 
-def mixed_kernel(
-    n_exc, row_count, chunks, sel_ref, cidx_hbm, widx_hbm, w_ref, mix_ref, *rest
-):
+def prep_kernel(n_pair, place_ref, src_ref, pair_ref, par_ref, ci_ref, wi_ref):
+    g, sel = place_ref[0], place_ref[1]
+    n_exc, row_count = src_ref.shape
+    row = lax.broadcasted_iota(jnp.int32, (LANES, row_count), 0)
+    col = lax.broadcasted_iota(jnp.int32, (LANES, row_count), 1)
+    want = (row >> 3) * (NS * RA) + sel * RA + (row & (RA - 1))
+    pick = jnp.where(col == want, 1.0, 0.0)
+    src = src_ref[...]
+    rel_g = ((src >> 9) - g) & (N_GRP - 1)
+    rel_s = ((src >> 3) & (NS - 1)) ^ sel
+    pos = (rel_s * N_GRP + rel_g) * NQ + ((src >> 5) & (NQ - 1))
+    pair = pair_ref[...] + n_pair * par_ref[...]
+    for value, out in (
+        (pos * (NT * RA) + (src & (RA - 1)), ci_ref),
+        ((pair >> 3) * (NT * RA) + (pair & (RA - 1)), wi_ref),
+    ):
+        chosen = lax.dot_general(
+            value.astype(jnp.float32),
+            pick,
+            (((1,), (1,)), ((), ())),
+            precision=HIGH,
+            preferred_element_type=jnp.float32,
+        )
+        out[pl.ds(0, n_exc), :] = (chosen + 0.5).astype(jnp.int32)
+        out[pl.ds(n_exc, EPAD - n_exc), :] = jnp.zeros((EPAD - n_exc, LANES), jnp.int32)
+
+
+def prep_call(place, src, pair, par, n_pair):
+    shape = jax.ShapeDtypeStruct((EPAD, LANES), jnp.int32)
+    ci, wi = pl.pallas_call(
+        functools.partial(prep_kernel, n_pair),
+        out_shape=(shape, shape),
+        in_specs=[SMEM, VMEM, VMEM, VMEM],
+        out_specs=(VMEM, VMEM),
+        name="prep",
+    )(place, src, pair, par)
+    return ci.reshape(-1), wi.reshape(-1)
+
+
+def mixed_kernel(n_exc, cidx_hbm, widx_hbm, w_ref, mix_ref, *rest):
     count = N_GRP * NS
     parts = rest[:count]
-    o_ref, table, cidx, widx, part_sem, idx_sem = rest[count:]
-    per = n_exc // chunks
-    length = per * row_count
+    o_ref, table, cidx, widx, idx_sem = rest[count:]
+    chunks = EPAD // CHUNK
+    length = CHUNK * LANES
 
     def index_copies(k):
         at = pl.ds(k * length, length)
@@ -63,95 +102,75 @@
             pltpu.make_async_copy(widx_hbm.at[at], widx.at[at], idx_sem.at[1, k]),
         )
 
-    for copy in index_copies(0):
-        copy.start()
-    copies = [
-        pltpu.make_async_copy(part, table.at[pl.ds(i * PART, PART)], part_sem.at[i])
-        for i, part in enumerate(parts)
-    ]
-    for copy in copies:
-        copy.start()
-    for k in range(1, chunks):
+    for k in range(chunks):
         for copy in index_copies(k):
             copy.start()
-    for copy in copies:
-        copy.wait()
-    shift = sel_ref[0] * RA
-    size = row_count - RA + 1 + (n_exc - per) * row_count
-
-    def gather(q, offset, a, acc):
-        start = q * (NS * RA) + shift + offset
-        for e in range(per):
-            base = e * row_count + a
-            ci = cidx.at[pl.ds(base, size)][start]
-            wi = widx.at[pl.ds(base, size)][start]
-            term = (
-                table[pl.ds(ci, NT, stride=RA), :] * w_ref[pl.ds(wi, NT, stride=RA), :]
-            )
-            acc = term if acc is None else acc + term
-        return acc
-
-    def first_block(q, carry):
-        for a in range(RA):
-            rows = pl.ds(q * (NT * RA) + a, NT, stride=RA)
-            o_ref[rows, :] = gather(q, 0, a, None)
-        mix = mix_ref[q, NT][:, : N_GRP * RA]
-        for t in range(NT):
-            at = q * (NT * RA) + t * RA
-            rows = [
-                table[pl.ds(pl.multiple_of(at + h * PART, RA), RA), :]
-                for h in range(N_GRP)
-            ]
-            alpha = jnp.dot(
-                mix,
-                jnp.concatenate(rows, axis=0),
-                precision=HIGH,
-                preferred_element_type=jnp.float32,
-            )
-            target = pl.ds(pl.multiple_of(at, RA), RA)
-            o_ref[target, :] = o_ref[target, :] + alpha
-        return carry
-
-    def later_chunk(k, carry):
+    for i, part in enumerate(parts):
+        table[pl.ds(i * PART, PART), :] = part[...]
+    size = (NQ - 1) * RA + 1
+
+    for k in range(chunks):
         for copy in index_copies(k):
             copy.wait()
 
-        def block(q, inner):
+        def block(q, carry, k=k):
+            start = q * RA
             for a in range(RA):
                 rows = pl.ds(q * (NT * RA) + a, NT, stride=RA)
-                o_ref[rows, :] = gather(q, k * length, a, o_ref[rows, :])
-            return inner
-
-        return lax.fori_loop(0, NQ, block, carry)
-
-    for copy in index_copies(0):
-        copy.wait()
-    lax.fori_loop(0, NQ, first_block, 0)
-    lax.fori_loop(1, chunks, later_chunk, 0)
-
-
-def mixed_call(sel, cidx, widx, wtab, mix, parts, n_exc, row_count, chunks=3):
+                acc = None if k == 0 else o_ref[rows, :]
+                for e in range(k * CHUNK, min((k + 1) * CHUNK, n_exc)):
+                    base = e * LANES + a
+                    ci = cidx.at[pl.ds(base, size)][start]
+                    wi = widx.at[pl.ds(base, size)][start]
+                    term = (
+                        table[pl.ds(ci, NT, stride=RA), :]
+                        * w_ref[pl.ds(wi, NT, stride=RA), :]
+                    )
+                    acc = term if acc is None else acc + term
+                o_ref[rows, :] = acc
+            if k == 0:
+                mix = mix_ref[q, NT][:, : N_GRP * RA]
+                for t in range(NT):
+                    at = q * (NT * RA) + t * RA
+                    stacked = [
+                        table[pl.ds(pl.multiple_of(at + h * PART, RA), RA), :]
+                        for h in range(N_GRP)
+                    ]
+                    alpha = jnp.dot(
+                        mix,
+                        jnp.concatenate(stacked, axis=0),
+                        precision=HIGH,
+                        preferred_element_type=jnp.float32,
+                    )
+                    target = pl.ds(pl.multiple_of(at, RA), RA)
+                    o_ref[target, :] = o_ref[target, :] + alpha
+            return carry
+
+        lax.fori_loop(0, NQ, block, 0)
+
+
+def mixed_call(cidx, widx, wtab, mix, parts, n_exc):
     count = N_GRP * NS
+    index = pltpu.SMEM((EPAD * LANES,), jnp.int32)
     return pl.pallas_call(
-        functools.partial(mixed_kernel, n_exc, row_count, chunks),
+        functools.partial(mixed_kernel, n_exc),
         out_shape=jax.ShapeDtypeStruct((PART, LANES), jnp.float32),
-        in_specs=[SMEM, ANY, ANY, VMEM, VMEM] + [ANY] * count,
+        in_specs=[ANY, ANY, VMEM, VMEM] + [VMEM] * count,
         out_specs=VMEM,
         scratch_shapes=[
             pltpu.VMEM((count * PART, LANES), jnp.float32),
-            pltpu.SMEM((n_exc * row_count,), jnp.int32),
-            pltpu.SMEM((n_exc * row_count,), jnp.int32),
-            pltpu.SemaphoreType.DMA((count,)),
-            pltpu.SemaphoreType.DMA((2, chunks)),
+            index,
+            index,
+            pltpu.SemaphoreType.DMA((2, EPAD // CHUNK)),
         ],
         compiler_params=pltpu.CompilerParams(vmem_limit_bytes=16 << 20),
         cost_estimate=pl.CostEstimate(
-            flops=n_exc * row_count * NT * LANES // 2,
+            flops=n_exc * NQ * RA * NT * LANES * 2,
             bytes_accessed=8 << 20,
             transcendentals=0,
         ),
         name="mixed",
-    )(sel, cidx, widx, wtab, mix, *parts)
+    )(cidx, widx, wtab, mix, *parts)
 
 
 def per_device(
@@ -170,7 +189,7 @@
     xl = lax.axis_index("xl")
     c = lax.axis_index("c")
     alpha_rows, beta_width = coeff.shape
-    n_exc, row_count = exc_source.shape
+    n_exc = exc_source.shape[0]
     n_pair = coulomb.shape[0]
 
     def shift(value, k):
@@ -204,20 +223,20 @@
         .reshape(2 * n_pair * NT, LANES)
     )
 
-    rel_g = ((exc_source >> 9) - g) & (N_GRP - 1)
-    rel_s = ((exc_source >> 3) & (NS - 1)) ^ sel
-    pos = (rel_s * N_GRP + rel_g) * NQ + ((exc_source >> 5) & (NQ - 1))
-    cidx = (pos * (NT * RA) + (exc_source & (RA - 1))).reshape(-1)
-    pair = exc_pair + n_pair * exc_parity
-    widx = ((pair >> 3) * (NT * RA) + (pair & (RA - 1))).reshape(-1)
+    place = jnp.stack([g, sel]).astype(jnp.int32)
+    cidx, widx = prep_call(place, exc_source, exc_pair, exc_parity, n_pair)
 
     arrived, wtab, cidx, widx, late = lax.optimization_barrier(
         (arrived, wtab, cidx, widx, coeff)
     )
     own = arrived[:, :NT].reshape(PART, LANES)
-    near = [own] + [shift(own, k) for k in range(1, N_GRP)]
-    across = [swap(near[0], "xl"), swap(near[1], "xl"), None, swap(near[3], "xl")]
-    across[2] = shift(across[0], 2)
+    after, before = shift(own, 1), shift(own, N_GRP - 1)
+    over = swap(own, "xl")
+    again, over_again, after, before = lax.optimization_barrier(
+        (own, over, after, before)
+    )
+    near = [own, after, shift(again, 2), before]
+    across = [over, swap(after, "xl"), shift(over_again, 2), swap(before, "xl")]
     parts = (
         near
         + [swap(v, "c") for v in near]
@@ -225,14 +244,12 @@
         + [swap(v, "c") for v in across]
     )
     mixed_local = mixed_call(
-        sel.reshape(1).astype(jnp.int32),
         cidx,
         widx,
         wtab,
         arrived,
         parts,
         n_exc,
-        row_count,
     )
     mixed = lax.all_to_all(
         mixed_local.reshape(NQ, NT, RA, LANES),

time: 97.1 us -> 91.4 us (0.941)
  starting transfers between devices: 28.1 us -> 23.9 us
  local copies, waits for them, and re-layouts: 0.81 us -> 3.12 us
  Pallas kernels: 21.5 us -> 19.3 us
  other arithmetic: 2.89 us -> 1.44 us
  waiting for transfers between devices: 34.4 us -> 33.2 us
    ppermute x4, starting transfers between devices: 7.5 us -> 3.02 us  [shift(): lax.ppermute(value, 'grp', [(i, (i - k) % N_GRP) for i in range(N_GRP)])]
    ppermute x11, waiting for transfers between devices: 8.08 us -> 4.89 us  [swap(): return lax.ppermute(value, axis, [(0, 1), (1, 0)])]
    ppermute x4, waiting for transfers between devices: 10.3 us -> 13.3 us  [shift(): lax.ppermute(value, 'grp', [(i, (i - k) % N_GRP) for i in range(N_GRP)])]
    pallas_call x1 -> x2, Pallas kernels: 19.7 us -> 17.6 us  [the longest x1 15.1 us: mixed_call(): pl.pallas_call(functools.partial(mixed_kernel, n_exc), out_shape=jax.Shap...]
    add x2 -> x0, other arithmetic: 2.1 us -> none  [the longest x1 1.07 us: per_device(): widx = ((pair >> 3) * (NT * RA) + (pair & RA - 1)).reshape(-1)]
    unnamed x7, local copies, waits for them, and re-layouts: 0.75 us -> 2.33 us
  transfers between devices with their start and end apart: 20 -> 20, of which waited for: 9 -> 8; matrix products, arithmetic and copies ran while one was open for 12% -> 13% of each run, Pallas kernels for 2% -> 5%
where the time goes in v4:
time: 91.4 us; the launch traced here: 90.9 us
  waiting for transfers between devices  33.2 us (36%)
  starting transfers between devices  23.9 us (26%)
  Pallas kernels  19.3 us (21%)
  matrix products  9.81 us (11%)
  local copies, waits for them, and re-layouts  3.12 us (3%)
  other arithmetic  1.44 us (2%)
    pallas_call x1, Pallas kernels, mixed_call(): pl.pallas_call(functools.partial(mixed_kernel, n_exc), out_shape=jax.Shap...  15.1 us
    ppermute x4, waiting for transfers between devices, shift(): lax.ppermute(value, 'grp', [(i, (i - k) % N_GRP) for i in range(N_GRP)])  13.3 us
    all_to_all x1, starting transfers between devices, per_device(): lax.all_to_all(packed, ('z', 'xh'), split_axis=0, concat_axis=0, tiled=True)  9.6 us
    all_to_all x1, waiting for transfers between devices, per_device(): lax.all_to_all(packed, ('z', 'xh'), split_axis=0, concat_axis=0, tiled=True)  9.2 us
    dot_general x1, matrix products, per_device(): applied = jnp.einsum('rpk,pkl->rpl', picked, beta_blocks, precision=HIGH)  7.46 us
    all_to_all x1, waiting for transfers between devices, per_device(): lax.all_to_all(mixed_local.reshape(NQ, NT, RA, LANES), ('z', 'xh'), split...  5.8 us
    ppermute x11, starting transfers between devices, swap(): return lax.ppermute(value, axis, [(0, 1), (1, 0)])  5.35 us
    ppermute x11, waiting for transfers between devices, swap(): return lax.ppermute(value, axis, [(0, 1), (1, 0)])  4.89 us
  transfers between devices with their start and end apart: 20, of which 8 were waited for; matrix products, arithmetic and copies ran while one was open for 13% of the time, Pallas kernels for 5%

profile of v4, /device:TPU:2, one launch (start us, length us, event | category | flops | bytes accessed | tf_op | source)
XLA Modules:
  0.0 90.9 jit_solution(13621642496572526917)
XLA Ops:
  0.0 0.0 collective-permute-start
  0.0 2.3 %collective-permute-start.1 = (s32[18,96]{1,0:T(8,128)}, s32[18,96]{1,0:T(8,128)S(1)}, u32[]{:S(2)}, u32[]{:S(2)}) collective-permute-start(s32[18,96]{1,0:T(8,128)} %param.18), channel_id=1, source_target_pairs={{0,2},{1,3},{2,0},{3,1},{4,6},{5,7},{6,4},{7,5},{8,10},{9,11},{10,... | collective-permute-start | bytes 20744 | tf_op jit(solution)/shard_map/ppermute | solution.py:210
  2.3 0.1 collective-permute-start.2
  2.4 1.7 %pack.1 = f32[16,4,8,128]{3,2,1,0:T(8,128)} custom-call(s32[1]{0:T(128)} %bitcast.g_ref, s32[1,4]{1,0:T(1,128)} %mask_ref.1, f32[8,6144]{1,0:T(8,128)} %x_ref.1, f32[1,4,8,8]{3,2,1,0:T(8,128)} %alpha_ref.1), custom_call_target="tpu_custom_call" | custom-call | tf_op jit(solution)/shard_map/pack/pallas_call | solution.py:43
  4.2 9.6 %all-to-all-start = ((f32[16,4,8,128]{3,2,1,0:T(8,128)}), f32[16,4,8,128]{3,2,1,0:T(8,128)S(1)}, u32[]{:S(2)}, u32[]{:S(2)}) async-start(f32[16,4,8,128]{3,2,1,0:T(8,128)} %pack.1), calls=%async_computation | async-start | bytes 524288 | tf_op jit(solution)/shard_map/all_to_all | solution.py:204
  13.8 0.7 pad_add_fusion.1.place_ref
  14.4 2.5 %prep.1 = (s32[96,128]{1,0:T(8,128)}, s32[96,128]{1,0:T(8,128)}) custom-call(s32[2]{0:T(128)} %pad_add_fusion.1.place_ref, s32[90,512]{1,0:T(8,128)} %src_ref.1, s32[90,512]{1,0:T(8,128)} %pair_ref.1, s32[90,512]{1,0:T(8,128)} %par_ref.1), custom_call_target="tpu_custom_call" | custom-call | tf_op jit(solution)/shard_map/prep/pallas_call | solution.py:81
  16.9 0.0 collective-permute-done
  16.9 0.0 collective-permute-done.1
  16.9 0.0 collective-permute-done.2
  16.9 0.7 pad_add_fusion
  17.7 0.8 fusion.26
  18.5 0.1 pad_maximum_fusion
  18.5 9.2 %all-to-all-done.mix_ref = f32[16,4,8,128]{3,2,1,0:T(8,128)S(1)} async-done(((f32[16,4,8,128]{3,2,1,0:T(8,128)}), f32[16,4,8,128]{3,2,1,0:T(8,128)S(1)}, u32[]{:S(2)}, u32[]{:S(2)}) %all-to-all-start) | async-done | bytes 262176 | tf_op jit(solution)/shard_map/all_to_all | solution.py:204
  27.8 1.5 %collective-permute-start.3 = (f32[384,128]{1,0:T(8,128)S(1)}, f32[384,128]{1,0:T(8,128)S(1)}, u32[]{:S(2)}, u32[]{:S(2)}) collective-permute-start(f32[384,128]{1,0:T(8,128)S(1)} %bitcast.56), channel_id=1, source_target_pairs={{0,2},{2,0},{1,3},{3,1},{4,6},{6,4},{5,7},{7,5},{8,10},{10,8},{9,1... | collective-permute-start | bytes 589832 | tf_op jit(solution)/shard_map/ppermute | solution.py:201
  29.3 3.0 %collective-permute-start.4 = (f32[384,128]{1,0:T(8,128)S(1)}, f32[384,128]{1,0:T(8,128)S(1)}, u32[]{:S(2)}, u32[]{:S(2)}) collective-permute-start(f32[384,128]{1,0:T(8,128)S(1)} %bitcast.57), channel_id=1, source_target_pairs={{0,192},{64,0},{128,64},{192,128},{1,193},{65,1},{129,65},{193,129... | collective-permute-start | bytes 589832 | tf_op jit(solution)/shard_map/ppermute | solution.py:196
  32.3 0.0 collective-permute-start.5
  32.3 0.0 collective-permute-start.7
  32.3 1.3 %collective-permute-done.3.rest_8_ = f32[384,128]{1,0:T(8,128)S(1)} collective-permute-done((f32[384,128]{1,0:T(8,128)S(1)}, f32[384,128]{1,0:T(8,128)S(1)}, u32[]{:S(2)}, u32[]{:S(2)}) %collective-permute-start.3) | collective-permute-done | bytes 196640 | tf_op jit(solution)/shard_map/ppermute | solution.py:201
  33.6 1.9 %collective-permute-done.4.rest_1_ = f32[384,128]{1,0:T(8,128)S(1)} collective-permute-done((f32[384,128]{1,0:T(8,128)S(1)}, f32[384,128]{1,0:T(8,128)S(1)}, u32[]{:S(2)}, u32[]{:S(2)}) %collective-permute-start.4) | collective-permute-done | bytes 196640 | tf_op jit(solution)/shard_map/ppermute | solution.py:196
  35.5 3.7 %collective-permute-done.5.rest_3_ = f32[384,128]{1,0:T(8,128)S(1)} collective-permute-done((f32[384,128]{1,0:T(8,128)S(1)}, f32[384,128]{1,0:T(8,128)S(1)}, u32[]{:S(2)}, u32[]{:S(2)}) %collective-permute-start.5) | collective-permute-done | bytes 196640 | tf_op jit(solution)/shard_map/ppermute | solution.py:196
  39.2 0.6 collective-permute-start.11
  39.8 1.4 %collective-permute-start.13 = (f32[384,128]{1,0:T(8,128)S(1)}, f32[384,128]{1,0:T(8,128)S(1)}, u32[]{:S(2)}, u32[]{:S(2)}) collective-permute-start(f32[384,128]{1,0:T(8,128)S(1)} %collective-permute-done.5.rest_3_), channel_id=1, source_target_pairs={{0,2},{2,0},{1,3},{3,1},{4,6},{6,4},{5,7},{7,5},{8,10},{10,8},{9,1... | collective-permute-start | bytes 589832 | tf_op jit(solution)/shard_map/ppermute | solution.py:201
  41.2 0.0 collective-permute-start.10
  41.2 0.5 collective-permute-start.8
  41.7 3.6 %collective-permute-done.11.rest_9_ = f32[384,128]{1,0:T(8,128)S(1)} collective-permute-done((f32[384,128]{1,0:T(8,128)S(1)}, f32[384,128]{1,0:T(8,128)S(1)}, u32[]{:S(2)}, u32[]{:S(2)}) %collective-permute-start.11) | collective-permute-done | bytes 196640 | tf_op jit(solution)/shard_map/ppermute | solution.py:201
  45.3 0.0 collective-permute-start.6
  45.3 0.8 slice_bitcast_fusion.1
  46.1 4.9 %collective-permute-done.12.rest_10_ = f32[384,128]{1,0:T(8,128)S(1)} collective-permute-done((f32[384,128]{1,0:T(8,128)S(1)}, f32[384,128]{1,0:T(8,128)S(1)}, u32[]{:S(2)}, u32[]{:S(2)}) %collective-permute-start.12) | collective-permute-done | bytes 196640 | tf_op jit(solution)/shard_map/ppermute | solution.py:196
  51.0 0.5 collective-permute-start.15
  51.5 2.7 %collective-permute-done.6.rest_2_ = f32[384,128]{1,0:T(8,128)S(1)} collective-permute-done((f32[384,128]{1,0:T(8,128)S(1)}, f32[384,128]{1,0:T(8,128)S(1)}, u32[]{:S(2)}, u32[]{:S(2)}) %collective-permute-start.6) | collective-permute-done | bytes 196640 | tf_op jit(solution)/shard_map/ppermute | solution.py:196
  54.2 0.0 collective-permute-done.10.rest_7_
  54.3 0.5 collective-permute-start.17
  54.8 0.0 collective-permute-done.8.rest_5_
  54.8 0.3 collective-permute-start.9
  55.0 1.3 %fusion.6 = f32[96,8,128]{2,0,1:T(8,128)S(1)} fusion(f32[8,48,128]{2,0,1:T(8,128)} %bitcast.65, s32[96]{0:T(128)S(1)} %get-tuple-element.32), kind=kOutput, calls=%fused_computation.9 | convolution fusion | flops 56627712 | bytes 590208 | tf_op jit(solution)/shard_map/rnk,pn->rpk/dot_general | solution.py:270
  56.3 0.0 collective-permute-done.15.rest_13_
  56.3 0.0 collective-permute-done.16.rest_14_
  56.4 0.0 collective-permute-done.9.rest_6_
  56.4 0.0 copy-start.1
  56.4 0.8 copy-done.1
  57.2 0.8 copy-done.2
  58.0 15.1 %mixed.1 = f32[384,128]{1,0:T(8,128)} custom-call(s32[12288]{0:T(1024)S(1)} %bitcast.62, s32[12288]{0:T(1024)S(1)} %bitcast.63, f32[1944,128]{1,0:T(8,128)S(1)} %bitcast.55, f32[16,4,8,128]{3,2,1,0:T(8,128)S(1)} %all-to-all-done.mix_ref, f32[384,128]{1,0:T(8,128)S(1)} %bitcast.61, f32[384,128]{1,0:T(8,128)S(1)} %collective-permute-done.4.rest_1_, ...), custom_call_target="tpu_custom_call" | custom-call | flops 8847360 | bytes 8388608 | tf_op jit(solution)/shard_map/mixed/pallas_call | solution.py:155
  73.0 3.5 %all-to-all-start.1 = ((f32[16,3,8,128]{3,2,1,0:T(8,128)}), f32[16,3,8,128]{3,2,1,0:T(8,128)S(1)}, u32[]{:S(2)}, u32[]{:S(2)}) async-start(f32[16,3,8,128]{3,2,1,0:T(8,128)} %bitcast.17), calls=%async_computation.1 | async-start | bytes 393216 | tf_op jit(solution)/shard_map/all_to_all | solution.py:254
  76.6 7.5 %fusion.2 = f32[96,8,128]{2,1,0:T(8,128)S(1)} fusion(f32[96,128,128]{2,1,0:T(8,128)} %param.11, f32[96,8,128]{2,0,1:T(8,128)S(1)} %fusion.6), kind=kOutput, calls=%fused_computation.4 | convolution fusion | flops 150994944 | bytes 7077888 | tf_op jit(solution)/shard_map/rpk,pkl->rpl/dot_general | solution.py:271
  84.0 5.8 %all-to-all-done.1 = f32[16,3,8,128]{3,2,1,0:T(8,128)S(1)} async-done(((f32[16,3,8,128]{3,2,1,0:T(8,128)}), f32[16,3,8,128]{3,2,1,0:T(8,128)S(1)}, u32[]{:S(2)}, u32[]{:S(2)}) %all-to-all-start.1) | async-done | bytes 196640 | tf_op jit(solution)/shard_map/all_to_all | solution.py:254
  89.8 0.3 fusion.8
  90.2 0.7 copy.33
  (12 shorter events, 0.0 us)
Async XLA Ops:
  0.0 17.7 %copy-start = (f32[324,18]{0,1:T(8,128)S(1)}, f32[324,18]{0,1:T(8,128)}, u32[]{:S(2)}) copy-start(f32[324,18]{0,1:T(8,128)} %param.19) | copy-start | bytes 69988
  0.0 16.9 %collective-permute-start = (s32[18,96]{1,0:T(8,128)}, s32[18,96]{1,0:T(8,128)S(1)}, u32[]{:S(2)}, u32[]{:S(2)}) collective-permute-start(s32[18,96]{1,0:T(8,128)} %param.18), channel_id=1, source_target_pairs={{0,1},{1,0},{2,3},{3,2},{4,5},{5,4},{6,7},{7,6},{8,9},{9,8},{10,11... | collective-permute-start | bytes 20744 | tf_op jit(solution)/shard_map/ppermute | solution.py:210
  0.0 16.9 %collective-permute-start.1 = (s32[18,96]{1,0:T(8,128)}, s32[18,96]{1,0:T(8,128)S(1)}, u32[]{:S(2)}, u32[]{:S(2)}) collective-permute-start(s32[18,96]{1,0:T(8,128)} %param.18), channel_id=1, source_target_pairs={{0,2},{1,3},{2,0},{3,1},{4,6},{5,7},{6,4},{7,5},{8,10},{9,11},{10,... | collective-permute-start | bytes 20744 | tf_op jit(solution)/shard_map/ppermute | solution.py:210
  2.3 14.7 %collective-permute-start.2 = (s32[18,96]{1,0:T(8,128)}, s32[18,96]{1,0:T(8,128)S(1)}, u32[]{:S(2)}, u32[]{:S(2)}) collective-permute-start(s32[18,96]{1,0:T(8,128)} %param.18), channel_id=1, source_target_pairs={{0,3},{1,2},{2,1},{3,0},{4,7},{5,6},{6,5},{7,4},{8,11},{9,10},{10,... | collective-permute-start | bytes 20744 | tf_op jit(solution)/shard_map/ppermute | solution.py:210
  4.2 23.6 %all-to-all-start = ((f32[16,4,8,128]{3,2,1,0:T(8,128)}), f32[16,4,8,128]{3,2,1,0:T(8,128)S(1)}, u32[]{:S(2)}, u32[]{:S(2)}) async-start(f32[16,4,8,128]{3,2,1,0:T(8,128)} %pack.1), calls=%async_computation | async-start | bytes 524288 | tf_op jit(solution)/shard_map/all_to_all | solution.py:204
  27.8 5.8 %collective-permute-start.3 = (f32[384,128]{1,0:T(8,128)S(1)}, f32[384,128]{1,0:T(8,128)S(1)}, u32[]{:S(2)}, u32[]{:S(2)}) collective-permute-start(f32[384,128]{1,0:T(8,128)S(1)} %bitcast.56), channel_id=1, source_target_pairs={{0,2},{2,0},{1,3},{3,1},{4,6},{6,4},{5,7},{7,5},{8,10},{10,8},{9,1... | collective-permute-start | bytes 589832 | tf_op jit(solution)/shard_map/ppermute | solution.py:201
  29.3 6.2 %collective-permute-start.4 = (f32[384,128]{1,0:T(8,128)S(1)}, f32[384,128]{1,0:T(8,128)S(1)}, u32[]{:S(2)}, u32[]{:S(2)}) collective-permute-start(f32[384,128]{1,0:T(8,128)S(1)} %bitcast.57), channel_id=1, source_target_pairs={{0,192},{64,0},{128,64},{192,128},{1,193},{65,1},{129,65},{193,129... | collective-permute-start | bytes 589832 | tf_op jit(solution)/shard_map/ppermute | solution.py:196
  32.3 6.9 %collective-permute-start.5 = (f32[384,128]{1,0:T(8,128)S(1)}, f32[384,128]{1,0:T(8,128)S(1)}, u32[]{:S(2)}, u32[]{:S(2)}) collective-permute-start(f32[384,128]{1,0:T(8,128)S(1)} %bitcast.58), channel_id=1, source_target_pairs={{0,64},{64,128},{128,192},{192,0},{1,65},{65,129},{129,193},{193,1... | collective-permute-start | bytes 589832 | tf_op jit(solution)/shard_map/ppermute | solution.py:196
  32.3 9.4 %collective-permute-start.7 = (f32[384,128]{1,0:T(8,128)S(1)}, f32[384,128]{1,0:T(8,128)S(1)}, u32[]{:S(2)}, u32[]{:S(2)}) collective-permute-start(f32[384,128]{1,0:T(8,128)S(1)} %bitcast.59), channel_id=1, source_target_pairs={{0,1},{1,0},{2,3},{3,2},{4,5},{5,4},{6,7},{7,6},{8,9},{9,8},{10,11... | collective-permute-start | bytes 589832 | tf_op jit(solution)/shard_map/ppermute | solution.py:201
  39.2 6.1 %collective-permute-start.11 = (f32[384,128]{1,0:T(8,128)S(1)}, f32[384,128]{1,0:T(8,128)S(1)}, u32[]{:S(2)}, u32[]{:S(2)}) collective-permute-start(f32[384,128]{1,0:T(8,128)S(1)} %collective-permute-done.4.rest_1_), channel_id=1, source_target_pairs={{0,2},{2,0},{1,3},{3,1},{4,6},{6,4},{5,7},{7,5},{8,10},{10,8},{9,1... | collective-permute-start | bytes 589832 | tf_op jit(solution)/shard_map/ppermute | solution.py:201
  39.8 11.2 %collective-permute-start.13 = (f32[384,128]{1,0:T(8,128)S(1)}, f32[384,128]{1,0:T(8,128)S(1)}, u32[]{:S(2)}, u32[]{:S(2)}) collective-permute-start(f32[384,128]{1,0:T(8,128)S(1)} %collective-permute-done.5.rest_3_), channel_id=1, source_target_pairs={{0,2},{2,0},{1,3},{3,1},{4,6},{6,4},{5,7},{7,5},{8,10},{10,8},{9,1... | collective-permute-start | bytes 589832 | tf_op jit(solution)/shard_map/ppermute | solution.py:201
  41.2 13.0 %collective-permute-start.10 = (f32[384,128]{1,0:T(8,128)S(1)}, f32[384,128]{1,0:T(8,128)S(1)}, u32[]{:S(2)}, u32[]{:S(2)}) collective-permute-start(f32[384,128]{1,0:T(8,128)S(1)} %collective-permute-done.5.rest_3_), channel_id=1, source_target_pairs={{0,1},{1,0},{2,3},{3,2},{4,5},{5,4},{6,7},{7,6},{8,9},{9,8},{10,11... | collective-permute-start | bytes 589832 | tf_op jit(solution)/shard_map/ppermute | solution.py:201
  41.2 13.6 %collective-permute-start.8 = (f32[384,128]{1,0:T(8,128)S(1)}, f32[384,128]{1,0:T(8,128)S(1)}, u32[]{:S(2)}, u32[]{:S(2)}) collective-permute-start(f32[384,128]{1,0:T(8,128)S(1)} %collective-permute-done.4.rest_1_), channel_id=1, source_target_pairs={{0,1},{1,0},{2,3},{3,2},{4,5},{5,4},{6,7},{7,6},{8,9},{9,8},{10,11... | collective-permute-start | bytes 589832 | tf_op jit(solution)/shard_map/ppermute | solution.py:201
  41.7 9.3 %collective-permute-start.12 = (f32[384,128]{1,0:T(8,128)S(1)}, f32[384,128]{1,0:T(8,128)S(1)}, u32[]{:S(2)}, u32[]{:S(2)}) collective-permute-start(f32[384,128]{1,0:T(8,128)S(1)} %collective-permute-done.3.rest_8_), channel_id=1, source_target_pairs={{0,128},{64,192},{128,0},{192,64},{1,129},{65,193},{129,1},{193,65... | collective-permute-start | bytes 589832 | tf_op jit(solution)/shard_map/ppermute | solution.py:196
  45.3 8.9 %collective-permute-start.6 = (f32[384,128]{1,0:T(8,128)S(1)}, f32[384,128]{1,0:T(8,128)S(1)}, u32[]{:S(2)}, u32[]{:S(2)}) collective-permute-start(f32[384,128]{1,0:T(8,128)S(1)} %bitcast.60), channel_id=1, source_target_pairs={{0,128},{64,192},{128,0},{192,64},{1,129},{65,193},{129,1},{193,65... | collective-permute-start | bytes 589832 | tf_op jit(solution)/shard_map/ppermute | solution.py:196
  51.0 5.3 %collective-permute-start.14 = (f32[384,128]{1,0:T(8,128)S(1)}, f32[384,128]{1,0:T(8,128)S(1)}, u32[]{:S(2)}, u32[]{:S(2)}) collective-permute-start(f32[384,128]{1,0:T(8,128)S(1)} %collective-permute-done.3.rest_8_), channel_id=1, source_target_pairs={{0,1},{1,0},{2,3},{3,2},{4,5},{5,4},{6,7},{7,6},{8,9},{9,8},{10,11... | collective-permute-start | bytes 589832 | tf_op jit(solution)/shard_map/ppermute | solution.py:201
  51.0 5.3 %collective-permute-start.15 = (f32[384,128]{1,0:T(8,128)S(1)}, f32[384,128]{1,0:T(8,128)S(1)}, u32[]{:S(2)}, u32[]{:S(2)}) collective-permute-start(f32[384,128]{1,0:T(8,128)S(1)} %collective-permute-done.11.rest_9_), channel_id=1, source_target_pairs={{0,1},{1,0},{2,3},{3,2},{4,5},{5,4},{6,7},{7,6},{8,9},{9,8},{10,11... | collective-permute-start | bytes 589832 | tf_op jit(solution)/shard_map/ppermute | solution.py:201
  54.2 2.1 %collective-permute-start.16 = (f32[384,128]{1,0:T(8,128)S(1)}, f32[384,128]{1,0:T(8,128)S(1)}, u32[]{:S(2)}, u32[]{:S(2)}) collective-permute-start(f32[384,128]{1,0:T(8,128)S(1)} %collective-permute-done.12.rest_10_), channel_id=1, source_target_pairs={{0,1},{1,0},{2,3},{3,2},{4,5},{5,4},{6,7},{7,6},{8,9},{9,8},{10,11... | collective-permute-start | bytes 589832 | tf_op jit(solution)/shard_map/ppermute | solution.py:201
  54.3 2.1 %collective-permute-start.17 = (f32[384,128]{1,0:T(8,128)S(1)}, f32[384,128]{1,0:T(8,128)S(1)}, u32[]{:S(2)}, u32[]{:S(2)}) collective-permute-start(f32[384,128]{1,0:T(8,128)S(1)} %collective-permute-done.13.rest_11_), channel_id=1, source_target_pairs={{0,1},{1,0},{2,3},{3,2},{4,5},{5,4},{6,7},{7,6},{8,9},{9,8},{10,11... | collective-permute-start | bytes 589832 | tf_op jit(solution)/shard_map/ppermute | solution.py:201
  54.8 1.6 %collective-permute-start.9 = (f32[384,128]{1,0:T(8,128)S(1)}, f32[384,128]{1,0:T(8,128)S(1)}, u32[]{:S(2)}, u32[]{:S(2)}) collective-permute-start(f32[384,128]{1,0:T(8,128)S(1)} %collective-permute-done.6.rest_2_), channel_id=1, source_target_pairs={{0,1},{1,0},{2,3},{3,2},{4,5},{5,4},{6,7},{7,6},{8,9},{9,8},{10,11... | collective-permute-start | bytes 589832 | tf_op jit(solution)/shard_map/ppermute | solution.py:201
  56.4 0.8 copy-start.1
  57.2 0.8 copy-start.2
  73.0 16.8 %all-to-all-start.1 = ((f32[16,3,8,128]{3,2,1,0:T(8,128)}), f32[16,3,8,128]{3,2,1,0:T(8,128)S(1)}, u32[]{:S(2)}, u32[]{:S(2)}) async-start(f32[16,3,8,128]{3,2,1,0:T(8,128)} %bitcast.17), calls=%async_computation.1 | async-start | bytes 393216 | tf_op jit(solution)/shard_map/all_to_all | solution.py:254

commit v5 on v4

--- a/solution.py
+++ b/solution.py
@@ -22,7 +22,7 @@
 
 SMEM = pl.BlockSpec(memory_space=pltpu.SMEM)
 VMEM = pl.BlockSpec(memory_space=pltpu.VMEM)
-ANY = pl.BlockSpec(memory_space=pl.ANY)
+HBM = pl.BlockSpec(memory_space=pltpu.HBM)
 
 
 def pack_kernel(g_ref, mask_ref, x_ref, alpha_ref, o_ref):
@@ -85,7 +85,9 @@
         out_specs=(VMEM, VMEM),
         name="prep",
     )(place, src, pair, par)
-    return ci.reshape(-1), wi.reshape(-1)
+    return tuple(
+        pltpu.with_memory_space_constraint(v.reshape(-1), pltpu.HBM) for v in (ci, wi)
+    )
 
 
 def mixed_kernel(n_exc, cidx_hbm, widx_hbm, w_ref, mix_ref, *rest):
@@ -155,7 +157,7 @@
     return pl.pallas_call(
         functools.partial(mixed_kernel, n_exc),
         out_shape=jax.ShapeDtypeStruct((PART, LANES), jnp.float32),
-        in_specs=[ANY, ANY, VMEM, VMEM] + [VMEM] * count,
+        in_specs=[HBM, HBM, VMEM, VMEM] + [VMEM] * count,
         out_specs=VMEM,
         scratch_shapes=[
             pltpu.VMEM((count * PART, LANES), jnp.float32),
@@ -206,6 +208,8 @@
     )
 
     sel = xl * NC + c
+    place = jnp.stack([g, sel]).astype(jnp.int32)
+    cidx, widx = prep_call(place, exc_source, exc_pair, exc_parity, n_pair)
     pieces = [
         lax.ppermute(occupation, ("xl", "c"), [(i, i ^ k) for i in range(NS)])
         for k in range(1, NS)
@@ -223,11 +227,14 @@
         .reshape(2 * n_pair * NT, LANES)
     )
 
-    place = jnp.stack([g, sel]).astype(jnp.int32)
-    cidx, widx = prep_call(place, exc_source, exc_pair, exc_parity, n_pair)
-
-    arrived, wtab, cidx, widx, late = lax.optimization_barrier(
-        (arrived, wtab, cidx, widx, coeff)
+    block_size = beta_blocks.shape[1]
+    block_count = beta_width // block_size
+    blocked = coeff.reshape(alpha_rows, block_count, block_size)
+    block_ids = jnp.arange(block_count, dtype=jnp.int32)
+    choosing = (block_list[0][:, None] == block_ids[None, :]).astype(jnp.float32)
+    picked = jnp.einsum("rnk,pn->rpk", blocked, choosing, precision=HIGH)
+    arrived, wtab, cidx, widx, picked = lax.optimization_barrier(
+        (arrived, wtab, cidx, widx, picked)
     )
     own = arrived[:, :NT].reshape(PART, LANES)
     after, before = shift(own, 1), shift(own, N_GRP - 1)
@@ -262,12 +269,6 @@
         mixed.reshape(NQ * NT, RA, LANES).transpose(1, 0, 2).reshape(alpha_rows, -1)
     )
 
-    block_size = beta_blocks.shape[1]
-    block_count = beta_width // block_size
-    blocked = late.reshape(alpha_rows, block_count, block_size)
-    block_ids = jnp.arange(block_count, dtype=jnp.int32)
-    choosing = (block_list[0][:, None] == block_ids[None, :]).astype(jnp.float32)
-    picked = jnp.einsum("rnk,pn->rpk", blocked, choosing, precision=HIGH)
     applied = jnp.einsum("rpk,pkl->rpl", picked, beta_blocks, precision=HIGH)
     placing = (block_list[1][:, None] == block_ids[None, :]).astype(jnp.float32)
     same_beta = jnp.einsum("rpl,pn->rnl", applied, placing, precision=HIGH).reshape(

time: 91.4 us -> 85.8 us (0.939)
  waiting for transfers between devices: 33.2 us -> 25.4 us
  starting transfers between devices: 23.9 us -> 27.2 us
  local copies, waits for them, and re-layouts: 3.12 us -> 1.53 us
    ppermute x4, waiting for transfers between devices: 13.3 us -> 6.28 us  [shift(): lax.ppermute(value, 'grp', [(i, (i - k) % N_GRP) for i in range(N_GRP)])]
    ppermute x4, starting transfers between devices: 3.02 us -> 6.84 us  [shift(): lax.ppermute(value, 'grp', [(i, (i - k) % N_GRP) for i in range(N_GRP)])]
    all_to_all x1, waiting for transfers between devices: 9.2 us -> 6.8 us  [per_device(): lax.all_to_all(packed, ('z', 'xh'), split_axis=0, concat_axis=0, tiled=True)]
    ppermute x11, waiting for transfers between devices: 4.89 us -> 6.49 us  [swap(): return lax.ppermute(value, axis, [(0, 1), (1, 0)])]
    unnamed x7 -> x3, local copies, waits for them, and re-layouts: 2.33 us -> 0.74 us
  transfers between devices with their start and end apart: 20 -> 20, of which waited for: 8 -> 11; matrix products, arithmetic and copies ran while one was open for 13% -> 14% of each run, Pallas kernels for 5% -> 5%
where the time goes in v5:
time: 85.8 us; the launch traced here: 84.8 us
  starting transfers between devices  27.2 us (32%)
  waiting for transfers between devices  25.4 us (30%)
  Pallas kernels  19.4 us (23%)
  matrix products  9.82 us (11%)
  local copies, waits for them, and re-layouts  1.53 us (2%)
  other arithmetic  1.35 us (2%)
    pallas_call x1, Pallas kernels, mixed_call(): pl.pallas_call(functools.partial(mixed_kernel, n_exc), out_shape=jax.Shap...  15.2 us
    all_to_all x1, starting transfers between devices, per_device(): lax.all_to_all(packed, ('z', 'xh'), split_axis=0, concat_axis=0, tiled=True)  9.88 us
    dot_general x1, matrix products, per_device(): applied = jnp.einsum('rpk,pkl->rpl', picked, beta_blocks, precision=HIGH)  7.45 us
    ppermute x4, starting transfers between devices, shift(): lax.ppermute(value, 'grp', [(i, (i - k) % N_GRP) for i in range(N_GRP)])  6.84 us
    all_to_all x1, waiting for transfers between devices, per_device(): lax.all_to_all(packed, ('z', 'xh'), split_axis=0, concat_axis=0, tiled=True)  6.8 us
    ppermute x11, waiting for transfers between devices, swap(): return lax.ppermute(value, axis, [(0, 1), (1, 0)])  6.49 us
    ppermute x4, waiting for transfers between devices, shift(): lax.ppermute(value, 'grp', [(i, (i - k) % N_GRP) for i in range(N_GRP)])  6.28 us
    all_to_all x1, waiting for transfers between devices, per_device(): lax.all_to_all(mixed_local.reshape(NQ, NT, RA, LANES), ('z', 'xh'), split...  5.8 us
  transfers between devices with their start and end apart: 20, of which 11 were waited for; matrix products, arithmetic and copies ran while one was open for 14% of the time, Pallas kernels for 5%

profile of v5, /device:TPU:2, one launch (start us, length us, event | category | flops | bytes accessed | tf_op | source)
XLA Modules:
  0.0 84.8 jit_solution(15821525964389529045)
XLA Ops:
  0.0 0.0 collective-permute-start
  0.0 2.4 %collective-permute-start.2 = (s32[18,96]{1,0:T(8,128)}, s32[18,96]{1,0:T(8,128)S(1)}, u32[]{:S(2)}, u32[]{:S(2)}) collective-permute-start(s32[18,96]{1,0:T(8,128)} %param.18), channel_id=1, source_target_pairs={{0,3},{1,2},{2,1},{3,0},{4,7},{5,6},{6,5},{7,4},{8,11},{9,10},{10,... | collective-permute-start | bytes 20744 | tf_op jit(solution)/shard_map/ppermute | solution.py:214
  2.4 1.7 %pack.1 = f32[16,4,8,128]{3,2,1,0:T(8,128)} custom-call(s32[1]{0:T(128)} %bitcast.g_ref, s32[1,4]{1,0:T(1,128)} %mask_ref.1, f32[8,6144]{1,0:T(8,128)} %x_ref.1, f32[1,4,8,8]{3,2,1,0:T(8,128)} %alpha_ref.1), custom_call_target="tpu_custom_call" | custom-call | tf_op jit(solution)/shard_map/pack/pallas_call | solution.py:43
  4.1 9.9 %all-to-all-start = ((f32[16,4,8,128]{3,2,1,0:T(8,128)}), f32[16,4,8,128]{3,2,1,0:T(8,128)S(1)}, u32[]{:S(2)}, u32[]{:S(2)}) async-start(f32[16,4,8,128]{3,2,1,0:T(8,128)} %pack.1), calls=%async_computation | async-start | bytes 524288 | tf_op jit(solution)/shard_map/all_to_all | solution.py:206
  14.0 0.8 slice_bitcast_fusion
  14.8 1.3 %convolution_bitcast_fusion.1 = f32[8,96,128]{2,1,0:T(8,128)S(1)} fusion(f32[8,48,128]{2,0,1:T(8,128)} %bitcast.62, s32[96]{0:T(128)S(1)} %get-tuple-element.32), kind=kOutput, calls=%fused_computation.1 | convolution fusion | flops 56627712 | bytes 590208 | tf_op jit(solution)/shard_map/rnk,pn->rpk/dot_general | solution.py:235
  16.1 0.6 pad_add_fusion.1.place_ref
  16.6 2.5 %prep.1 = (s32[96,128]{1,0:T(8,128)}, s32[96,128]{1,0:T(8,128)}) custom-call(s32[2]{0:T(128)} %pad_add_fusion.1.place_ref, s32[90,512]{1,0:T(8,128)} %src_ref.1, s32[90,512]{1,0:T(8,128)} %pair_ref.1, s32[90,512]{1,0:T(8,128)} %par_ref.1), custom_call_target="tpu_custom_call" | custom-call | tf_op jit(solution)/shard_map/prep/pallas_call | solution.py:81
  19.2 0.0 collective-permute-done
  19.2 0.0 collective-permute-done.2
  19.2 0.7 pad_add_fusion
  19.9 0.8 fusion.24
  20.7 0.1 pad_maximum_fusion
  20.8 6.8 %all-to-all-done.mix_ref = f32[16,4,8,128]{3,2,1,0:T(8,128)S(1)} async-done(((f32[16,4,8,128]{3,2,1,0:T(8,128)}), f32[16,4,8,128]{3,2,1,0:T(8,128)S(1)}, u32[]{:S(2)}, u32[]{:S(2)}) %all-to-all-start) | async-done | bytes 262176 | tf_op jit(solution)/shard_map/all_to_all | solution.py:206
  27.6 1.7 %collective-permute-start.5 = (f32[384,128]{1,0:T(8,128)S(1)}, f32[384,128]{1,0:T(8,128)S(1)}, u32[]{:S(2)}, u32[]{:S(2)}) collective-permute-start(f32[384,128]{1,0:T(8,128)S(1)} %bitcast.55), channel_id=1, source_target_pairs={{0,64},{64,128},{128,192},{192,0},{1,65},{65,129},{129,193},{193,1... | collective-permute-start | bytes 589832 | tf_op jit(solution)/shard_map/ppermute | solution.py:198
  29.2 1.7 %collective-permute-start.4 = (f32[384,128]{1,0:T(8,128)S(1)}, f32[384,128]{1,0:T(8,128)S(1)}, u32[]{:S(2)}, u32[]{:S(2)}) collective-permute-start(f32[384,128]{1,0:T(8,128)S(1)} %bitcast.56), channel_id=1, source_target_pairs={{0,192},{64,0},{128,64},{192,128},{1,193},{65,1},{129,65},{193,129... | collective-permute-start | bytes 589832 | tf_op jit(solution)/shard_map/ppermute | solution.py:198
  30.9 1.4 %collective-permute-start.3 = (f32[384,128]{1,0:T(8,128)S(1)}, f32[384,128]{1,0:T(8,128)S(1)}, u32[]{:S(2)}, u32[]{:S(2)}) collective-permute-start(f32[384,128]{1,0:T(8,128)S(1)} %bitcast.57), channel_id=1, source_target_pairs={{0,2},{2,0},{1,3},{3,1},{4,6},{6,4},{5,7},{7,5},{8,10},{10,8},{9,1... | collective-permute-start | bytes 589832 | tf_op jit(solution)/shard_map/ppermute | solution.py:203
  32.3 0.0 collective-permute-start.7
  32.3 2.2 %collective-permute-done.5.rest_3_ = f32[384,128]{1,0:T(8,128)S(1)} collective-permute-done((f32[384,128]{1,0:T(8,128)S(1)}, f32[384,128]{1,0:T(8,128)S(1)}, u32[]{:S(2)}, u32[]{:S(2)}) %collective-permute-start.5) | collective-permute-done | bytes 196640 | tf_op jit(solution)/shard_map/ppermute | solution.py:198
  34.6 0.4 collective-permute-done.4.rest_1_
  34.9 1.7 %collective-permute-done.3.rest_8_ = f32[384,128]{1,0:T(8,128)S(1)} collective-permute-done((f32[384,128]{1,0:T(8,128)S(1)}, f32[384,128]{1,0:T(8,128)S(1)}, u32[]{:S(2)}, u32[]{:S(2)}) %collective-permute-start.3) | collective-permute-done | bytes 196640 | tf_op jit(solution)/shard_map/ppermute | solution.py:203
  36.6 2.0 %collective-permute-start.6 = (f32[384,128]{1,0:T(8,128)S(1)}, f32[384,128]{1,0:T(8,128)S(1)}, u32[]{:S(2)}, u32[]{:S(2)}) collective-permute-start(f32[384,128]{1,0:T(8,128)S(1)} %bitcast.59), channel_id=1, source_target_pairs={{0,128},{64,192},{128,0},{192,64},{1,129},{65,193},{129,1},{193,65... | collective-permute-start | bytes 589832 | tf_op jit(solution)/shard_map/ppermute | solution.py:198
  38.6 1.5 %collective-permute-start.12 = (f32[384,128]{1,0:T(8,128)S(1)}, f32[384,128]{1,0:T(8,128)S(1)}, u32[]{:S(2)}, u32[]{:S(2)}) collective-permute-start(f32[384,128]{1,0:T(8,128)S(1)} %collective-permute-done.3.rest_8_), channel_id=1, source_target_pairs={{0,128},{64,192},{128,0},{192,64},{1,129},{65,193},{129,1},{193,65... | collective-permute-start | bytes 589832 | tf_op jit(solution)/shard_map/ppermute | solution.py:198
  40.1 1.4 %collective-permute-start.11 = (f32[384,128]{1,0:T(8,128)S(1)}, f32[384,128]{1,0:T(8,128)S(1)}, u32[]{:S(2)}, u32[]{:S(2)}) collective-permute-start(f32[384,128]{1,0:T(8,128)S(1)} %collective-permute-done.4.rest_1_), channel_id=1, source_target_pairs={{0,2},{2,0},{1,3},{3,1},{4,6},{6,4},{5,7},{7,5},{8,10},{10,8},{9,1... | collective-permute-start | bytes 589832 | tf_op jit(solution)/shard_map/ppermute | solution.py:203
  41.5 0.0 collective-permute-start.8
  41.5 0.0 collective-permute-done.7.rest_4_
  41.6 0.6 collective-permute-start.13
  42.1 1.6 %collective-permute-done.6.rest_2_ = f32[384,128]{1,0:T(8,128)S(1)} collective-permute-done((f32[384,128]{1,0:T(8,128)S(1)}, f32[384,128]{1,0:T(8,128)S(1)}, u32[]{:S(2)}, u32[]{:S(2)}) %collective-permute-start.6) | collective-permute-done | bytes 196640 | tf_op jit(solution)/shard_map/ppermute | solution.py:198
  43.8 0.0 collective-permute-start.10
  43.8 2.1 %collective-permute-done.12.rest_10_ = f32[384,128]{1,0:T(8,128)S(1)} collective-permute-done((f32[384,128]{1,0:T(8,128)S(1)}, f32[384,128]{1,0:T(8,128)S(1)}, u32[]{:S(2)}, u32[]{:S(2)}) %collective-permute-start.12) | collective-permute-done | bytes 196640 | tf_op jit(solution)/shard_map/ppermute | solution.py:198
  45.9 0.0 collective-permute-start.14
  45.9 1.0 %collective-permute-done.11.rest_9_ = f32[384,128]{1,0:T(8,128)S(1)} collective-permute-done((f32[384,128]{1,0:T(8,128)S(1)}, f32[384,128]{1,0:T(8,128)S(1)}, u32[]{:S(2)}, u32[]{:S(2)}) %collective-permute-start.11) | collective-permute-done | bytes 196640 | tf_op jit(solution)/shard_map/ppermute | solution.py:203
  46.9 0.0 collective-permute-start.9
  46.9 0.0 collective-permute-done.8.rest_5_
  46.9 0.5 collective-permute-start.16
  47.4 2.6 %collective-permute-done.13.rest_11_ = f32[384,128]{1,0:T(8,128)S(1)} collective-permute-done((f32[384,128]{1,0:T(8,128)S(1)}, f32[384,128]{1,0:T(8,128)S(1)}, u32[]{:S(2)}, u32[]{:S(2)}) %collective-permute-start.13) | collective-permute-done | bytes 196640 | tf_op jit(solution)/shard_map/ppermute | solution.py:203
  50.0 0.0 collective-permute-start.15
  50.0 0.0 collective-permute-done.10.rest_7_
  50.0 0.5 collective-permute-start.17
  50.5 0.0 collective-permute-done.14.rest_12_
  50.5 0.9 %collective-permute-done.15.rest_13_ = f32[384,128]{1,0:T(8,128)S(1)} collective-permute-done((f32[384,128]{1,0:T(8,128)S(1)}, f32[384,128]{1,0:T(8,128)S(1)}, u32[]{:S(2)}, u32[]{:S(2)}) %collective-permute-start.15) | collective-permute-done | bytes 196640 | tf_op jit(solution)/shard_map/ppermute | solution.py:203
  51.4 0.3 collective-permute-done.17.rest_15_
  51.7 15.2 %mixed.1 = f32[384,128]{1,0:T(8,128)} custom-call(s32[12288]{0:T(1024)} %bitcast.63, s32[12288]{0:T(1024)} %bitcast.64, f32[1944,128]{1,0:T(8,128)S(1)} %bitcast.54, f32[16,4,8,128]{3,2,1,0:T(8,128)S(1)} %all-to-all-done.mix_ref, f32[384,128]{1,0:T(8,128)S(1)} %bitcast.60, f32[384,128]{1,0:T(8,128)S(1)} %collective-permute-done.4.rest_1_, ...), custom_call_target="tpu_custom_call" | custom-call | flops 8847360 | bytes 8388608 | tf_op jit(solution)/shard_map/mixed/pallas_call | solution.py:157
  66.9 3.5 %all-to-all-start.1 = ((f32[16,3,8,128]{3,2,1,0:T(8,128)}), f32[16,3,8,128]{3,2,1,0:T(8,128)S(1)}, u32[]{:S(2)}, u32[]{:S(2)}) async-start(f32[16,3,8,128]{3,2,1,0:T(8,128)} %bitcast.21), calls=%async_computation.1 | async-start | bytes 393216 | tf_op jit(solution)/shard_map/all_to_all | solution.py:261
  70.5 7.5 %fusion.3 = f32[96,8,128]{2,1,0:T(8,128)S(1)} fusion(f32[96,128,128]{2,1,0:T(8,128)} %param.11, f32[8,96,128]{2,1,0:T(8,128)S(1)} %convolution_bitcast_fusion.1), kind=kOutput, calls=%fused_computation.6 | convolution fusion | flops 150994944 | bytes 7077888 | tf_op jit(solution)/shard_map/rpk,pkl->rpl/dot_general | solution.py:272
  77.9 5.8 %all-to-all-done.1 = f32[16,3,8,128]{3,2,1,0:T(8,128)S(1)} async-done(((f32[16,3,8,128]{3,2,1,0:T(8,128)}), f32[16,3,8,128]{3,2,1,0:T(8,128)S(1)}, u32[]{:S(2)}, u32[]{:S(2)}) %all-to-all-start.1) | async-done | bytes 196640 | tf_op jit(solution)/shard_map/all_to_all | solution.py:261
  83.7 0.3 fusion.5
  84.0 0.7 copy.32
  (8 shorter events, 0.0 us)
Async XLA Ops:
  0.0 19.9 %copy-start = (f32[324,18]{0,1:T(8,128)S(1)}, f32[324,18]{0,1:T(8,128)}, u32[]{:S(2)}) copy-start(f32[324,18]{0,1:T(8,128)} %param.19) | copy-start | bytes 69988
  0.0 19.2 %collective-permute-start = (s32[18,96]{1,0:T(8,128)}, s32[18,96]{1,0:T(8,128)S(1)}, u32[]{:S(2)}, u32[]{:S(2)}) collective-permute-start(s32[18,96]{1,0:T(8,128)} %param.18), channel_id=1, source_target_pairs={{0,1},{1,0},{2,3},{3,2},{4,5},{5,4},{6,7},{7,6},{8,9},{9,8},{10,11... | collective-permute-start | bytes 20744 | tf_op jit(solution)/shard_map/ppermute | solution.py:214
  0.0 19.2 %collective-permute-start.2 = (s32[18,96]{1,0:T(8,128)}, s32[18,96]{1,0:T(8,128)S(1)}, u32[]{:S(2)}, u32[]{:S(2)}) collective-permute-start(s32[18,96]{1,0:T(8,128)} %param.18), channel_id=1, source_target_pairs={{0,3},{1,2},{2,1},{3,0},{4,7},{5,6},{6,5},{7,4},{8,11},{9,10},{10,... | collective-permute-start | bytes 20744 | tf_op jit(solution)/shard_map/ppermute | solution.py:214
  2.4 16.8 %collective-permute-start.1 = (s32[18,96]{1,0:T(8,128)}, s32[18,96]{1,0:T(8,128)S(1)}, u32[]{:S(2)}, u32[]{:S(2)}) collective-permute-start(s32[18,96]{1,0:T(8,128)} %param.18), channel_id=1, source_target_pairs={{0,2},{1,3},{2,0},{3,1},{4,6},{5,7},{6,4},{7,5},{8,10},{9,11},{10,... | collective-permute-start | bytes 20744 | tf_op jit(solution)/shard_map/ppermute | solution.py:214
  4.1 23.4 %all-to-all-start = ((f32[16,4,8,128]{3,2,1,0:T(8,128)}), f32[16,4,8,128]{3,2,1,0:T(8,128)S(1)}, u32[]{:S(2)}, u32[]{:S(2)}) async-start(f32[16,4,8,128]{3,2,1,0:T(8,128)} %pack.1), calls=%async_computation | async-start | bytes 524288 | tf_op jit(solution)/shard_map/all_to_all | solution.py:206
  27.6 7.0 %collective-permute-start.5 = (f32[384,128]{1,0:T(8,128)S(1)}, f32[384,128]{1,0:T(8,128)S(1)}, u32[]{:S(2)}, u32[]{:S(2)}) collective-permute-start(f32[384,128]{1,0:T(8,128)S(1)} %bitcast.55), channel_id=1, source_target_pairs={{0,64},{64,128},{128,192},{192,0},{1,65},{65,129},{129,193},{193,1... | collective-permute-start | bytes 589832 | tf_op jit(solution)/shard_map/ppermute | solution.py:198
  29.2 5.7 %collective-permute-start.4 = (f32[384,128]{1,0:T(8,128)S(1)}, f32[384,128]{1,0:T(8,128)S(1)}, u32[]{:S(2)}, u32[]{:S(2)}) collective-permute-start(f32[384,128]{1,0:T(8,128)S(1)} %bitcast.56), channel_id=1, source_target_pairs={{0,192},{64,0},{128,64},{192,128},{1,193},{65,1},{129,65},{193,129... | collective-permute-start | bytes 589832 | tf_op jit(solution)/shard_map/ppermute | solution.py:198
  30.9 5.7 %collective-permute-start.3 = (f32[384,128]{1,0:T(8,128)S(1)}, f32[384,128]{1,0:T(8,128)S(1)}, u32[]{:S(2)}, u32[]{:S(2)}) collective-permute-start(f32[384,128]{1,0:T(8,128)S(1)} %bitcast.57), channel_id=1, source_target_pairs={{0,2},{2,0},{1,3},{3,1},{4,6},{6,4},{5,7},{7,5},{8,10},{10,8},{9,1... | collective-permute-start | bytes 589832 | tf_op jit(solution)/shard_map/ppermute | solution.py:203
  32.3 9.2 %collective-permute-start.7 = (f32[384,128]{1,0:T(8,128)S(1)}, f32[384,128]{1,0:T(8,128)S(1)}, u32[]{:S(2)}, u32[]{:S(2)}) collective-permute-start(f32[384,128]{1,0:T(8,128)S(1)} %bitcast.58), channel_id=1, source_target_pairs={{0,1},{1,0},{2,3},{3,2},{4,5},{5,4},{6,7},{7,6},{8,9},{9,8},{10,11... | collective-permute-start | bytes 589832 | tf_op jit(solution)/shard_map/ppermute | solution.py:203
  36.6 7.2 %collective-permute-start.6 = (f32[384,128]{1,0:T(8,128)S(1)}, f32[384,128]{1,0:T(8,128)S(1)}, u32[]{:S(2)}, u32[]{:S(2)}) collective-permute-start(f32[384,128]{1,0:T(8,128)S(1)} %bitcast.59), channel_id=1, source_target_pairs={{0,128},{64,192},{128,0},{192,64},{1,129},{65,193},{129,1},{193,65... | collective-permute-start | bytes 589832 | tf_op jit(solution)/shard_map/ppermute | solution.py:198
  38.6 7.3 %collective-permute-start.12 = (f32[384,128]{1,0:T(8,128)S(1)}, f32[384,128]{1,0:T(8,128)S(1)}, u32[]{:S(2)}, u32[]{:S(2)}) collective-permute-start(f32[384,128]{1,0:T(8,128)S(1)} %collective-permute-done.3.rest_8_), channel_id=1, source_target_pairs={{0,128},{64,192},{128,0},{192,64},{1,129},{65,193},{129,1},{193,65... | collective-permute-start | bytes 589832 | tf_op jit(solution)/shard_map/ppermute | solution.py:198
  40.1 6.8 %collective-permute-start.11 = (f32[384,128]{1,0:T(8,128)S(1)}, f32[384,128]{1,0:T(8,128)S(1)}, u32[]{:S(2)}, u32[]{:S(2)}) collective-permute-start(f32[384,128]{1,0:T(8,128)S(1)} %collective-permute-done.4.rest_1_), channel_id=1, source_target_pairs={{0,2},{2,0},{1,3},{3,1},{4,6},{6,4},{5,7},{7,5},{8,10},{10,8},{9,1... | collective-permute-start | bytes 589832 | tf_op jit(solution)/shard_map/ppermute | solution.py:203
  41.5 5.4 %collective-permute-start.8 = (f32[384,128]{1,0:T(8,128)S(1)}, f32[384,128]{1,0:T(8,128)S(1)}, u32[]{:S(2)}, u32[]{:S(2)}) collective-permute-start(f32[384,128]{1,0:T(8,128)S(1)} %collective-permute-done.4.rest_1_), channel_id=1, source_target_pairs={{0,1},{1,0},{2,3},{3,2},{4,5},{5,4},{6,7},{7,6},{8,9},{9,8},{10,11... | collective-permute-start | bytes 589832 | tf_op jit(solution)/shard_map/ppermute | solution.py:203
  41.6 8.4 %collective-permute-start.13 = (f32[384,128]{1,0:T(8,128)S(1)}, f32[384,128]{1,0:T(8,128)S(1)}, u32[]{:S(2)}, u32[]{:S(2)}) collective-permute-start(f32[384,128]{1,0:T(8,128)S(1)} %collective-permute-done.5.rest_3_), channel_id=1, source_target_pairs={{0,2},{2,0},{1,3},{3,1},{4,6},{6,4},{5,7},{7,5},{8,10},{10,8},{9,1... | collective-permute-start | bytes 589832 | tf_op jit(solution)/shard_map/ppermute | solution.py:203
  43.8 6.2 %collective-permute-start.10 = (f32[384,128]{1,0:T(8,128)S(1)}, f32[384,128]{1,0:T(8,128)S(1)}, u32[]{:S(2)}, u32[]{:S(2)}) collective-permute-start(f32[384,128]{1,0:T(8,128)S(1)} %collective-permute-done.5.rest_3_), channel_id=1, source_target_pairs={{0,1},{1,0},{2,3},{3,2},{4,5},{5,4},{6,7},{7,6},{8,9},{9,8},{10,11... | collective-permute-start | bytes 589832 | tf_op jit(solution)/shard_map/ppermute | solution.py:203
  45.9 4.7 %collective-permute-start.14 = (f32[384,128]{1,0:T(8,128)S(1)}, f32[384,128]{1,0:T(8,128)S(1)}, u32[]{:S(2)}, u32[]{:S(2)}) collective-permute-start(f32[384,128]{1,0:T(8,128)S(1)} %collective-permute-done.3.rest_8_), channel_id=1, source_target_pairs={{0,1},{1,0},{2,3},{3,2},{4,5},{5,4},{6,7},{7,6},{8,9},{9,8},{10,11... | collective-permute-start | bytes 589832 | tf_op jit(solution)/shard_map/ppermute | solution.py:203
  46.9 3.6 %collective-permute-start.9 = (f32[384,128]{1,0:T(8,128)S(1)}, f32[384,128]{1,0:T(8,128)S(1)}, u32[]{:S(2)}, u32[]{:S(2)}) collective-permute-start(f32[384,128]{1,0:T(8,128)S(1)} %collective-permute-done.6.rest_2_), channel_id=1, source_target_pairs={{0,1},{1,0},{2,3},{3,2},{4,5},{5,4},{6,7},{7,6},{8,9},{9,8},{10,11... | collective-permute-start | bytes 589832 | tf_op jit(solution)/shard_map/ppermute | solution.py:203
  46.9 3.6 %collective-permute-start.16 = (f32[384,128]{1,0:T(8,128)S(1)}, f32[384,128]{1,0:T(8,128)S(1)}, u32[]{:S(2)}, u32[]{:S(2)}) collective-permute-start(f32[384,128]{1,0:T(8,128)S(1)} %collective-permute-done.12.rest_10_), channel_id=1, source_target_pairs={{0,1},{1,0},{2,3},{3,2},{4,5},{5,4},{6,7},{7,6},{8,9},{9,8},{10,11... | collective-permute-start | bytes 589832 | tf_op jit(solution)/shard_map/ppermute | solution.py:203
  50.0 1.4 %collective-permute-start.15 = (f32[384,128]{1,0:T(8,128)S(1)}, f32[384,128]{1,0:T(8,128)S(1)}, u32[]{:S(2)}, u32[]{:S(2)}) collective-permute-start(f32[384,128]{1,0:T(8,128)S(1)} %collective-permute-done.11.rest_9_), channel_id=1, source_target_pairs={{0,1},{1,0},{2,3},{3,2},{4,5},{5,4},{6,7},{7,6},{8,9},{9,8},{10,11... | collective-permute-start | bytes 589832 | tf_op jit(solution)/shard_map/ppermute | solution.py:203
  50.0 1.7 %collective-permute-start.17 = (f32[384,128]{1,0:T(8,128)S(1)}, f32[384,128]{1,0:T(8,128)S(1)}, u32[]{:S(2)}, u32[]{:S(2)}) collective-permute-start(f32[384,128]{1,0:T(8,128)S(1)} %collective-permute-done.13.rest_11_), channel_id=1, source_target_pairs={{0,1},{1,0},{2,3},{3,2},{4,5},{5,4},{6,7},{7,6},{8,9},{9,8},{10,11... | collective-permute-start | bytes 589832 | tf_op jit(solution)/shard_map/ppermute | solution.py:203
  66.9 16.8 %all-to-all-start.1 = ((f32[16,3,8,128]{3,2,1,0:T(8,128)}), f32[16,3,8,128]{3,2,1,0:T(8,128)S(1)}, u32[]{:S(2)}, u32[]{:S(2)}) async-start(f32[16,3,8,128]{3,2,1,0:T(8,128)} %bitcast.21), calls=%async_computation.1 | async-start | bytes 393216 | tf_op jit(solution)/shard_map/all_to_all | solution.py:261

commit v6 on v5

--- a/solution.py
+++ b/solution.py
@@ -239,11 +239,14 @@
     own = arrived[:, :NT].reshape(PART, LANES)
     after, before = shift(own, 1), shift(own, N_GRP - 1)
     over = swap(own, "xl")
-    again, over_again, after, before = lax.optimization_barrier(
-        (own, over, after, before)
-    )
-    near = [own, after, shift(again, 2), before]
-    across = [over, swap(after, "xl"), shift(over_again, 2), swap(before, "xl")]
+    again, over, after, before = lax.optimization_barrier((own, over, after, before))
+    over_after, over_before = swap(after, "xl"), swap(before, "xl")
+    two, over_two = shift(again, 2), shift(over, 2)
+    (start, after, before, over), over_after = lax.optimization_barrier(
+        ((again, after, before, over), over_after)
+    )
+    near = [start, after, two, before]
+    across = [over, over_after, over_two, over_before]
     parts = (
         near
         + [swap(v, "c") for v in near]

time: 85.8 us -> 84.1 us (0.980)
  waiting for transfers between devices: 25.4 us -> 23.2 us
    ppermute x11, waiting for transfers between devices: 6.49 us -> 4.21 us  [swap(): return lax.ppermute(value, axis, [(0, 1), (1, 0)])]
  transfers between devices with their start and end apart: 20 -> 20, of which waited for: 11 -> 12; matrix products, arithmetic and copies ran while one was open for 14% -> 14% of each run, Pallas kernels for 5% -> 5%
where the time goes in v6:
time: 84.1 us; the launch traced here: 83.1 us
  starting transfers between devices  27.7 us (33%)
  waiting for transfers between devices  23.2 us (28%)
  Pallas kernels  19.4 us (23%)
  matrix products  9.82 us (12%)
  local copies, waits for them, and re-layouts  1.53 us (2%)
  other arithmetic  1.35 us (2%)
    pallas_call x1, Pallas kernels, mixed_call(): pl.pallas_call(functools.partial(mixed_kernel, n_exc), out_shape=jax.Shap...  15.2 us
    all_to_all x1, starting transfers between devices, per_device(): lax.all_to_all(packed, ('z', 'xh'), split_axis=0, concat_axis=0, tiled=True)  9.88 us
    dot_general x1, matrix products, per_device(): applied = jnp.einsum('rpk,pkl->rpl', picked, beta_blocks, precision=HIGH)  7.45 us
    ppermute x4, starting transfers between devices, shift(): lax.ppermute(value, 'grp', [(i, (i - k) % N_GRP) for i in range(N_GRP)])  6.84 us
    all_to_all x1, waiting for transfers between devices, per_device(): lax.all_to_all(packed, ('z', 'xh'), split_axis=0, concat_axis=0, tiled=True)  6.8 us
    ppermute x4, waiting for transfers between devices, shift(): lax.ppermute(value, 'grp', [(i, (i - k) % N_GRP) for i in range(N_GRP)])  6.39 us
    all_to_all x1, waiting for transfers between devices, per_device(): lax.all_to_all(mixed_local.reshape(NQ, NT, RA, LANES), ('z', 'xh'), split...  5.8 us
    ppermute x11, starting transfers between devices, swap(): return lax.ppermute(value, axis, [(0, 1), (1, 0)])  5 us
  transfers between devices with their start and end apart: 20, of which 12 were waited for; matrix products, arithmetic and copies ran while one was open for 14% of the time, Pallas kernels for 5%

profile of v6, /device:TPU:2, one launch (start us, length us, event | category | flops | bytes accessed | tf_op | source)
XLA Modules:
  0.0 83.1 jit_solution(7308088645999125598)
XLA Ops:
  0.0 0.0 collective-permute-start
  0.0 2.4 %collective-permute-start.2 = (s32[18,96]{1,0:T(8,128)}, s32[18,96]{1,0:T(8,128)S(1)}, u32[]{:S(2)}, u32[]{:S(2)}) collective-permute-start(s32[18,96]{1,0:T(8,128)} %param.18), channel_id=1, source_target_pairs={{0,3},{1,2},{2,1},{3,0},{4,7},{5,6},{6,5},{7,4},{8,11},{9,10},{10,... | collective-permute-start | bytes 20744 | tf_op jit(solution)/shard_map/ppermute | solution.py:214
  2.4 0.0 collective-permute-start.1
  2.4 1.7 %pack.1 = f32[16,4,8,128]{3,2,1,0:T(8,128)} custom-call(s32[1]{0:T(128)} %bitcast.g_ref, s32[1,4]{1,0:T(1,128)} %mask_ref.1, f32[8,6144]{1,0:T(8,128)} %x_ref.1, f32[1,4,8,8]{3,2,1,0:T(8,128)} %alpha_ref.1), custom_call_target="tpu_custom_call" | custom-call | tf_op jit(solution)/shard_map/pack/pallas_call | solution.py:43
  4.1 9.9 %all-to-all-start = ((f32[16,4,8,128]{3,2,1,0:T(8,128)}), f32[16,4,8,128]{3,2,1,0:T(8,128)S(1)}, u32[]{:S(2)}, u32[]{:S(2)}) async-start(f32[16,4,8,128]{3,2,1,0:T(8,128)} %pack.1), calls=%async_computation | async-start | bytes 524288 | tf_op jit(solution)/shard_map/all_to_all | solution.py:206
  14.0 0.8 slice_bitcast_fusion
  14.8 1.3 %convolution_bitcast_fusion.1 = f32[8,96,128]{2,1,0:T(8,128)S(1)} fusion(f32[8,48,128]{2,0,1:T(8,128)} %bitcast.62, s32[96]{0:T(128)S(1)} %get-tuple-element.42), kind=kOutput, calls=%fused_computation.1 | convolution fusion | flops 56627712 | bytes 590208 | tf_op jit(solution)/shard_map/rnk,pn->rpk/dot_general | solution.py:235
  16.1 0.6 pad_add_fusion.1.place_ref
  16.6 2.5 %prep.1 = (s32[96,128]{1,0:T(8,128)}, s32[96,128]{1,0:T(8,128)}) custom-call(s32[2]{0:T(128)} %pad_add_fusion.1.place_ref, s32[90,512]{1,0:T(8,128)} %src_ref.1, s32[90,512]{1,0:T(8,128)} %pair_ref.1, s32[90,512]{1,0:T(8,128)} %par_ref.1), custom_call_target="tpu_custom_call" | custom-call | tf_op jit(solution)/shard_map/prep/pallas_call | solution.py:81
  19.2 0.0 collective-permute-done
  19.2 0.0 collective-permute-done.1
  19.2 0.7 pad_add_fusion
  19.9 0.8 fusion.24
  20.7 0.1 pad_maximum_fusion
  20.8 6.8 %all-to-all-done.mix_ref = f32[16,4,8,128]{3,2,1,0:T(8,128)S(1)} async-done(((f32[16,4,8,128]{3,2,1,0:T(8,128)}), f32[16,4,8,128]{3,2,1,0:T(8,128)S(1)}, u32[]{:S(2)}, u32[]{:S(2)}) %all-to-all-start) | async-done | bytes 262176 | tf_op jit(solution)/shard_map/all_to_all | solution.py:206
  27.6 1.7 %collective-permute-start.5 = (f32[384,128]{1,0:T(8,128)S(1)}, f32[384,128]{1,0:T(8,128)S(1)}, u32[]{:S(2)}, u32[]{:S(2)}) collective-permute-start(f32[384,128]{1,0:T(8,128)S(1)} %bitcast.55), channel_id=1, source_target_pairs={{0,64},{64,128},{128,192},{192,0},{1,65},{65,129},{129,193},{193,1... | collective-permute-start | bytes 589832 | tf_op jit(solution)/shard_map/ppermute | solution.py:198
  29.2 1.7 %collective-permute-start.4 = (f32[384,128]{1,0:T(8,128)S(1)}, f32[384,128]{1,0:T(8,128)S(1)}, u32[]{:S(2)}, u32[]{:S(2)}) collective-permute-start(f32[384,128]{1,0:T(8,128)S(1)} %bitcast.56), channel_id=1, source_target_pairs={{0,192},{64,0},{128,64},{192,128},{1,193},{65,1},{129,65},{193,129... | collective-permute-start | bytes 589832 | tf_op jit(solution)/shard_map/ppermute | solution.py:198
  30.9 1.4 %collective-permute-start.3 = (f32[384,128]{1,0:T(8,128)S(1)}, f32[384,128]{1,0:T(8,128)S(1)}, u32[]{:S(2)}, u32[]{:S(2)}) collective-permute-start(f32[384,128]{1,0:T(8,128)S(1)} %bitcast.57), channel_id=1, source_target_pairs={{0,2},{2,0},{1,3},{3,1},{4,6},{6,4},{5,7},{7,5},{8,10},{10,8},{9,1... | collective-permute-start | bytes 589832 | tf_op jit(solution)/shard_map/ppermute | solution.py:203
  32.3 2.2 %collective-permute-done.5.rest_3_ = f32[384,128]{1,0:T(8,128)S(1)} collective-permute-done((f32[384,128]{1,0:T(8,128)S(1)}, f32[384,128]{1,0:T(8,128)S(1)}, u32[]{:S(2)}, u32[]{:S(2)}) %collective-permute-start.5) | collective-permute-done | bytes 196640 | tf_op jit(solution)/shard_map/ppermute | solution.py:198
  34.6 0.4 collective-permute-done.4.rest_1_
  34.9 1.7 %collective-permute-done.3.rest_8_ = f32[384,128]{1,0:T(8,128)S(1)} collective-permute-done((f32[384,128]{1,0:T(8,128)S(1)}, f32[384,128]{1,0:T(8,128)S(1)}, u32[]{:S(2)}, u32[]{:S(2)}) %collective-permute-start.3) | collective-permute-done | bytes 196640 | tf_op jit(solution)/shard_map/ppermute | solution.py:203
  36.6 2.0 %collective-permute-start.7 = (f32[384,128]{1,0:T(8,128)S(1)}, f32[384,128]{1,0:T(8,128)S(1)}, u32[]{:S(2)}, u32[]{:S(2)}) collective-permute-start(f32[384,128]{1,0:T(8,128)S(1)} %bitcast.58), channel_id=1, source_target_pairs={{0,128},{64,192},{128,0},{192,64},{1,129},{65,193},{129,1},{193,65... | collective-permute-start | bytes 589832 | tf_op jit(solution)/shard_map/ppermute | solution.py:198
  38.6 1.4 %collective-permute-start.6 = (f32[384,128]{1,0:T(8,128)S(1)}, f32[384,128]{1,0:T(8,128)S(1)}, u32[]{:S(2)}, u32[]{:S(2)}) collective-permute-start(f32[384,128]{1,0:T(8,128)S(1)} %collective-permute-done.4.rest_1_), channel_id=1, source_target_pairs={{0,2},{2,0},{1,3},{3,1},{4,6},{6,4},{5,7},{7,5},{8,10},{10,8},{9,1... | collective-permute-start | bytes 589832 | tf_op jit(solution)/shard_map/ppermute | solution.py:203
  40.0 0.6 collective-permute-start.13
  40.6 1.5 %collective-permute-start.12 = (f32[384,128]{1,0:T(8,128)S(1)}, f32[384,128]{1,0:T(8,128)S(1)}, u32[]{:S(2)}, u32[]{:S(2)}) collective-permute-start(f32[384,128]{1,0:T(8,128)S(1)} %collective-permute-done.3.rest_8_), channel_id=1, source_target_pairs={{0,128},{64,192},{128,0},{192,64},{1,129},{65,193},{129,1},{193,65... | collective-permute-start | bytes 589832 | tf_op jit(solution)/shard_map/ppermute | solution.py:198
  42.1 2.4 %collective-permute-done.7.rest_2_ = f32[384,128]{1,0:T(8,128)S(1)} collective-permute-done((f32[384,128]{1,0:T(8,128)S(1)}, f32[384,128]{1,0:T(8,128)S(1)}, u32[]{:S(2)}, u32[]{:S(2)}) %collective-permute-start.7) | collective-permute-done | bytes 196640 | tf_op jit(solution)/shard_map/ppermute | solution.py:198
  44.5 0.5 collective-permute-start.8
  45.0 0.0 collective-permute-start.9
  45.1 1.3 %collective-permute-done.13.rest_11_ = f32[384,128]{1,0:T(8,128)S(1)} collective-permute-done((f32[384,128]{1,0:T(8,128)S(1)}, f32[384,128]{1,0:T(8,128)S(1)}, u32[]{:S(2)}, u32[]{:S(2)}) %collective-permute-start.13) | collective-permute-done | bytes 196640 | tf_op jit(solution)/shard_map/ppermute | solution.py:203
  46.3 1.4 %collective-permute-done.12.rest_10_ = f32[384,128]{1,0:T(8,128)S(1)} collective-permute-done((f32[384,128]{1,0:T(8,128)S(1)}, f32[384,128]{1,0:T(8,128)S(1)}, u32[]{:S(2)}, u32[]{:S(2)}) %collective-permute-start.12) | collective-permute-done | bytes 196640 | tf_op jit(solution)/shard_map/ppermute | solution.py:198
  47.8 0.0 collective-permute-start.14
  47.8 0.0 collective-permute-done.10.rest_6_
  47.8 0.5 collective-permute-start.15
  48.3 0.0 collective-permute-done.8.rest_4_
  48.3 0.1 collective-permute-start.17
  48.4 0.0 collective-permute-done.9.rest_5_
  48.4 0.4 collective-permute-start.16
  48.8 0.0 collective-permute-done.11.rest_7_
  48.8 0.4 collective-permute-done.14.rest_12_
  49.2 0.3 collective-permute-done.15.rest_13_
  49.5 0.3 collective-permute-done.17.rest_15_
  49.8 0.3 collective-permute-done.16.rest_14_
  50.1 15.2 %mixed.1 = f32[384,128]{1,0:T(8,128)} custom-call(s32[12288]{0:T(1024)} %bitcast.63, s32[12288]{0:T(1024)} %bitcast.64, f32[1944,128]{1,0:T(8,128)S(1)} %bitcast.54, f32[16,4,8,128]{3,2,1,0:T(8,128)S(1)} %all-to-all-done.mix_ref, f32[384,128]{1,0:T(8,128)S(1)} %bitcast.60, f32[384,128]{1,0:T(8,128)S(1)} %collective-permute-done.4.rest_1_, ...), custom_call_target="tpu_custom_call" | custom-call | flops 8847360 | bytes 8388608 | tf_op jit(solution)/shard_map/mixed/pallas_call | solution.py:157
  65.2 3.5 %all-to-all-start.1 = ((f32[16,3,8,128]{3,2,1,0:T(8,128)}), f32[16,3,8,128]{3,2,1,0:T(8,128)S(1)}, u32[]{:S(2)}, u32[]{:S(2)}) async-start(f32[16,3,8,128]{3,2,1,0:T(8,128)} %bitcast.21), calls=%async_computation.1 | async-start | bytes 393216 | tf_op jit(solution)/shard_map/all_to_all | solution.py:264
  68.8 7.5 %fusion.3 = f32[96,8,128]{2,1,0:T(8,128)S(1)} fusion(f32[96,128,128]{2,1,0:T(8,128)} %param.11, f32[8,96,128]{2,1,0:T(8,128)S(1)} %convolution_bitcast_fusion.1), kind=kOutput, calls=%fused_computation.6 | convolution fusion | flops 150994944 | bytes 7077888 | tf_op jit(solution)/shard_map/rpk,pkl->rpl/dot_general | solution.py:275
  76.2 5.8 %all-to-all-done.1 = f32[16,3,8,128]{3,2,1,0:T(8,128)S(1)} async-done(((f32[16,3,8,128]{3,2,1,0:T(8,128)}), f32[16,3,8,128]{3,2,1,0:T(8,128)S(1)}, u32[]{:S(2)}, u32[]{:S(2)}) %all-to-all-start.1) | async-done | bytes 196640 | tf_op jit(solution)/shard_map/all_to_all | solution.py:264
  82.0 0.3 fusion.5
  82.4 0.7 copy.32
  (8 shorter events, 0.0 us)
Async XLA Ops:
  0.0 19.9 %copy-start = (f32[324,18]{0,1:T(8,128)S(1)}, f32[324,18]{0,1:T(8,128)}, u32[]{:S(2)}) copy-start(f32[324,18]{0,1:T(8,128)} %param.19) | copy-start | bytes 69988
  0.0 19.2 %collective-permute-start = (s32[18,96]{1,0:T(8,128)}, s32[18,96]{1,0:T(8,128)S(1)}, u32[]{:S(2)}, u32[]{:S(2)}) collective-permute-start(s32[18,96]{1,0:T(8,128)} %param.18), channel_id=1, source_target_pairs={{0,1},{1,0},{2,3},{3,2},{4,5},{5,4},{6,7},{7,6},{8,9},{9,8},{10,11... | collective-permute-start | bytes 20744 | tf_op jit(solution)/shard_map/ppermute | solution.py:214
  0.0 19.2 %collective-permute-start.2 = (s32[18,96]{1,0:T(8,128)}, s32[18,96]{1,0:T(8,128)S(1)}, u32[]{:S(2)}, u32[]{:S(2)}) collective-permute-start(s32[18,96]{1,0:T(8,128)} %param.18), channel_id=1, source_target_pairs={{0,3},{1,2},{2,1},{3,0},{4,7},{5,6},{6,5},{7,4},{8,11},{9,10},{10,... | collective-permute-start | bytes 20744 | tf_op jit(solution)/shard_map/ppermute | solution.py:214
  2.4 16.8 %collective-permute-start.1 = (s32[18,96]{1,0:T(8,128)}, s32[18,96]{1,0:T(8,128)S(1)}, u32[]{:S(2)}, u32[]{:S(2)}) collective-permute-start(s32[18,96]{1,0:T(8,128)} %param.18), channel_id=1, source_target_pairs={{0,2},{1,3},{2,0},{3,1},{4,6},{5,7},{6,4},{7,5},{8,10},{9,11},{10,... | collective-permute-start | bytes 20744 | tf_op jit(solution)/shard_map/ppermute | solution.py:214
  4.1 23.4 %all-to-all-start = ((f32[16,4,8,128]{3,2,1,0:T(8,128)}), f32[16,4,8,128]{3,2,1,0:T(8,128)S(1)}, u32[]{:S(2)}, u32[]{:S(2)}) async-start(f32[16,4,8,128]{3,2,1,0:T(8,128)} %pack.1), calls=%async_computation | async-start | bytes 524288 | tf_op jit(solution)/shard_map/all_to_all | solution.py:206
  27.6 7.0 %collective-permute-start.5 = (f32[384,128]{1,0:T(8,128)S(1)}, f32[384,128]{1,0:T(8,128)S(1)}, u32[]{:S(2)}, u32[]{:S(2)}) collective-permute-start(f32[384,128]{1,0:T(8,128)S(1)} %bitcast.55), channel_id=1, source_target_pairs={{0,64},{64,128},{128,192},{192,0},{1,65},{65,129},{129,193},{193,1... | collective-permute-start | bytes 589832 | tf_op jit(solution)/shard_map/ppermute | solution.py:198
  29.2 5.7 %collective-permute-start.4 = (f32[384,128]{1,0:T(8,128)S(1)}, f32[384,128]{1,0:T(8,128)S(1)}, u32[]{:S(2)}, u32[]{:S(2)}) collective-permute-start(f32[384,128]{1,0:T(8,128)S(1)} %bitcast.56), channel_id=1, source_target_pairs={{0,192},{64,0},{128,64},{192,128},{1,193},{65,1},{129,65},{193,129... | collective-permute-start | bytes 589832 | tf_op jit(solution)/shard_map/ppermute | solution.py:198
  30.9 5.7 %collective-permute-start.3 = (f32[384,128]{1,0:T(8,128)S(1)}, f32[384,128]{1,0:T(8,128)S(1)}, u32[]{:S(2)}, u32[]{:S(2)}) collective-permute-start(f32[384,128]{1,0:T(8,128)S(1)} %bitcast.57), channel_id=1, source_target_pairs={{0,2},{2,0},{1,3},{3,1},{4,6},{6,4},{5,7},{7,5},{8,10},{10,8},{9,1... | collective-permute-start | bytes 589832 | tf_op jit(solution)/shard_map/ppermute | solution.py:203
  36.6 8.0 %collective-permute-start.7 = (f32[384,128]{1,0:T(8,128)S(1)}, f32[384,128]{1,0:T(8,128)S(1)}, u32[]{:S(2)}, u32[]{:S(2)}) collective-permute-start(f32[384,128]{1,0:T(8,128)S(1)} %bitcast.58), channel_id=1, source_target_pairs={{0,128},{64,192},{128,0},{192,64},{1,129},{65,193},{129,1},{193,65... | collective-permute-start | bytes 589832 | tf_op jit(solution)/shard_map/ppermute | solution.py:198
  38.6 6.0 %collective-permute-start.6 = (f32[384,128]{1,0:T(8,128)S(1)}, f32[384,128]{1,0:T(8,128)S(1)}, u32[]{:S(2)}, u32[]{:S(2)}) collective-permute-start(f32[384,128]{1,0:T(8,128)S(1)} %collective-permute-done.4.rest_1_), channel_id=1, source_target_pairs={{0,2},{2,0},{1,3},{3,1},{4,6},{6,4},{5,7},{7,5},{8,10},{10,8},{9,1... | collective-permute-start | bytes 589832 | tf_op jit(solution)/shard_map/ppermute | solution.py:203
  40.0 6.3 %collective-permute-start.13 = (f32[384,128]{1,0:T(8,128)S(1)}, f32[384,128]{1,0:T(8,128)S(1)}, u32[]{:S(2)}, u32[]{:S(2)}) collective-permute-start(f32[384,128]{1,0:T(8,128)S(1)} %collective-permute-done.5.rest_3_), channel_id=1, source_target_pairs={{0,2},{2,0},{1,3},{3,1},{4,6},{6,4},{5,7},{7,5},{8,10},{10,8},{9,1... | collective-permute-start | bytes 589832 | tf_op jit(solution)/shard_map/ppermute | solution.py:203
  40.6 7.2 %collective-permute-start.12 = (f32[384,128]{1,0:T(8,128)S(1)}, f32[384,128]{1,0:T(8,128)S(1)}, u32[]{:S(2)}, u32[]{:S(2)}) collective-permute-start(f32[384,128]{1,0:T(8,128)S(1)} %collective-permute-done.3.rest_8_), channel_id=1, source_target_pairs={{0,128},{64,192},{128,0},{192,64},{1,129},{65,193},{129,1},{193,65... | collective-permute-start | bytes 589832 | tf_op jit(solution)/shard_map/ppermute | solution.py:198
  44.5 3.2 %collective-permute-start.10 = (f32[384,128]{1,0:T(8,128)S(1)}, f32[384,128]{1,0:T(8,128)S(1)}, u32[]{:S(2)}, u32[]{:S(2)}) collective-permute-start(f32[384,128]{1,0:T(8,128)S(1)} %collective-permute-done.7.rest_2_), channel_id=1, source_target_pairs={{0,1},{1,0},{2,3},{3,2},{4,5},{5,4},{6,7},{7,6},{8,9},{9,8},{10,11... | collective-permute-start | bytes 589832 | tf_op jit(solution)/shard_map/ppermute | solution.py:203
  44.5 3.7 %collective-permute-start.8 = (f32[384,128]{1,0:T(8,128)S(1)}, f32[384,128]{1,0:T(8,128)S(1)}, u32[]{:S(2)}, u32[]{:S(2)}) collective-permute-start(f32[384,128]{1,0:T(8,128)S(1)} %bitcast.59), channel_id=1, source_target_pairs={{0,1},{1,0},{2,3},{3,2},{4,5},{5,4},{6,7},{7,6},{8,9},{9,8},{10,11... | collective-permute-start | bytes 589832 | tf_op jit(solution)/shard_map/ppermute | solution.py:203
  45.0 3.3 %collective-permute-start.9 = (f32[384,128]{1,0:T(8,128)S(1)}, f32[384,128]{1,0:T(8,128)S(1)}, u32[]{:S(2)}, u32[]{:S(2)}) collective-permute-start(f32[384,128]{1,0:T(8,128)S(1)} %collective-permute-done.4.rest_1_), channel_id=1, source_target_pairs={{0,1},{1,0},{2,3},{3,2},{4,5},{5,4},{6,7},{7,6},{8,9},{9,8},{10,11... | collective-permute-start | bytes 589832 | tf_op jit(solution)/shard_map/ppermute | solution.py:203
  46.3 2.5 %collective-permute-start.11 = (f32[384,128]{1,0:T(8,128)S(1)}, f32[384,128]{1,0:T(8,128)S(1)}, u32[]{:S(2)}, u32[]{:S(2)}) collective-permute-start(f32[384,128]{1,0:T(8,128)S(1)} %collective-permute-done.5.rest_3_), channel_id=1, source_target_pairs={{0,1},{1,0},{2,3},{3,2},{4,5},{5,4},{6,7},{7,6},{8,9},{9,8},{10,11... | collective-permute-start | bytes 589832 | tf_op jit(solution)/shard_map/ppermute | solution.py:203
  47.8 1.4 %collective-permute-start.14 = (f32[384,128]{1,0:T(8,128)S(1)}, f32[384,128]{1,0:T(8,128)S(1)}, u32[]{:S(2)}, u32[]{:S(2)}) collective-permute-start(f32[384,128]{1,0:T(8,128)S(1)} %collective-permute-done.3.rest_8_), channel_id=1, source_target_pairs={{0,1},{1,0},{2,3},{3,2},{4,5},{5,4},{6,7},{7,6},{8,9},{9,8},{10,11... | collective-permute-start | bytes 589832 | tf_op jit(solution)/shard_map/ppermute | solution.py:203
  47.8 1.7 %collective-permute-start.15 = (f32[384,128]{1,0:T(8,128)S(1)}, f32[384,128]{1,0:T(8,128)S(1)}, u32[]{:S(2)}, u32[]{:S(2)}) collective-permute-start(f32[384,128]{1,0:T(8,128)S(1)} %collective-permute-done.6.rest_9_), channel_id=1, source_target_pairs={{0,1},{1,0},{2,3},{3,2},{4,5},{5,4},{6,7},{7,6},{8,9},{9,8},{10,11... | collective-permute-start | bytes 589832 | tf_op jit(solution)/shard_map/ppermute | solution.py:203
  48.3 1.5 %collective-permute-start.17 = (f32[384,128]{1,0:T(8,128)S(1)}, f32[384,128]{1,0:T(8,128)S(1)}, u32[]{:S(2)}, u32[]{:S(2)}) collective-permute-start(f32[384,128]{1,0:T(8,128)S(1)} %collective-permute-done.13.rest_11_), channel_id=1, source_target_pairs={{0,1},{1,0},{2,3},{3,2},{4,5},{5,4},{6,7},{7,6},{8,9},{9,8},{10,11... | collective-permute-start | bytes 589832 | tf_op jit(solution)/shard_map/ppermute | solution.py:203
  48.4 1.7 %collective-permute-start.16 = (f32[384,128]{1,0:T(8,128)S(1)}, f32[384,128]{1,0:T(8,128)S(1)}, u32[]{:S(2)}, u32[]{:S(2)}) collective-permute-start(f32[384,128]{1,0:T(8,128)S(1)} %collective-permute-done.12.rest_10_), channel_id=1, source_target_pairs={{0,1},{1,0},{2,3},{3,2},{4,5},{5,4},{6,7},{7,6},{8,9},{9,8},{10,11... | collective-permute-start | bytes 589832 | tf_op jit(solution)/shard_map/ppermute | solution.py:203
  65.2 16.8 %all-to-all-start.1 = ((f32[16,3,8,128]{3,2,1,0:T(8,128)}), f32[16,3,8,128]{3,2,1,0:T(8,128)S(1)}, u32[]{:S(2)}, u32[]{:S(2)}) async-start(f32[16,3,8,128]{3,2,1,0:T(8,128)} %bitcast.21), calls=%async_computation.1 | async-start | bytes 393216 | tf_op jit(solution)/shard_map/all_to_all | solution.py:264

commit v7 on v6

--- a/solution.py
+++ b/solution.py
@@ -175,6 +175,23 @@
     )(cidx, widx, wtab, mix, *parts)
 
 
+def place_kernel(list_ref, applied_ref, o_ref):
+    o_ref[...] = jnp.zeros(o_ref.shape, jnp.float32)
+    for p in range(applied_ref.shape[0]):
+        t = list_ref[1, p]
+        o_ref[t] = o_ref[t] + applied_ref[p]
+
+
+def place_call(block_list, applied, block_count):
+    return pl.pallas_call(
+        place_kernel,
+        out_shape=jax.ShapeDtypeStruct((block_count,) + applied.shape[1:], jnp.float32),
+        in_specs=[SMEM, VMEM],
+        out_specs=VMEM,
+        name="place",
+    )(block_list, applied)
+
+
 def per_device(
     coeff,
     beta_blocks,
@@ -232,7 +249,7 @@
     blocked = coeff.reshape(alpha_rows, block_count, block_size)
     block_ids = jnp.arange(block_count, dtype=jnp.int32)
     choosing = (block_list[0][:, None] == block_ids[None, :]).astype(jnp.float32)
-    picked = jnp.einsum("rnk,pn->rpk", blocked, choosing, precision=HIGH)
+    picked = jnp.einsum("rnk,pn->prk", blocked, choosing, precision=HIGH)
     arrived, wtab, cidx, widx, picked = lax.optimization_barrier(
         (arrived, wtab, cidx, widx, picked)
     )
@@ -242,8 +259,8 @@
     again, over, after, before = lax.optimization_barrier((own, over, after, before))
     over_after, over_before = swap(after, "xl"), swap(before, "xl")
     two, over_two = shift(again, 2), shift(over, 2)
-    (start, after, before, over), over_after = lax.optimization_barrier(
-        ((again, after, before, over), over_after)
+    (start, after, before, over), two = lax.optimization_barrier(
+        ((again, after, before, over), two)
     )
     near = [start, after, two, before]
     across = [over, over_after, over_two, over_before]
@@ -268,17 +285,12 @@
         concat_axis=0,
         tiled=True,
     )
-    mixed = (
-        mixed.reshape(NQ * NT, RA, LANES).transpose(1, 0, 2).reshape(alpha_rows, -1)
-    )
-
-    applied = jnp.einsum("rpk,pkl->rpl", picked, beta_blocks, precision=HIGH)
-    placing = (block_list[1][:, None] == block_ids[None, :]).astype(jnp.float32)
-    same_beta = jnp.einsum("rpl,pn->rnl", applied, placing, precision=HIGH).reshape(
-        alpha_rows, beta_width
-    )
-
-    return mixed + same_beta
+    mixed = mixed.reshape(block_count, alpha_rows, block_size)
+
+    applied = jnp.einsum("prk,pkl->prl", picked, beta_blocks, precision=HIGH)
+    same_beta = place_call(block_list, applied, block_count)
+    total = mixed + same_beta
+    return total.transpose(1, 0, 2).reshape(alpha_rows, beta_width)
 
 
 def solution(mesh):

time: 84.1 us -> 85.3 us (1.014)
  Pallas kernels: 19.4 us -> 21.3 us
  waiting for transfers between devices: 23.2 us -> 21.5 us
  other arithmetic: 1.35 us -> 3 us
    all_to_all x1, waiting for transfers between devices: 5.8 us -> 2.61 us  [per_device(): lax.all_to_all(mixed_local.reshape(NQ, NT, RA, LANES), ('z', 'xh'), split...]
    ppermute x4, waiting for transfers between devices: 6.39 us -> 8.91 us  [shift(): lax.ppermute(value, 'grp', [(i, (i - k) % N_GRP) for i in range(N_GRP)])]
    pallas_call x0 -> x1, Pallas kernels: none -> 1.91 us  [place_call(): pl.pallas_call(place_kernel, out_shape=jax.ShapeDtypeStruct((block_count,...]
    add x0 -> x1, other arithmetic: none -> 1.62 us  [per_device(): total = mixed + same_beta]
    ppermute x11, waiting for transfers between devices: 4.21 us -> 2.94 us  [swap(): return lax.ppermute(value, axis, [(0, 1), (1, 0)])]
    dot_general x3 -> x2, matrix products: 9.05 us -> 9.42 us  [the longest x1 8.13 us: per_device(): applied = jnp.einsum('prk,pkl->prl', picked, beta_blocks, precision=HIGH)]
  transfers between devices with their start and end apart: 20 -> 20, of which waited for: 12 -> 12; matrix products, arithmetic and copies ran while one was open for 14% -> 15% of each run, Pallas kernels for 5% -> 7%
where the time goes in v7:
time: 85.3 us; the launch traced here: 84.5 us
  starting transfers between devices  27.7 us (32%)
  waiting for transfers between devices  21.5 us (25%)
  Pallas kernels  21.3 us (25%)
  matrix products  10.2 us (12%)
  other arithmetic  3 us (4%)
    pallas_call x1, Pallas kernels, mixed_call(): pl.pallas_call(functools.partial(mixed_kernel, n_exc), out_shape=jax.Shap...  15.2 us
    all_to_all x1, starting transfers between devices, per_device(): lax.all_to_all(packed, ('z', 'xh'), split_axis=0, concat_axis=0, tiled=True)  9.6 us
    ppermute x4, waiting for transfers between devices, shift(): lax.ppermute(value, 'grp', [(i, (i - k) % N_GRP) for i in range(N_GRP)])  8.91 us
    dot_general x1, matrix products, per_device(): applied = jnp.einsum('prk,pkl->prl', picked, beta_blocks, precision=HIGH)  8.13 us
    all_to_all x1, waiting for transfers between devices, per_device(): lax.all_to_all(packed, ('z', 'xh'), split_axis=0, concat_axis=0, tiled=True)  7.07 us
    ppermute x4, starting transfers between devices, shift(): lax.ppermute(value, 'grp', [(i, (i - k) % N_GRP) for i in range(N_GRP)])  6.55 us
    ppermute x11, starting transfers between devices, swap(): return lax.ppermute(value, axis, [(0, 1), (1, 0)])  5.09 us
    all_to_all x1, starting transfers between devices, per_device(): lax.all_to_all(mixed_local.reshape(NQ, NT, RA, LANES), ('z', 'xh'), split...  4.03 us
  transfers between devices with their start and end apart: 20, of which 12 were waited for; matrix products, arithmetic and copies ran while one was open for 15% of the time, Pallas kernels for 7%

profile of v7, /device:TPU:2, one launch (start us, length us, event | category | flops | bytes accessed | tf_op | source)
XLA Modules:
  0.0 84.5 jit_solution(15149071276688158464)
XLA Ops:
  0.0 0.0 collective-permute-start.2
  0.0 2.3 %collective-permute-start.1 = (s32[18,96]{1,0:T(8,128)}, s32[18,96]{1,0:T(8,128)S(1)}, u32[]{:S(2)}, u32[]{:S(2)}) collective-permute-start(s32[18,96]{1,0:T(8,128)} %param.18), channel_id=1, source_target_pairs={{0,2},{1,3},{2,0},{3,1},{4,6},{5,7},{6,4},{7,5},{8,10},{9,11},{10,... | collective-permute-start | bytes 20744 | tf_op jit(solution)/shard_map/ppermute | solution.py:231
  2.3 0.1 collective-permute-start
  2.4 1.7 %pack.1 = f32[16,4,8,128]{3,2,1,0:T(8,128)} custom-call(s32[1]{0:T(128)} %bitcast.g_ref, s32[1,4]{1,0:T(1,128)} %mask_ref.1, f32[8,6144]{1,0:T(8,128)} %x_ref.1, f32[1,4,8,8]{3,2,1,0:T(8,128)} %alpha_ref.1), custom_call_target="tpu_custom_call" | custom-call | tf_op jit(solution)/shard_map/pack/pallas_call | solution.py:43
  4.1 9.6 %all-to-all-start = ((f32[16,4,8,128]{3,2,1,0:T(8,128)}), f32[16,4,8,128]{3,2,1,0:T(8,128)S(1)}, u32[]{:S(2)}, u32[]{:S(2)}) async-start(f32[16,4,8,128]{3,2,1,0:T(8,128)} %pack.1), calls=%async_computation | async-start | bytes 524288 | tf_op jit(solution)/shard_map/all_to_all | solution.py:223
  13.7 0.7 slice_bitcast_fusion
  14.4 1.3 %fusion.2 = f32[96,8,128]{2,0,1:T(8,128)S(1)} fusion(f32[8,48,128]{2,0,1:T(8,128)} %bitcast.45, s32[96]{0:T(128)S(1)} %slice_bitcast_fusion), kind=kOutput, calls=%fused_computation.5 | convolution fusion | flops 56627712 | bytes 590208 | tf_op jit(solution)/shard_map/rnk,pn->prk/dot_general | solution.py:252
  15.7 0.6 pad_add_fusion.1.place_ref
  16.3 2.5 %prep.1 = (s32[96,128]{1,0:T(8,128)}, s32[96,128]{1,0:T(8,128)}) custom-call(s32[2]{0:T(128)} %pad_add_fusion.1.place_ref, s32[90,512]{1,0:T(8,128)} %src_ref.1, s32[90,512]{1,0:T(8,128)} %pair_ref.1, s32[90,512]{1,0:T(8,128)} %par_ref.1), custom_call_target="tpu_custom_call" | custom-call | tf_op jit(solution)/shard_map/prep/pallas_call | solution.py:81
  18.8 0.0 collective-permute-done.2
  18.8 0.0 collective-permute-done.1
  18.8 0.0 collective-permute-done
  18.8 0.7 pad_add_fusion
  19.6 0.8 fusion.14
  20.3 0.1 pad_maximum_fusion
  20.4 7.1 %all-to-all-done.mix_ref = f32[16,4,8,128]{3,2,1,0:T(8,128)S(1)} async-done(((f32[16,4,8,128]{3,2,1,0:T(8,128)}), f32[16,4,8,128]{3,2,1,0:T(8,128)S(1)}, u32[]{:S(2)}, u32[]{:S(2)}) %all-to-all-start) | async-done | bytes 262176 | tf_op jit(solution)/shard_map/all_to_all | solution.py:223
  27.5 1.5 %collective-permute-start.3 = (f32[384,128]{1,0:T(8,128)S(1)}, f32[384,128]{1,0:T(8,128)S(1)}, u32[]{:S(2)}, u32[]{:S(2)}) collective-permute-start(f32[384,128]{1,0:T(8,128)S(1)} %bitcast.39), channel_id=1, source_target_pairs={{0,2},{2,0},{1,3},{3,1},{4,6},{6,4},{5,7},{7,5},{8,10},{10,8},{9,1... | collective-permute-start | bytes 589832 | tf_op jit(solution)/shard_map/ppermute | solution.py:220
  29.0 3.0 %collective-permute-start.4 = (f32[384,128]{1,0:T(8,128)S(1)}, f32[384,128]{1,0:T(8,128)S(1)}, u32[]{:S(2)}, u32[]{:S(2)}) collective-permute-start(f32[384,128]{1,0:T(8,128)S(1)} %bitcast.40), channel_id=1, source_target_pairs={{0,192},{64,0},{128,64},{192,128},{1,193},{65,1},{129,65},{193,129... | collective-permute-start | bytes 589832 | tf_op jit(solution)/shard_map/ppermute | solution.py:215
  32.1 0.0 collective-permute-start.5
  32.1 1.2 %collective-permute-done.3.rest_8_ = f32[384,128]{1,0:T(8,128)S(1)} collective-permute-done((f32[384,128]{1,0:T(8,128)S(1)}, f32[384,128]{1,0:T(8,128)S(1)}, u32[]{:S(2)}, u32[]{:S(2)}) %collective-permute-start.3) | collective-permute-done | bytes 196640 | tf_op jit(solution)/shard_map/ppermute | solution.py:220
  33.3 2.0 %collective-permute-done.4.rest_1_ = f32[384,128]{1,0:T(8,128)S(1)} collective-permute-done((f32[384,128]{1,0:T(8,128)S(1)}, f32[384,128]{1,0:T(8,128)S(1)}, u32[]{:S(2)}, u32[]{:S(2)}) %collective-permute-start.4) | collective-permute-done | bytes 196640 | tf_op jit(solution)/shard_map/ppermute | solution.py:215
  35.2 3.7 %collective-permute-done.5.rest_3_ = f32[384,128]{1,0:T(8,128)S(1)} collective-permute-done((f32[384,128]{1,0:T(8,128)S(1)}, f32[384,128]{1,0:T(8,128)S(1)}, u32[]{:S(2)}, u32[]{:S(2)}) %collective-permute-start.5) | collective-permute-done | bytes 196640 | tf_op jit(solution)/shard_map/ppermute | solution.py:215
  38.9 0.0 collective-permute-start.6
  38.9 0.6 collective-permute-start.11
  39.5 3.5 %collective-permute-start.12 = (f32[384,128]{1,0:T(8,128)S(1)}, f32[384,128]{1,0:T(8,128)S(1)}, u32[]{:S(2)}, u32[]{:S(2)}) collective-permute-start(f32[384,128]{1,0:T(8,128)S(1)} %collective-permute-done.3.rest_8_), channel_id=1, source_target_pairs={{0,128},{64,192},{128,0},{192,64},{1,129},{65,193},{129,1},{193,65... | collective-permute-start | bytes 589832 | tf_op jit(solution)/shard_map/ppermute | solution.py:215
  43.1 1.4 %collective-permute-start.13 = (f32[384,128]{1,0:T(8,128)S(1)}, f32[384,128]{1,0:T(8,128)S(1)}, u32[]{:S(2)}, u32[]{:S(2)}) collective-permute-start(f32[384,128]{1,0:T(8,128)S(1)} %collective-permute-done.5.rest_3_), channel_id=1, source_target_pairs={{0,2},{2,0},{1,3},{3,1},{4,6},{6,4},{5,7},{7,5},{8,10},{10,8},{9,1... | collective-permute-start | bytes 589832 | tf_op jit(solution)/shard_map/ppermute | solution.py:220
  44.5 1.7 %collective-permute-done.6.rest_2_ = f32[384,128]{1,0:T(8,128)S(1)} collective-permute-done((f32[384,128]{1,0:T(8,128)S(1)}, f32[384,128]{1,0:T(8,128)S(1)}, u32[]{:S(2)}, u32[]{:S(2)}) %collective-permute-start.6) | collective-permute-done | bytes 196640 | tf_op jit(solution)/shard_map/ppermute | solution.py:215
  46.2 0.0 collective-permute-start.7
  46.2 0.5 collective-permute-start.8
  46.7 0.0 collective-permute-start.9
  46.7 1.6 %collective-permute-done.12.rest_10_ = f32[384,128]{1,0:T(8,128)S(1)} collective-permute-done((f32[384,128]{1,0:T(8,128)S(1)}, f32[384,128]{1,0:T(8,128)S(1)}, u32[]{:S(2)}, u32[]{:S(2)}) %collective-permute-start.12) | collective-permute-done | bytes 196640 | tf_op jit(solution)/shard_map/ppermute | solution.py:215
  48.3 0.0 collective-permute-start.10
  48.3 0.5 collective-permute-done.13.rest_11_
  48.7 0.1 collective-permute-start.14
  48.8 0.0 collective-permute-done.7.rest_4_
  48.8 0.5 collective-permute-start.15
  49.3 0.1 collective-permute-start.16
  49.3 0.4 collective-permute-start.17
  49.8 0.4 collective-permute-done.14.rest_12_
  50.2 0.3 collective-permute-done.15.rest_13_
  50.5 0.3 collective-permute-done.16.rest_14_
  50.7 0.3 collective-permute-done.17.rest_15_
  51.0 15.2 %mixed.1 = f32[384,128]{1,0:T(8,128)} custom-call(s32[12288]{0:T(1024)} %bitcast.46, s32[12288]{0:T(1024)} %bitcast.47, f32[1944,128]{1,0:T(8,128)S(1)} %bitcast.38, f32[16,4,8,128]{3,2,1,0:T(8,128)S(1)} %all-to-all-done.mix_ref, f32[384,128]{1,0:T(8,128)S(1)} %bitcast.44, f32[384,128]{1,0:T(8,128)S(1)} %collective-permute-done.4.rest_1_, ...), custom_call_target="tpu_custom_call" | custom-call | flops 8847360 | bytes 8388608 | tf_op jit(solution)/shard_map/mixed/pallas_call | solution.py:157
  66.2 4.0 %all-to-all-start.1 = ((f32[16,3,8,128]{3,2,1,0:T(8,128)}), f32[16,3,8,128]{3,2,1,0:T(8,128)S(1)}, u32[]{:S(2)}, u32[]{:S(2)}) async-start(f32[16,3,8,128]{3,2,1,0:T(8,128)} %bitcast.20), calls=%async_computation.1 | async-start | bytes 393216 | tf_op jit(solution)/shard_map/all_to_all | solution.py:281
  70.3 8.1 %fusion.applied_ref = f32[96,8,128]{2,1,0:T(8,128)} fusion(f32[96,128,128]{2,1,0:T(8,128)} %param.11, f32[96,8,128]{2,0,1:T(8,128)S(1)} %fusion.2), kind=kOutput, calls=%fused_computation.2 | convolution fusion | flops 150994944 | bytes 7077888 | tf_op jit(solution)/shard_map/prk,pkl->prl/dot_general | solution.py:290
  78.4 1.9 %place.1 = f32[48,8,128]{2,1,0:T(8,128)} custom-call(s32[2,96]{1,0:T(2,128)} %list_ref.1, f32[96,8,128]{2,1,0:T(8,128)} %fusion.applied_ref), custom_call_target="tpu_custom_call" | custom-call | tf_op jit(solution)/shard_map/place/pallas_call | solution.py:186
  80.3 2.6 %all-to-all-done.1 = f32[16,3,8,128]{3,2,1,0:T(8,128)S(1)} async-done(((f32[16,3,8,128]{3,2,1,0:T(8,128)}), f32[16,3,8,128]{3,2,1,0:T(8,128)S(1)}, u32[]{:S(2)}, u32[]{:S(2)}) %all-to-all-start.1) | async-done | bytes 196640 | tf_op jit(solution)/shard_map/all_to_all | solution.py:281
  82.9 1.6 %bitcast_add_fusion = f32[48,8,128]{2,1,0:T(8,128)} fusion(f32[48,8,128]{2,1,0:T(8,128)} %place.1, f32[16,3,8,128]{3,2,1,0:T(8,128)S(1)} %all-to-all-done.1), kind=kLoop, calls=%fused_computation.4 | loop fusion | flops 49152 | bytes 589824 | tf_op jit(solution)/shard_map/add | solution.py:292
  (8 shorter events, 0.0 us)
Async XLA Ops:
  0.0 19.6 %copy-start = (f32[324,18]{0,1:T(8,128)S(1)}, f32[324,18]{0,1:T(8,128)}, u32[]{:S(2)}) copy-start(f32[324,18]{0,1:T(8,128)} %param.19) | copy-start | bytes 69988
  0.0 18.8 %collective-permute-start.2 = (s32[18,96]{1,0:T(8,128)}, s32[18,96]{1,0:T(8,128)S(1)}, u32[]{:S(2)}, u32[]{:S(2)}) collective-permute-start(s32[18,96]{1,0:T(8,128)} %param.18), channel_id=1, source_target_pairs={{0,3},{1,2},{2,1},{3,0},{4,7},{5,6},{6,5},{7,4},{8,11},{9,10},{10,... | collective-permute-start | bytes 20744 | tf_op jit(solution)/shard_map/ppermute | solution.py:231
  0.0 18.8 %collective-permute-start.1 = (s32[18,96]{1,0:T(8,128)}, s32[18,96]{1,0:T(8,128)S(1)}, u32[]{:S(2)}, u32[]{:S(2)}) collective-permute-start(s32[18,96]{1,0:T(8,128)} %param.18), channel_id=1, source_target_pairs={{0,2},{1,3},{2,0},{3,1},{4,6},{5,7},{6,4},{7,5},{8,10},{9,11},{10,... | collective-permute-start | bytes 20744 | tf_op jit(solution)/shard_map/ppermute | solution.py:231
  2.3 16.5 %collective-permute-start = (s32[18,96]{1,0:T(8,128)}, s32[18,96]{1,0:T(8,128)S(1)}, u32[]{:S(2)}, u32[]{:S(2)}) collective-permute-start(s32[18,96]{1,0:T(8,128)} %param.18), channel_id=1, source_target_pairs={{0,1},{1,0},{2,3},{3,2},{4,5},{5,4},{6,7},{7,6},{8,9},{9,8},{10,11... | collective-permute-start | bytes 20744 | tf_op jit(solution)/shard_map/ppermute | solution.py:231
  4.1 23.4 %all-to-all-start = ((f32[16,4,8,128]{3,2,1,0:T(8,128)}), f32[16,4,8,128]{3,2,1,0:T(8,128)S(1)}, u32[]{:S(2)}, u32[]{:S(2)}) async-start(f32[16,4,8,128]{3,2,1,0:T(8,128)} %pack.1), calls=%async_computation | async-start | bytes 524288 | tf_op jit(solution)/shard_map/all_to_all | solution.py:223
  27.5 5.8 %collective-permute-start.3 = (f32[384,128]{1,0:T(8,128)S(1)}, f32[384,128]{1,0:T(8,128)S(1)}, u32[]{:S(2)}, u32[]{:S(2)}) collective-permute-start(f32[384,128]{1,0:T(8,128)S(1)} %bitcast.39), channel_id=1, source_target_pairs={{0,2},{2,0},{1,3},{3,1},{4,6},{6,4},{5,7},{7,5},{8,10},{10,8},{9,1... | collective-permute-start | bytes 589832 | tf_op jit(solution)/shard_map/ppermute | solution.py:220
  29.0 6.2 %collective-permute-start.4 = (f32[384,128]{1,0:T(8,128)S(1)}, f32[384,128]{1,0:T(8,128)S(1)}, u32[]{:S(2)}, u32[]{:S(2)}) collective-permute-start(f32[384,128]{1,0:T(8,128)S(1)} %bitcast.40), channel_id=1, source_target_pairs={{0,192},{64,0},{128,64},{192,128},{1,193},{65,1},{129,65},{193,129... | collective-permute-start | bytes 589832 | tf_op jit(solution)/shard_map/ppermute | solution.py:215
  32.1 6.9 %collective-permute-start.5 = (f32[384,128]{1,0:T(8,128)S(1)}, f32[384,128]{1,0:T(8,128)S(1)}, u32[]{:S(2)}, u32[]{:S(2)}) collective-permute-start(f32[384,128]{1,0:T(8,128)S(1)} %bitcast.41), channel_id=1, source_target_pairs={{0,64},{64,128},{128,192},{192,0},{1,65},{65,129},{129,193},{193,1... | collective-permute-start | bytes 589832 | tf_op jit(solution)/shard_map/ppermute | solution.py:215
  38.9 7.2 %collective-permute-start.6 = (f32[384,128]{1,0:T(8,128)S(1)}, f32[384,128]{1,0:T(8,128)S(1)}, u32[]{:S(2)}, u32[]{:S(2)}) collective-permute-start(f32[384,128]{1,0:T(8,128)S(1)} %bitcast.42), channel_id=1, source_target_pairs={{0,128},{64,192},{128,0},{192,64},{1,129},{65,193},{129,1},{193,65... | collective-permute-start | bytes 589832 | tf_op jit(solution)/shard_map/ppermute | solution.py:215
  38.9 7.7 %collective-permute-start.11 = (f32[384,128]{1,0:T(8,128)S(1)}, f32[384,128]{1,0:T(8,128)S(1)}, u32[]{:S(2)}, u32[]{:S(2)}) collective-permute-start(f32[384,128]{1,0:T(8,128)S(1)} %collective-permute-done.4.rest_1_), channel_id=1, source_target_pairs={{0,2},{2,0},{1,3},{3,1},{4,6},{6,4},{5,7},{7,5},{8,10},{10,8},{9,1... | collective-permute-start | bytes 589832 | tf_op jit(solution)/shard_map/ppermute | solution.py:220
  39.5 8.7 %collective-permute-start.12 = (f32[384,128]{1,0:T(8,128)S(1)}, f32[384,128]{1,0:T(8,128)S(1)}, u32[]{:S(2)}, u32[]{:S(2)}) collective-permute-start(f32[384,128]{1,0:T(8,128)S(1)} %collective-permute-done.3.rest_8_), channel_id=1, source_target_pairs={{0,128},{64,192},{128,0},{192,64},{1,129},{65,193},{129,1},{193,65... | collective-permute-start | bytes 589832 | tf_op jit(solution)/shard_map/ppermute | solution.py:215
  43.1 5.7 %collective-permute-start.13 = (f32[384,128]{1,0:T(8,128)S(1)}, f32[384,128]{1,0:T(8,128)S(1)}, u32[]{:S(2)}, u32[]{:S(2)}) collective-permute-start(f32[384,128]{1,0:T(8,128)S(1)} %collective-permute-done.5.rest_3_), channel_id=1, source_target_pairs={{0,2},{2,0},{1,3},{3,1},{4,6},{6,4},{5,7},{7,5},{8,10},{10,8},{9,1... | collective-permute-start | bytes 589832 | tf_op jit(solution)/shard_map/ppermute | solution.py:220
  46.2 2.6 %collective-permute-start.7 = (f32[384,128]{1,0:T(8,128)S(1)}, f32[384,128]{1,0:T(8,128)S(1)}, u32[]{:S(2)}, u32[]{:S(2)}) collective-permute-start(f32[384,128]{1,0:T(8,128)S(1)} %bitcast.43), channel_id=1, source_target_pairs={{0,1},{1,0},{2,3},{3,2},{4,5},{5,4},{6,7},{7,6},{8,9},{9,8},{10,11... | collective-permute-start | bytes 589832 | tf_op jit(solution)/shard_map/ppermute | solution.py:220
  46.2 3.1 %collective-permute-start.8 = (f32[384,128]{1,0:T(8,128)S(1)}, f32[384,128]{1,0:T(8,128)S(1)}, u32[]{:S(2)}, u32[]{:S(2)}) collective-permute-start(f32[384,128]{1,0:T(8,128)S(1)} %collective-permute-done.4.rest_1_), channel_id=1, source_target_pairs={{0,1},{1,0},{2,3},{3,2},{4,5},{5,4},{6,7},{7,6},{8,9},{9,8},{10,11... | collective-permute-start | bytes 589832 | tf_op jit(solution)/shard_map/ppermute | solution.py:220
  46.7 2.7 %collective-permute-start.9 = (f32[384,128]{1,0:T(8,128)S(1)}, f32[384,128]{1,0:T(8,128)S(1)}, u32[]{:S(2)}, u32[]{:S(2)}) collective-permute-start(f32[384,128]{1,0:T(8,128)S(1)} %collective-permute-done.6.rest_2_), channel_id=1, source_target_pairs={{0,1},{1,0},{2,3},{3,2},{4,5},{5,4},{6,7},{7,6},{8,9},{9,8},{10,11... | collective-permute-start | bytes 589832 | tf_op jit(solution)/shard_map/ppermute | solution.py:220
  48.3 1.5 %collective-permute-start.10 = (f32[384,128]{1,0:T(8,128)S(1)}, f32[384,128]{1,0:T(8,128)S(1)}, u32[]{:S(2)}, u32[]{:S(2)}) collective-permute-start(f32[384,128]{1,0:T(8,128)S(1)} %collective-permute-done.5.rest_3_), channel_id=1, source_target_pairs={{0,1},{1,0},{2,3},{3,2},{4,5},{5,4},{6,7},{7,6},{8,9},{9,8},{10,11... | collective-permute-start | bytes 589832 | tf_op jit(solution)/shard_map/ppermute | solution.py:220
  48.7 1.4 %collective-permute-start.14 = (f32[384,128]{1,0:T(8,128)S(1)}, f32[384,128]{1,0:T(8,128)S(1)}, u32[]{:S(2)}, u32[]{:S(2)}) collective-permute-start(f32[384,128]{1,0:T(8,128)S(1)} %collective-permute-done.3.rest_8_), channel_id=1, source_target_pairs={{0,1},{1,0},{2,3},{3,2},{4,5},{5,4},{6,7},{7,6},{8,9},{9,8},{10,11... | collective-permute-start | bytes 589832 | tf_op jit(solution)/shard_map/ppermute | solution.py:220
  48.8 1.7 %collective-permute-start.15 = (f32[384,128]{1,0:T(8,128)S(1)}, f32[384,128]{1,0:T(8,128)S(1)}, u32[]{:S(2)}, u32[]{:S(2)}) collective-permute-start(f32[384,128]{1,0:T(8,128)S(1)} %collective-permute-done.11.rest_9_), channel_id=1, source_target_pairs={{0,1},{1,0},{2,3},{3,2},{4,5},{5,4},{6,7},{7,6},{8,9},{9,8},{10,11... | collective-permute-start | bytes 589832 | tf_op jit(solution)/shard_map/ppermute | solution.py:220
  49.3 1.5 %collective-permute-start.16 = (f32[384,128]{1,0:T(8,128)S(1)}, f32[384,128]{1,0:T(8,128)S(1)}, u32[]{:S(2)}, u32[]{:S(2)}) collective-permute-start(f32[384,128]{1,0:T(8,128)S(1)} %collective-permute-done.12.rest_10_), channel_id=1, source_target_pairs={{0,1},{1,0},{2,3},{3,2},{4,5},{5,4},{6,7},{7,6},{8,9},{9,8},{10,11... | collective-permute-start | bytes 589832 | tf_op jit(solution)/shard_map/ppermute | solution.py:220
  49.3 1.7 %collective-permute-start.17 = (f32[384,128]{1,0:T(8,128)S(1)}, f32[384,128]{1,0:T(8,128)S(1)}, u32[]{:S(2)}, u32[]{:S(2)}) collective-permute-start(f32[384,128]{1,0:T(8,128)S(1)} %collective-permute-done.13.rest_11_), channel_id=1, source_target_pairs={{0,1},{1,0},{2,3},{3,2},{4,5},{5,4},{6,7},{7,6},{8,9},{9,8},{10,11... | collective-permute-start | bytes 589832 | tf_op jit(solution)/shard_map/ppermute | solution.py:220
  66.2 16.7 %all-to-all-start.1 = ((f32[16,3,8,128]{3,2,1,0:T(8,128)}), f32[16,3,8,128]{3,2,1,0:T(8,128)S(1)}, u32[]{:S(2)}, u32[]{:S(2)}) async-start(f32[16,3,8,128]{3,2,1,0:T(8,128)} %bitcast.20), calls=%async_computation.1 | async-start | bytes 393216 | tf_op jit(solution)/shard_map/all_to_all | solution.py:281

commit v8 on v6

--- a/solution.py
+++ b/solution.py
@@ -18,6 +18,7 @@
 NT = 3
 PART = NQ * NT * RA
 EPAD = 96
+PLACES = [(i,) for i in (0, 1, 2, 3, 8, 9, 10, 11, 6, 13, 14, 15)] + [(4, 5, 7, 12)]
 CHUNK = 32
 
 SMEM = pl.BlockSpec(memory_space=pltpu.SMEM)
@@ -91,7 +92,7 @@
 
 
 def mixed_kernel(n_exc, cidx_hbm, widx_hbm, w_ref, mix_ref, *rest):
-    count = N_GRP * NS
+    count = len(PLACES)
     parts = rest[:count]
     o_ref, table, cidx, widx, idx_sem = rest[count:]
     chunks = EPAD // CHUNK
@@ -107,8 +108,9 @@
     for k in range(chunks):
         for copy in index_copies(k):
             copy.start()
-    for i, part in enumerate(parts):
-        table[pl.ds(i * PART, PART), :] = part[...]
+    for part, slots in zip(parts, PLACES):
+        for i, slot in enumerate(slots):
+            table[pl.ds(slot * PART, PART), :] = part[pl.ds(i * PART, PART), :]
     size = (NQ - 1) * RA + 1
 
     for k in range(chunks):
@@ -157,7 +159,7 @@
     return pl.pallas_call(
         functools.partial(mixed_kernel, n_exc),
         out_shape=jax.ShapeDtypeStruct((PART, LANES), jnp.float32),
-        in_specs=[HBM, HBM, VMEM, VMEM] + [VMEM] * count,
+        in_specs=[HBM, HBM, VMEM, VMEM] + [VMEM] * len(parts),
         out_specs=VMEM,
         scratch_shapes=[
             pltpu.VMEM((count * PART, LANES), jnp.float32),
@@ -242,17 +244,11 @@
     again, over, after, before = lax.optimization_barrier((own, over, after, before))
     over_after, over_before = swap(after, "xl"), swap(before, "xl")
     two, over_two = shift(again, 2), shift(over, 2)
-    (start, after, before, over), over_after = lax.optimization_barrier(
-        ((again, after, before, over), over_after)
-    )
-    near = [start, after, two, before]
+    joined = swap(jnp.concatenate([again, after, before, over], axis=0), "c")
+    near = [again, after, two, before]
     across = [over, over_after, over_two, over_before]
-    parts = (
-        near
-        + [swap(v, "c") for v in near]
-        + across
-        + [swap(v, "c") for v in across]
-    )
+    late = [swap(v, "c") for v in (two, over_after, over_two, over_before)]
+    parts = near + across + late + [joined]
     mixed_local = mixed_call(
         cidx,
         widx,

time: 84.1 us -> 87.6 us (1.042)
  waiting for transfers between devices: 23.2 us -> 27.7 us
    ppermute x4, waiting for transfers between devices: 6.39 us -> 12.5 us  [shift(): lax.ppermute(value, 'grp', [(i, (i - k) % N_GRP) for i in range(N_GRP)])]
    ppermute x11 -> x8, waiting for transfers between devices: 4.21 us -> 2.5 us  [swap(): return lax.ppermute(value, axis, [(0, 1), (1, 0)])]
    ppermute x11 -> x8, starting transfers between devices: 5 us -> 4.75 us  [swap(): return lax.ppermute(value, axis, [(0, 1), (1, 0)])]
  transfers between devices with their start and end apart: 20 -> 17, of which waited for: 12 -> 9; matrix products, arithmetic and copies ran while one was open for 14% -> 13% of each run, Pallas kernels for 5% -> 5%
where the time goes in v8:
time: 87.6 us; the launch traced here: 87 us
  waiting for transfers between devices  27.7 us (32%)
  starting transfers between devices  27 us (31%)
  Pallas kernels  19.3 us (22%)
  matrix products  9.83 us (11%)
  local copies, waits for them, and re-layouts  1.53 us (2%)
  other arithmetic  1.49 us (2%)
    pallas_call x1, Pallas kernels, mixed_call(): pl.pallas_call(functools.partial(mixed_kernel, n_exc), out_shape=jax.Shap...  15.1 us
    ppermute x4, waiting for transfers between devices, shift(): lax.ppermute(value, 'grp', [(i, (i - k) % N_GRP) for i in range(N_GRP)])  12.5 us
    all_to_all x1, starting transfers between devices, per_device(): lax.all_to_all(packed, ('z', 'xh'), split_axis=0, concat_axis=0, tiled=True)  9.6 us
    dot_general x1, matrix products, per_device(): applied = jnp.einsum('rpk,pkl->rpl', picked, beta_blocks, precision=HIGH)  7.45 us
    all_to_all x1, waiting for transfers between devices, per_device(): lax.all_to_all(packed, ('z', 'xh'), split_axis=0, concat_axis=0, tiled=True)  7.14 us
    ppermute x4, starting transfers between devices, shift(): lax.ppermute(value, 'grp', [(i, (i - k) % N_GRP) for i in range(N_GRP)])  6.54 us
    all_to_all x1, waiting for transfers between devices, per_device(): lax.all_to_all(mixed_local.reshape(NQ, NT, RA, LANES), ('z', 'xh'), split...  5.62 us
    ppermute x8, starting transfers between devices, swap(): return lax.ppermute(value, axis, [(0, 1), (1, 0)])  4.75 us
  transfers between devices with their start and end apart: 17, of which 9 were waited for; matrix products, arithmetic and copies ran while one was open for 13% of the time, Pallas kernels for 5%

profile of v8, /device:TPU:2, one launch (start us, length us, event | category | flops | bytes accessed | tf_op | source)
XLA Modules:
  0.0 87.0 jit_solution(951160390800155683)
XLA Ops:
  0.0 0.0 copy-start
  0.0 0.0 collective-permute-start
  0.0 2.3 %collective-permute-start.1 = (s32[18,96]{1,0:T(8,128)}, s32[18,96]{1,0:T(8,128)S(1)}, u32[]{:S(2)}, u32[]{:S(2)}) collective-permute-start(s32[18,96]{1,0:T(8,128)} %param.18), channel_id=1, source_target_pairs={{0,2},{1,3},{2,0},{3,1},{4,6},{5,7},{6,4},{7,5},{8,10},{9,11},{10,... | collective-permute-start | bytes 20744 | tf_op jit(solution)/shard_map/ppermute | solution.py:216
  2.3 0.1 collective-permute-start.2
  2.4 1.7 %pack.1 = f32[16,4,8,128]{3,2,1,0:T(8,128)} custom-call(s32[1]{0:T(128)} %bitcast.g_ref, s32[1,4]{1,0:T(1,128)} %mask_ref.1, f32[8,6144]{1,0:T(8,128)} %x_ref.1, f32[1,4,8,8]{3,2,1,0:T(8,128)} %alpha_ref.1), custom_call_target="tpu_custom_call" | custom-call | tf_op jit(solution)/shard_map/pack/pallas_call | solution.py:44
  4.1 9.6 %all-to-all-start = ((f32[16,4,8,128]{3,2,1,0:T(8,128)}), f32[16,4,8,128]{3,2,1,0:T(8,128)S(1)}, u32[]{:S(2)}, u32[]{:S(2)}) async-start(f32[16,4,8,128]{3,2,1,0:T(8,128)} %pack.1), calls=%async_computation | async-start | bytes 524288 | tf_op jit(solution)/shard_map/all_to_all | solution.py:208
  13.8 0.8 slice_bitcast_fusion
  14.5 1.3 %convolution_bitcast_fusion.1 = f32[8,96,128]{2,1,0:T(8,128)S(1)} fusion(f32[8,48,128]{2,0,1:T(8,128)} %bitcast.62, s32[96]{0:T(128)S(1)} %get-tuple-element.32), kind=kOutput, calls=%fused_computation.1 | convolution fusion | flops 56627712 | bytes 590208 | tf_op jit(solution)/shard_map/rnk,pn->rpk/dot_general | solution.py:237
  15.8 0.6 pad_add_fusion.1.place_ref
  16.5 2.5 %prep.1 = (s32[96,128]{1,0:T(8,128)}, s32[96,128]{1,0:T(8,128)}) custom-call(s32[2]{0:T(128)} %pad_add_fusion.1.place_ref, s32[90,512]{1,0:T(8,128)} %src_ref.1, s32[90,512]{1,0:T(8,128)} %pair_ref.1, s32[90,512]{1,0:T(8,128)} %par_ref.1), custom_call_target="tpu_custom_call" | custom-call | tf_op jit(solution)/shard_map/prep/pallas_call | solution.py:82
  19.0 0.0 collective-permute-done
  19.0 0.0 collective-permute-done.1
  19.0 0.0 collective-permute-done.2
  19.0 0.7 pad_add_fusion
  19.7 0.8 fusion.24
  20.5 0.1 pad_maximum_fusion
  20.6 7.1 %all-to-all-done.mix_ref = f32[16,4,8,128]{3,2,1,0:T(8,128)S(1)} async-done(((f32[16,4,8,128]{3,2,1,0:T(8,128)}), f32[16,4,8,128]{3,2,1,0:T(8,128)S(1)}, u32[]{:S(2)}, u32[]{:S(2)}) %all-to-all-start) | async-done | bytes 262176 | tf_op jit(solution)/shard_map/all_to_all | solution.py:208
  27.7 1.5 %collective-permute-start.3 = (f32[384,128]{1,0:T(8,128)S(1)}, f32[384,128]{1,0:T(8,128)S(1)}, u32[]{:S(2)}, u32[]{:S(2)}) collective-permute-start(f32[384,128]{1,0:T(8,128)S(1)} %bitcast.55), channel_id=1, source_target_pairs={{0,2},{2,0},{1,3},{3,1},{4,6},{6,4},{5,7},{7,5},{8,10},{10,8},{9,1... | collective-permute-start | bytes 589832 | tf_op jit(solution)/shard_map/ppermute | solution.py:205
  29.3 3.0 %collective-permute-start.4 = (f32[384,128]{1,0:T(8,128)S(1)}, f32[384,128]{1,0:T(8,128)S(1)}, u32[]{:S(2)}, u32[]{:S(2)}) collective-permute-start(f32[384,128]{1,0:T(8,128)S(1)} %bitcast.56), channel_id=1, source_target_pairs={{0,192},{64,0},{128,64},{192,128},{1,193},{65,1},{129,65},{193,129... | collective-permute-start | bytes 589832 | tf_op jit(solution)/shard_map/ppermute | solution.py:200
  32.3 0.0 collective-permute-start.5
  32.3 1.3 %collective-permute-done.3.rest_4_ = f32[384,128]{1,0:T(8,128)S(1)} collective-permute-done((f32[384,128]{1,0:T(8,128)S(1)}, f32[384,128]{1,0:T(8,128)S(1)}, u32[]{:S(2)}, u32[]{:S(2)}) %collective-permute-start.3) | collective-permute-done | bytes 196640 | tf_op jit(solution)/shard_map/ppermute | solution.py:205
  33.6 1.9 %collective-permute-done.4.rest_1_ = f32[384,128]{1,0:T(8,128)S(1)} collective-permute-done((f32[384,128]{1,0:T(8,128)S(1)}, f32[384,128]{1,0:T(8,128)S(1)}, u32[]{:S(2)}, u32[]{:S(2)}) %collective-permute-start.4) | collective-permute-done | bytes 196640 | tf_op jit(solution)/shard_map/ppermute | solution.py:200
  35.5 3.7 %collective-permute-done.5.rest_3_ = f32[384,128]{1,0:T(8,128)S(1)} collective-permute-done((f32[384,128]{1,0:T(8,128)S(1)}, f32[384,128]{1,0:T(8,128)S(1)}, u32[]{:S(2)}, u32[]{:S(2)}) %collective-permute-start.5) | collective-permute-done | bytes 196640 | tf_op jit(solution)/shard_map/ppermute | solution.py:200
  39.2 0.1 pad_maximum_fusion.1
  39.2 0.1 collective-permute-start.14
  39.3 0.1 collective-permute-start.6
  39.4 0.7 collective-permute-start.7
  40.1 3.4 %collective-permute-start.8 = (f32[384,128]{1,0:T(8,128)S(1)}, f32[384,128]{1,0:T(8,128)S(1)}, u32[]{:S(2)}, u32[]{:S(2)}) collective-permute-start(f32[384,128]{1,0:T(8,128)S(1)} %collective-permute-done.3.rest_4_), channel_id=1, source_target_pairs={{0,128},{64,192},{128,0},{192,64},{1,129},{65,193},{129,1},{193,65... | collective-permute-start | bytes 589832 | tf_op jit(solution)/shard_map/ppermute | solution.py:200
  43.5 1.4 %collective-permute-start.9 = (f32[384,128]{1,0:T(8,128)S(1)}, f32[384,128]{1,0:T(8,128)S(1)}, u32[]{:S(2)}, u32[]{:S(2)}) collective-permute-start(f32[384,128]{1,0:T(8,128)S(1)} %collective-permute-done.5.rest_3_), channel_id=1, source_target_pairs={{0,2},{2,0},{1,3},{3,1},{4,6},{6,4},{5,7},{7,5},{8,10},{10,8},{9,1... | collective-permute-start | bytes 589832 | tf_op jit(solution)/shard_map/ppermute | solution.py:205
  45.0 3.7 %collective-permute-done.6.rest_2_ = f32[384,128]{1,0:T(8,128)S(1)} collective-permute-done((f32[384,128]{1,0:T(8,128)S(1)}, f32[384,128]{1,0:T(8,128)S(1)}, u32[]{:S(2)}, u32[]{:S(2)}) %collective-permute-start.6) | collective-permute-done | bytes 196640 | tf_op jit(solution)/shard_map/ppermute | solution.py:200
  48.6 0.0 collective-permute-start.10
  48.6 0.0 collective-permute-done.7.rest_5_
  48.6 0.5 collective-permute-start.11
  49.1 3.2 %collective-permute-done.8.rest_6_ = f32[384,128]{1,0:T(8,128)S(1)} collective-permute-done((f32[384,128]{1,0:T(8,128)S(1)}, f32[384,128]{1,0:T(8,128)S(1)}, u32[]{:S(2)}, u32[]{:S(2)}) %collective-permute-start.8) | collective-permute-done | bytes 196640 | tf_op jit(solution)/shard_map/ppermute | solution.py:200
  52.4 0.0 collective-permute-start.12
  52.4 0.0 collective-permute-done.9.rest_7_
  52.4 0.5 collective-permute-start.13
  52.9 0.0 collective-permute-done.10.rest_8_
  52.9 0.0 collective-permute-done.11.rest_9_
  52.9 0.9 %collective-permute-done.12.rest_10_ = f32[384,128]{1,0:T(8,128)S(1)} collective-permute-done((f32[384,128]{1,0:T(8,128)S(1)}, f32[384,128]{1,0:T(8,128)S(1)}, u32[]{:S(2)}, u32[]{:S(2)}) %collective-permute-start.12) | collective-permute-done | bytes 196640 | tf_op jit(solution)/shard_map/ppermute | solution.py:205
  53.8 0.3 collective-permute-done.13.rest_11_
  54.1 0.0 collective-permute-done.14.rest_12_
  54.1 15.1 %mixed.1 = f32[384,128]{1,0:T(8,128)} custom-call(s32[12288]{0:T(1024)} %bitcast.63, s32[12288]{0:T(1024)} %bitcast.64, f32[1944,128]{1,0:T(8,128)S(1)} %bitcast.54, f32[16,4,8,128]{3,2,1,0:T(8,128)S(1)} %all-to-all-done.mix_ref, f32[384,128]{1,0:T(8,128)S(1)} %bitcast.60, f32[384,128]{1,0:T(8,128)S(1)} %collective-permute-done.4.rest_1_, ...), custom_call_target="tpu_custom_call" | custom-call | flops 8847360 | bytes 8388608 | tf_op jit(solution)/shard_map/mixed/pallas_call | solution.py:159
  69.2 3.7 %all-to-all-start.1 = ((f32[16,3,8,128]{3,2,1,0:T(8,128)}), f32[16,3,8,128]{3,2,1,0:T(8,128)S(1)}, u32[]{:S(2)}, u32[]{:S(2)}) async-start(f32[16,3,8,128]{3,2,1,0:T(8,128)} %bitcast.21), calls=%async_computation.1 | async-start | bytes 393216 | tf_op jit(solution)/shard_map/all_to_all | solution.py:260
  72.9 7.5 %fusion.3 = f32[96,8,128]{2,1,0:T(8,128)S(1)} fusion(f32[96,128,128]{2,1,0:T(8,128)} %param.11, f32[8,96,128]{2,1,0:T(8,128)S(1)} %convolution_bitcast_fusion.1), kind=kOutput, calls=%fused_computation.7 | convolution fusion | flops 150994944 | bytes 7077888 | tf_op jit(solution)/shard_map/rpk,pkl->rpl/dot_general | solution.py:271
  80.4 5.6 %all-to-all-done.1 = f32[16,3,8,128]{3,2,1,0:T(8,128)S(1)} async-done(((f32[16,3,8,128]{3,2,1,0:T(8,128)}), f32[16,3,8,128]{3,2,1,0:T(8,128)S(1)}, u32[]{:S(2)}, u32[]{:S(2)}) %all-to-all-start.1) | async-done | bytes 196640 | tf_op jit(solution)/shard_map/all_to_all | solution.py:260
  86.0 0.3 fusion.5
  86.3 0.7 copy.32
  (3 shorter events, 0.0 us)
Async XLA Ops:
  0.0 19.7 %copy-start = (f32[324,18]{0,1:T(8,128)S(1)}, f32[324,18]{0,1:T(8,128)}, u32[]{:S(2)}) copy-start(f32[324,18]{0,1:T(8,128)} %param.19) | copy-start | bytes 69988
  0.0 19.0 %collective-permute-start = (s32[18,96]{1,0:T(8,128)}, s32[18,96]{1,0:T(8,128)S(1)}, u32[]{:S(2)}, u32[]{:S(2)}) collective-permute-start(s32[18,96]{1,0:T(8,128)} %param.18), channel_id=1, source_target_pairs={{0,1},{1,0},{2,3},{3,2},{4,5},{5,4},{6,7},{7,6},{8,9},{9,8},{10,11... | collective-permute-start | bytes 20744 | tf_op jit(solution)/shard_map/ppermute | solution.py:216
  0.0 19.0 %collective-permute-start.1 = (s32[18,96]{1,0:T(8,128)}, s32[18,96]{1,0:T(8,128)S(1)}, u32[]{:S(2)}, u32[]{:S(2)}) collective-permute-start(s32[18,96]{1,0:T(8,128)} %param.18), channel_id=1, source_target_pairs={{0,2},{1,3},{2,0},{3,1},{4,6},{5,7},{6,4},{7,5},{8,10},{9,11},{10,... | collective-permute-start | bytes 20744 | tf_op jit(solution)/shard_map/ppermute | solution.py:216
  2.3 16.7 %collective-permute-start.2 = (s32[18,96]{1,0:T(8,128)}, s32[18,96]{1,0:T(8,128)S(1)}, u32[]{:S(2)}, u32[]{:S(2)}) collective-permute-start(s32[18,96]{1,0:T(8,128)} %param.18), channel_id=1, source_target_pairs={{0,3},{1,2},{2,1},{3,0},{4,7},{5,6},{6,5},{7,4},{8,11},{9,10},{10,... | collective-permute-start | bytes 20744 | tf_op jit(solution)/shard_map/ppermute | solution.py:216
  4.1 23.6 %all-to-all-start = ((f32[16,4,8,128]{3,2,1,0:T(8,128)}), f32[16,4,8,128]{3,2,1,0:T(8,128)S(1)}, u32[]{:S(2)}, u32[]{:S(2)}) async-start(f32[16,4,8,128]{3,2,1,0:T(8,128)} %pack.1), calls=%async_computation | async-start | bytes 524288 | tf_op jit(solution)/shard_map/all_to_all | solution.py:208
  27.7 5.8 %collective-permute-start.3 = (f32[384,128]{1,0:T(8,128)S(1)}, f32[384,128]{1,0:T(8,128)S(1)}, u32[]{:S(2)}, u32[]{:S(2)}) collective-permute-start(f32[384,128]{1,0:T(8,128)S(1)} %bitcast.55), channel_id=1, source_target_pairs={{0,2},{2,0},{1,3},{3,1},{4,6},{6,4},{5,7},{7,5},{8,10},{10,8},{9,1... | collective-permute-start | bytes 589832 | tf_op jit(solution)/shard_map/ppermute | solution.py:205
  29.3 6.2 %collective-permute-start.4 = (f32[384,128]{1,0:T(8,128)S(1)}, f32[384,128]{1,0:T(8,128)S(1)}, u32[]{:S(2)}, u32[]{:S(2)}) collective-permute-start(f32[384,128]{1,0:T(8,128)S(1)} %bitcast.56), channel_id=1, source_target_pairs={{0,192},{64,0},{128,64},{192,128},{1,193},{65,1},{129,65},{193,129... | collective-permute-start | bytes 589832 | tf_op jit(solution)/shard_map/ppermute | solution.py:200
  32.3 6.9 %collective-permute-start.5 = (f32[384,128]{1,0:T(8,128)S(1)}, f32[384,128]{1,0:T(8,128)S(1)}, u32[]{:S(2)}, u32[]{:S(2)}) collective-permute-start(f32[384,128]{1,0:T(8,128)S(1)} %bitcast.57), channel_id=1, source_target_pairs={{0,64},{64,128},{128,192},{192,0},{1,65},{65,129},{129,193},{193,1... | collective-permute-start | bytes 589832 | tf_op jit(solution)/shard_map/ppermute | solution.py:200
  39.2 14.9 %collective-permute-start.14 = (f32[1536,128]{1,0:T(8,128)S(1)}, f32[1536,128]{1,0:T(8,128)S(1)}, u32[]{:S(2)}, u32[]{:S(2)}) collective-permute-start(f32[1536,128]{1,0:T(8,128)S(1)} %pad_maximum_fusion.1), channel_id=1, source_target_pairs={{0,1},{1,0},{2,3},{3,2},{4,5},{5,4},{6,7},{7,6},{8,9},{9,8},{10,11... | collective-permute-start | bytes 2359304 | tf_op jit(solution)/shard_map/ppermute | solution.py:205
  39.3 9.3 %collective-permute-start.6 = (f32[384,128]{1,0:T(8,128)S(1)}, f32[384,128]{1,0:T(8,128)S(1)}, u32[]{:S(2)}, u32[]{:S(2)}) collective-permute-start(f32[384,128]{1,0:T(8,128)S(1)} %bitcast.59), channel_id=1, source_target_pairs={{0,128},{64,192},{128,0},{192,64},{1,129},{65,193},{129,1},{193,65... | collective-permute-start | bytes 589832 | tf_op jit(solution)/shard_map/ppermute | solution.py:200
  39.4 9.2 %collective-permute-start.7 = (f32[384,128]{1,0:T(8,128)S(1)}, f32[384,128]{1,0:T(8,128)S(1)}, u32[]{:S(2)}, u32[]{:S(2)}) collective-permute-start(f32[384,128]{1,0:T(8,128)S(1)} %collective-permute-done.4.rest_1_), channel_id=1, source_target_pairs={{0,2},{2,0},{1,3},{3,1},{4,6},{6,4},{5,7},{7,5},{8,10},{10,8},{9,1... | collective-permute-start | bytes 589832 | tf_op jit(solution)/shard_map/ppermute | solution.py:205
  40.1 12.3 %collective-permute-start.8 = (f32[384,128]{1,0:T(8,128)S(1)}, f32[384,128]{1,0:T(8,128)S(1)}, u32[]{:S(2)}, u32[]{:S(2)}) collective-permute-start(f32[384,128]{1,0:T(8,128)S(1)} %collective-permute-done.3.rest_4_), channel_id=1, source_target_pairs={{0,128},{64,192},{128,0},{192,64},{1,129},{65,193},{129,1},{193,65... | collective-permute-start | bytes 589832 | tf_op jit(solution)/shard_map/ppermute | solution.py:200
  43.5 8.8 %collective-permute-start.9 = (f32[384,128]{1,0:T(8,128)S(1)}, f32[384,128]{1,0:T(8,128)S(1)}, u32[]{:S(2)}, u32[]{:S(2)}) collective-permute-start(f32[384,128]{1,0:T(8,128)S(1)} %collective-permute-done.5.rest_3_), channel_id=1, source_target_pairs={{0,2},{2,0},{1,3},{3,1},{4,6},{6,4},{5,7},{7,5},{8,10},{10,8},{9,1... | collective-permute-start | bytes 589832 | tf_op jit(solution)/shard_map/ppermute | solution.py:205
  48.6 4.3 %collective-permute-start.10 = (f32[384,128]{1,0:T(8,128)S(1)}, f32[384,128]{1,0:T(8,128)S(1)}, u32[]{:S(2)}, u32[]{:S(2)}) collective-permute-start(f32[384,128]{1,0:T(8,128)S(1)} %collective-permute-done.6.rest_2_), channel_id=1, source_target_pairs={{0,1},{1,0},{2,3},{3,2},{4,5},{5,4},{6,7},{7,6},{8,9},{9,8},{10,11... | collective-permute-start | bytes 589832 | tf_op jit(solution)/shard_map/ppermute | solution.py:205
  48.6 4.3 %collective-permute-start.11 = (f32[384,128]{1,0:T(8,128)S(1)}, f32[384,128]{1,0:T(8,128)S(1)}, u32[]{:S(2)}, u32[]{:S(2)}) collective-permute-start(f32[384,128]{1,0:T(8,128)S(1)} %collective-permute-done.7.rest_5_), channel_id=1, source_target_pairs={{0,1},{1,0},{2,3},{3,2},{4,5},{5,4},{6,7},{7,6},{8,9},{9,8},{10,11... | collective-permute-start | bytes 589832 | tf_op jit(solution)/shard_map/ppermute | solution.py:205
  52.4 1.4 %collective-permute-start.12 = (f32[384,128]{1,0:T(8,128)S(1)}, f32[384,128]{1,0:T(8,128)S(1)}, u32[]{:S(2)}, u32[]{:S(2)}) collective-permute-start(f32[384,128]{1,0:T(8,128)S(1)} %collective-permute-done.8.rest_6_), channel_id=1, source_target_pairs={{0,1},{1,0},{2,3},{3,2},{4,5},{5,4},{6,7},{7,6},{8,9},{9,8},{10,11... | collective-permute-start | bytes 589832 | tf_op jit(solution)/shard_map/ppermute | solution.py:205
  52.4 1.7 %collective-permute-start.13 = (f32[384,128]{1,0:T(8,128)S(1)}, f32[384,128]{1,0:T(8,128)S(1)}, u32[]{:S(2)}, u32[]{:S(2)}) collective-permute-start(f32[384,128]{1,0:T(8,128)S(1)} %collective-permute-done.9.rest_7_), channel_id=1, source_target_pairs={{0,1},{1,0},{2,3},{3,2},{4,5},{5,4},{6,7},{7,6},{8,9},{9,8},{10,11... | collective-permute-start | bytes 589832 | tf_op jit(solution)/shard_map/ppermute | solution.py:205
  69.2 16.8 %all-to-all-start.1 = ((f32[16,3,8,128]{3,2,1,0:T(8,128)}), f32[16,3,8,128]{3,2,1,0:T(8,128)S(1)}, u32[]{:S(2)}, u32[]{:S(2)}) async-start(f32[16,3,8,128]{3,2,1,0:T(8,128)} %bitcast.21), calls=%async_computation.1 | async-start | bytes 393216 | tf_op jit(solution)/shard_map/all_to_all | solution.py:260

commit v9 on v6

--- a/solution.py
+++ b/solution.py
@@ -175,6 +175,22 @@
     )(cidx, widx, wtab, mix, *parts)
 
 
+def weights_table(pieces, coulomb, sel):
+    n_pair = coulomb.shape[0]
+    pieces = jnp.stack(pieces)
+    ordered = [
+        lax.dynamic_index_in_dim(pieces, sel ^ k, 0, keepdims=False) for k in range(NS)
+    ]
+    occ = jnp.concatenate(ordered, axis=1).astype(jnp.float32)
+    weights = jnp.dot(coulomb, occ, precision=HIGH, preferred_element_type=jnp.float32)
+    signed = jnp.concatenate([weights, -weights], axis=0)
+    return (
+        signed.reshape(2 * n_pair // RA, RA, NT, LANES)
+        .transpose(0, 2, 1, 3)
+        .reshape(2 * n_pair * NT, LANES)
+    )
+
+
 def per_device(
     coeff,
     beta_blocks,
@@ -210,40 +226,30 @@
     sel = xl * NC + c
     place = jnp.stack([g, sel]).astype(jnp.int32)
     cidx, widx = prep_call(place, exc_source, exc_pair, exc_parity, n_pair)
-    pieces = [
-        lax.ppermute(occupation, ("xl", "c"), [(i, i ^ k) for i in range(NS)])
-        for k in range(1, NS)
-    ]
-    pieces = jnp.stack([occupation] + pieces)
-    ordered = [
-        lax.dynamic_index_in_dim(pieces, sel ^ k, 0, keepdims=False) for k in range(NS)
-    ]
-    occ = jnp.concatenate(ordered, axis=1).astype(jnp.float32)
-    weights = jnp.dot(coulomb, occ, precision=HIGH, preferred_element_type=jnp.float32)
-    signed = jnp.concatenate([weights, -weights], axis=0)
-    wtab = (
-        signed.reshape(2 * n_pair // RA, RA, NT, LANES)
-        .transpose(0, 2, 1, 3)
-        .reshape(2 * n_pair * NT, LANES)
-    )
-
     block_size = beta_blocks.shape[1]
     block_count = beta_width // block_size
     blocked = coeff.reshape(alpha_rows, block_count, block_size)
     block_ids = jnp.arange(block_count, dtype=jnp.int32)
     choosing = (block_list[0][:, None] == block_ids[None, :]).astype(jnp.float32)
     picked = jnp.einsum("rnk,pn->rpk", blocked, choosing, precision=HIGH)
-    arrived, wtab, cidx, widx, picked = lax.optimization_barrier(
-        (arrived, wtab, cidx, widx, picked)
+    arrived, cidx, widx, picked, occupation = lax.optimization_barrier(
+        (arrived, cidx, widx, picked, occupation)
     )
     own = arrived[:, :NT].reshape(PART, LANES)
     after, before = shift(own, 1), shift(own, N_GRP - 1)
     over = swap(own, "xl")
-    again, over, after, before = lax.optimization_barrier((own, over, after, before))
+    pieces = [occupation] + [
+        lax.ppermute(occupation, ("xl", "c"), [(i, i ^ k) for i in range(NS)])
+        for k in range(1, NS)
+    ]
+    again, over, after, before, pieces = lax.optimization_barrier(
+        (own, over, after, before, pieces)
+    )
     over_after, over_before = swap(after, "xl"), swap(before, "xl")
     two, over_two = shift(again, 2), shift(over, 2)
-    (start, after, before, over), over_after = lax.optimization_barrier(
-        ((again, after, before, over), over_after)
+    wtab = weights_table(pieces, coulomb, sel)
+    (start, after, before, over), over_after, wtab = lax.optimization_barrier(
+        ((again, after, before, over), over_after, wtab)
     )
     near = [start, after, two, before]
     across = [over, over_after, over_two, over_before]

time: 84.1 us -> 87.1 us (1.036)
  waiting for transfers between devices: 23.2 us -> 26.3 us
    ppermute x3, waiting for transfers between devices: 0.01 us -> 4 us  [per_device(): lax.ppermute(occupation, ('xl', 'c'), [(i, i ^ k) for i in range(NS)])]
    ppermute x4, waiting for transfers between devices: 6.39 us -> 2.95 us  [shift(): lax.ppermute(value, 'grp', [(i, (i - k) % N_GRP) for i in range(N_GRP)])]
    all_to_all x1, waiting for transfers between devices: 6.8 us -> 8.41 us  [per_device(): lax.all_to_all(packed, ('z', 'xh'), split_axis=0, concat_axis=0, tiled=True)]
    ppermute x11, waiting for transfers between devices: 4.21 us -> 5.12 us  [swap(): return lax.ppermute(value, axis, [(0, 1), (1, 0)])]
  transfers between devices with their start and end apart: 20 -> 20, of which waited for: 12 -> 12; matrix products, arithmetic and copies ran while one was open for 14% -> 14% of each run, Pallas kernels for 5% -> 3%
where the time goes in v9:
time: 87.1 us; the launch traced here: 86.1 us
  starting transfers between devices  27.6 us (32%)
  waiting for transfers between devices  26.3 us (30%)
  Pallas kernels  19.4 us (22%)
  matrix products  9.83 us (11%)
  local copies, waits for them, and re-layouts  1.53 us (2%)
  other arithmetic  1.34 us (2%)
    pallas_call x1, Pallas kernels, mixed_call(): pl.pallas_call(functools.partial(mixed_kernel, n_exc), out_shape=jax.Shap...  15.2 us
    all_to_all x1, starting transfers between devices, per_device(): lax.all_to_all(packed, ('z', 'xh'), split_axis=0, concat_axis=0, tiled=True)  10.1 us
    all_to_all x1, waiting for transfers between devices, per_device(): lax.all_to_all(packed, ('z', 'xh'), split_axis=0, concat_axis=0, tiled=True)  8.41 us
    dot_general x1, matrix products, per_device(): applied = jnp.einsum('rpk,pkl->rpl', picked, beta_blocks, precision=HIGH)  7.45 us
    ppermute x4, starting transfers between devices, shift(): lax.ppermute(value, 'grp', [(i, (i - k) % N_GRP) for i in range(N_GRP)])  6.93 us
    all_to_all x1, waiting for transfers between devices, per_device(): lax.all_to_all(mixed_local.reshape(NQ, NT, RA, LANES), ('z', 'xh'), split...  5.8 us
    ppermute x11, starting transfers between devices, swap(): return lax.ppermute(value, axis, [(0, 1), (1, 0)])  5.35 us
    ppermute x11, waiting for transfers between devices, swap(): return lax.ppermute(value, axis, [(0, 1), (1, 0)])  5.12 us
  transfers between devices with their start and end apart: 20, of which 12 were waited for; matrix products, arithmetic and copies ran while one was open for 14% of the time, Pallas kernels for 3%

profile of v9, /device:TPU:2, one launch (start us, length us, event | category | flops | bytes accessed | tf_op | source)
XLA Modules:
  0.0 86.1 jit_solution(11111898561732683079)
XLA Ops:
  0.0 1.7 %pack.1 = f32[16,4,8,128]{3,2,1,0:T(8,128)} custom-call(s32[1]{0:T(128)} %bitcast.g_ref, s32[1,4]{1,0:T(1,128)} %mask_ref.1, f32[8,6144]{1,0:T(8,128)} %x_ref.1, f32[1,4,8,8]{3,2,1,0:T(8,128)} %alpha_ref.1), custom_call_target="tpu_custom_call" | custom-call | tf_op jit(solution)/shard_map/pack/pallas_call | solution.py:43
  1.7 10.1 %all-to-all-start = ((f32[16,4,8,128]{3,2,1,0:T(8,128)}), f32[16,4,8,128]{3,2,1,0:T(8,128)S(1)}, u32[]{:S(2)}, u32[]{:S(2)}) async-start(f32[16,4,8,128]{3,2,1,0:T(8,128)} %pack.1), calls=%async_computation | async-start | bytes 524288 | tf_op jit(solution)/shard_map/all_to_all | solution.py:222
  11.9 0.6 pad_add_fusion.1.place_ref
  12.4 2.5 %prep.1 = (s32[96,128]{1,0:T(8,128)}, s32[96,128]{1,0:T(8,128)}) custom-call(s32[2]{0:T(128)} %pad_add_fusion.1.place_ref, s32[90,512]{1,0:T(8,128)} %src_ref.1, s32[90,512]{1,0:T(8,128)} %pair_ref.1, s32[90,512]{1,0:T(8,128)} %par_ref.1), custom_call_target="tpu_custom_call" | custom-call | tf_op jit(solution)/shard_map/prep/pallas_call | solution.py:81
  15.0 0.8 slice_bitcast_fusion
  15.7 1.3 %convolution_bitcast_fusion.1 = f32[8,96,128]{2,1,0:T(8,128)S(1)} fusion(f32[8,48,128]{2,0,1:T(8,128)} %bitcast.62, s32[96]{0:T(128)S(1)} %get-tuple-element.52), kind=kOutput, calls=%fused_computation.1 | convolution fusion | flops 56627712 | bytes 590208 | tf_op jit(solution)/shard_map/rnk,pn->rpk/dot_general | solution.py:234
  17.0 8.4 %all-to-all-done.mix_ref = f32[16,4,8,128]{3,2,1,0:T(8,128)S(1)} async-done(((f32[16,4,8,128]{3,2,1,0:T(8,128)}), f32[16,4,8,128]{3,2,1,0:T(8,128)S(1)}, u32[]{:S(2)}, u32[]{:S(2)}) %all-to-all-start) | async-done | bytes 262176 | tf_op jit(solution)/shard_map/all_to_all | solution.py:222
  25.4 1.7 %collective-permute-start.2 = (f32[384,128]{1,0:T(8,128)S(1)}, f32[384,128]{1,0:T(8,128)S(1)}, u32[]{:S(2)}, u32[]{:S(2)}) collective-permute-start(f32[384,128]{1,0:T(8,128)S(1)} %bitcast.55), channel_id=1, source_target_pairs={{0,64},{64,128},{128,192},{192,0},{1,65},{65,129},{129,193},{193,1... | collective-permute-start | bytes 589832 | tf_op jit(solution)/shard_map/ppermute | solution.py:214
  27.1 1.7 %collective-permute-start.1 = (f32[384,128]{1,0:T(8,128)S(1)}, f32[384,128]{1,0:T(8,128)S(1)}, u32[]{:S(2)}, u32[]{:S(2)}) collective-permute-start(f32[384,128]{1,0:T(8,128)S(1)} %bitcast.56), channel_id=1, source_target_pairs={{0,192},{64,0},{128,64},{192,128},{1,193},{65,1},{129,65},{193,129... | collective-permute-start | bytes 589832 | tf_op jit(solution)/shard_map/ppermute | solution.py:214
  28.8 1.4 %collective-permute-start = (f32[384,128]{1,0:T(8,128)S(1)}, f32[384,128]{1,0:T(8,128)S(1)}, u32[]{:S(2)}, u32[]{:S(2)}) collective-permute-start(f32[384,128]{1,0:T(8,128)S(1)} %bitcast.57), channel_id=1, source_target_pairs={{0,2},{2,0},{1,3},{3,1},{4,6},{6,4},{5,7},{7,5},{8,10},{10,8},{9,1... | collective-permute-start | bytes 589832 | tf_op jit(solution)/shard_map/ppermute | solution.py:219
  30.2 0.0 collective-permute-start.5
  30.2 0.6 collective-permute-start.4
  30.8 3.0 %collective-permute-done.5 = s32[18,96]{1,0:T(8,128)S(1)} collective-permute-done((s32[18,96]{1,0:T(8,128)}, s32[18,96]{1,0:T(8,128)S(1)}, u32[]{:S(2)}, u32[]{:S(2)}) %collective-permute-start.5) | collective-permute-done | bytes 6944 | tf_op jit(solution)/shard_map/ppermute | solution.py:242
  33.8 1.0 %collective-permute-start.3 = (s32[18,96]{1,0:T(8,128)}, s32[18,96]{1,0:T(8,128)S(1)}, u32[]{:S(2)}, u32[]{:S(2)}) collective-permute-start(s32[18,96]{1,0:T(8,128)} %param.18), channel_id=1, source_target_pairs={{0,1},{1,0},{2,3},{3,2},{4,5},{5,4},{6,7},{7,6},{8,9},{9,8},{10,11... | collective-permute-start | bytes 20744 | tf_op jit(solution)/shard_map/ppermute | solution.py:242
  34.8 0.1 collective-permute-done.4
  35.0 0.9 %collective-permute-done.3 = s32[18,96]{1,0:T(8,128)S(1)} collective-permute-done((s32[18,96]{1,0:T(8,128)}, s32[18,96]{1,0:T(8,128)S(1)}, u32[]{:S(2)}, u32[]{:S(2)}) %collective-permute-start.3) | collective-permute-done | bytes 6944 | tf_op jit(solution)/shard_map/ppermute | solution.py:242
  35.9 0.0 collective-permute-done.2.rest_3_
  35.9 0.0 collective-permute-done.1.rest_1_
  35.9 0.0 collective-permute-done.rest_8_
  35.9 2.1 %collective-permute-start.7 = (f32[384,128]{1,0:T(8,128)S(1)}, f32[384,128]{1,0:T(8,128)S(1)}, u32[]{:S(2)}, u32[]{:S(2)}) collective-permute-start(f32[384,128]{1,0:T(8,128)S(1)} %bitcast.58), channel_id=1, source_target_pairs={{0,128},{64,192},{128,0},{192,64},{1,129},{65,193},{129,1},{193,65... | collective-permute-start | bytes 589832 | tf_op jit(solution)/shard_map/ppermute | solution.py:214
  37.9 1.4 %collective-permute-start.6 = (f32[384,128]{1,0:T(8,128)S(1)}, f32[384,128]{1,0:T(8,128)S(1)}, u32[]{:S(2)}, u32[]{:S(2)}) collective-permute-start(f32[384,128]{1,0:T(8,128)S(1)} %collective-permute-done.1.rest_1_), channel_id=1, source_target_pairs={{0,2},{2,0},{1,3},{3,1},{4,6},{6,4},{5,7},{7,5},{8,10},{10,8},{9,1... | collective-permute-start | bytes 589832 | tf_op jit(solution)/shard_map/ppermute | solution.py:219
  39.4 0.6 collective-permute-start.13
  40.0 1.5 %collective-permute-start.12 = (f32[384,128]{1,0:T(8,128)S(1)}, f32[384,128]{1,0:T(8,128)S(1)}, u32[]{:S(2)}, u32[]{:S(2)}) collective-permute-start(f32[384,128]{1,0:T(8,128)S(1)} %collective-permute-done.rest_8_), channel_id=1, source_target_pairs={{0,128},{64,192},{128,0},{192,64},{1,129},{65,193},{129,1},{193,65... | collective-permute-start | bytes 589832 | tf_op jit(solution)/shard_map/ppermute | solution.py:214
  41.5 0.7 pad_add_fusion
  42.2 2.9 %collective-permute-done.7.rest_2_ = f32[384,128]{1,0:T(8,128)S(1)} collective-permute-done((f32[384,128]{1,0:T(8,128)S(1)}, f32[384,128]{1,0:T(8,128)S(1)}, u32[]{:S(2)}, u32[]{:S(2)}) %collective-permute-start.7) | collective-permute-done | bytes 196640 | tf_op jit(solution)/shard_map/ppermute | solution.py:214
  45.2 3.8 %collective-permute-done.13.rest_11_ = f32[384,128]{1,0:T(8,128)S(1)} collective-permute-done((f32[384,128]{1,0:T(8,128)S(1)}, f32[384,128]{1,0:T(8,128)S(1)}, u32[]{:S(2)}, u32[]{:S(2)}) %collective-permute-start.13) | collective-permute-done | bytes 196640 | tf_op jit(solution)/shard_map/ppermute | solution.py:219
  49.0 0.5 collective-permute-start.16
  49.5 0.8 fusion.24
  50.3 0.1 pad_maximum_fusion
  50.4 0.0 collective-permute-done.6.rest_9_
  50.4 0.1 collective-permute-start.8
  50.5 0.5 collective-permute-start.9
  51.0 0.0 collective-permute-done.10.rest_6_
  51.0 0.1 collective-permute-start.11
  51.1 0.4 collective-permute-start.14
  51.5 0.0 collective-permute-done.16.rest_14_
  51.5 0.3 collective-permute-start.15
  51.8 0.1 collective-permute-done.8.rest_4_
  51.9 0.3 collective-permute-done.9.rest_5_
  52.2 0.3 collective-permute-done.11.rest_7_
  52.5 0.3 collective-permute-done.14.rest_12_
  52.8 0.3 collective-permute-done.15.rest_13_
  53.1 15.2 %mixed.1 = f32[384,128]{1,0:T(8,128)} custom-call(s32[12288]{0:T(1024)} %bitcast.63, s32[12288]{0:T(1024)} %bitcast.64, f32[1944,128]{1,0:T(8,128)S(1)} %bitcast.54, f32[16,4,8,128]{3,2,1,0:T(8,128)S(1)} %all-to-all-done.mix_ref, f32[384,128]{1,0:T(8,128)S(1)} %bitcast.60, f32[384,128]{1,0:T(8,128)S(1)} %collective-permute-done.1.rest_1_, ...), custom_call_target="tpu_custom_call" | custom-call | flops 8847360 | bytes 8388608 | tf_op jit(solution)/shard_map/mixed/pallas_call | solution.py:157
  68.3 3.5 %all-to-all-start.1 = ((f32[16,3,8,128]{3,2,1,0:T(8,128)}), f32[16,3,8,128]{3,2,1,0:T(8,128)S(1)}, u32[]{:S(2)}, u32[]{:S(2)}) async-start(f32[16,3,8,128]{3,2,1,0:T(8,128)} %bitcast.21), calls=%async_computation.1 | async-start | bytes 393216 | tf_op jit(solution)/shard_map/all_to_all | solution.py:270
  71.8 7.5 %fusion.3 = f32[96,8,128]{2,1,0:T(8,128)S(1)} fusion(f32[96,128,128]{2,1,0:T(8,128)} %param.11, f32[8,96,128]{2,1,0:T(8,128)S(1)} %convolution_bitcast_fusion.1), kind=kOutput, calls=%fused_computation.6 | convolution fusion | flops 150994944 | bytes 7077888 | tf_op jit(solution)/shard_map/rpk,pkl->rpl/dot_general | solution.py:281
  79.3 5.8 %all-to-all-done.1 = f32[16,3,8,128]{3,2,1,0:T(8,128)S(1)} async-done(((f32[16,3,8,128]{3,2,1,0:T(8,128)}), f32[16,3,8,128]{3,2,1,0:T(8,128)S(1)}, u32[]{:S(2)}, u32[]{:S(2)}) %all-to-all-start.1) | async-done | bytes 196640 | tf_op jit(solution)/shard_map/all_to_all | solution.py:270
  85.1 0.3 fusion.5
  85.4 0.7 copy.32
  (8 shorter events, 0.0 us)
Async XLA Ops:
  0.0 49.5 %copy-start = (f32[324,18]{0,1:T(8,128)S(1)}, f32[324,18]{0,1:T(8,128)}, u32[]{:S(2)}) copy-start(f32[324,18]{0,1:T(8,128)} %param.19) | copy-start | bytes 69988
  1.7 23.7 %all-to-all-start = ((f32[16,4,8,128]{3,2,1,0:T(8,128)}), f32[16,4,8,128]{3,2,1,0:T(8,128)S(1)}, u32[]{:S(2)}, u32[]{:S(2)}) async-start(f32[16,4,8,128]{3,2,1,0:T(8,128)} %pack.1), calls=%async_computation | async-start | bytes 524288 | tf_op jit(solution)/shard_map/all_to_all | solution.py:222
  25.4 10.4 %collective-permute-start.2 = (f32[384,128]{1,0:T(8,128)S(1)}, f32[384,128]{1,0:T(8,128)S(1)}, u32[]{:S(2)}, u32[]{:S(2)}) collective-permute-start(f32[384,128]{1,0:T(8,128)S(1)} %bitcast.55), channel_id=1, source_target_pairs={{0,64},{64,128},{128,192},{192,0},{1,65},{65,129},{129,193},{193,1... | collective-permute-start | bytes 589832 | tf_op jit(solution)/shard_map/ppermute | solution.py:214
  27.1 8.8 %collective-permute-start.1 = (f32[384,128]{1,0:T(8,128)S(1)}, f32[384,128]{1,0:T(8,128)S(1)}, u32[]{:S(2)}, u32[]{:S(2)}) collective-permute-start(f32[384,128]{1,0:T(8,128)S(1)} %bitcast.56), channel_id=1, source_target_pairs={{0,192},{64,0},{128,64},{192,128},{1,193},{65,1},{129,65},{193,129... | collective-permute-start | bytes 589832 | tf_op jit(solution)/shard_map/ppermute | solution.py:214
  28.8 7.1 %collective-permute-start = (f32[384,128]{1,0:T(8,128)S(1)}, f32[384,128]{1,0:T(8,128)S(1)}, u32[]{:S(2)}, u32[]{:S(2)}) collective-permute-start(f32[384,128]{1,0:T(8,128)S(1)} %bitcast.57), channel_id=1, source_target_pairs={{0,2},{2,0},{1,3},{3,1},{4,6},{6,4},{5,7},{7,5},{8,10},{10,8},{9,1... | collective-permute-start | bytes 589832 | tf_op jit(solution)/shard_map/ppermute | solution.py:219
  30.2 3.6 %collective-permute-start.5 = (s32[18,96]{1,0:T(8,128)}, s32[18,96]{1,0:T(8,128)S(1)}, u32[]{:S(2)}, u32[]{:S(2)}) collective-permute-start(s32[18,96]{1,0:T(8,128)} %param.18), channel_id=1, source_target_pairs={{0,3},{1,2},{2,1},{3,0},{4,7},{5,6},{6,5},{7,4},{8,11},{9,10},{10,... | collective-permute-start | bytes 20744 | tf_op jit(solution)/shard_map/ppermute | solution.py:242
  30.2 4.8 %collective-permute-start.4 = (s32[18,96]{1,0:T(8,128)}, s32[18,96]{1,0:T(8,128)S(1)}, u32[]{:S(2)}, u32[]{:S(2)}) collective-permute-start(s32[18,96]{1,0:T(8,128)} %param.18), channel_id=1, source_target_pairs={{0,2},{1,3},{2,0},{3,1},{4,6},{5,7},{6,4},{7,5},{8,10},{9,11},{10,... | collective-permute-start | bytes 20744 | tf_op jit(solution)/shard_map/ppermute | solution.py:242
  33.8 2.1 %collective-permute-start.3 = (s32[18,96]{1,0:T(8,128)}, s32[18,96]{1,0:T(8,128)S(1)}, u32[]{:S(2)}, u32[]{:S(2)}) collective-permute-start(s32[18,96]{1,0:T(8,128)} %param.18), channel_id=1, source_target_pairs={{0,1},{1,0},{2,3},{3,2},{4,5},{5,4},{6,7},{7,6},{8,9},{9,8},{10,11... | collective-permute-start | bytes 20744 | tf_op jit(solution)/shard_map/ppermute | solution.py:242
  35.9 9.3 %collective-permute-start.7 = (f32[384,128]{1,0:T(8,128)S(1)}, f32[384,128]{1,0:T(8,128)S(1)}, u32[]{:S(2)}, u32[]{:S(2)}) collective-permute-start(f32[384,128]{1,0:T(8,128)S(1)} %bitcast.58), channel_id=1, source_target_pairs={{0,128},{64,192},{128,0},{192,64},{1,129},{65,193},{129,1},{193,65... | collective-permute-start | bytes 589832 | tf_op jit(solution)/shard_map/ppermute | solution.py:214
  37.9 12.5 %collective-permute-start.6 = (f32[384,128]{1,0:T(8,128)S(1)}, f32[384,128]{1,0:T(8,128)S(1)}, u32[]{:S(2)}, u32[]{:S(2)}) collective-permute-start(f32[384,128]{1,0:T(8,128)S(1)} %collective-permute-done.1.rest_1_), channel_id=1, source_target_pairs={{0,2},{2,0},{1,3},{3,1},{4,6},{6,4},{5,7},{7,5},{8,10},{10,8},{9,1... | collective-permute-start | bytes 589832 | tf_op jit(solution)/shard_map/ppermute | solution.py:219
  39.4 9.6 %collective-permute-start.13 = (f32[384,128]{1,0:T(8,128)S(1)}, f32[384,128]{1,0:T(8,128)S(1)}, u32[]{:S(2)}, u32[]{:S(2)}) collective-permute-start(f32[384,128]{1,0:T(8,128)S(1)} %collective-permute-done.2.rest_3_), channel_id=1, source_target_pairs={{0,2},{2,0},{1,3},{3,1},{4,6},{6,4},{5,7},{7,5},{8,10},{10,8},{9,1... | collective-permute-start | bytes 589832 | tf_op jit(solution)/shard_map/ppermute | solution.py:219
  40.0 9.1 %collective-permute-start.12 = (f32[384,128]{1,0:T(8,128)S(1)}, f32[384,128]{1,0:T(8,128)S(1)}, u32[]{:S(2)}, u32[]{:S(2)}) collective-permute-start(f32[384,128]{1,0:T(8,128)S(1)} %collective-permute-done.rest_8_), channel_id=1, source_target_pairs={{0,128},{64,192},{128,0},{192,64},{1,129},{65,193},{129,1},{193,65... | collective-permute-start | bytes 589832 | tf_op jit(solution)/shard_map/ppermute | solution.py:214
  45.2 5.8 %collective-permute-start.10 = (f32[384,128]{1,0:T(8,128)S(1)}, f32[384,128]{1,0:T(8,128)S(1)}, u32[]{:S(2)}, u32[]{:S(2)}) collective-permute-start(f32[384,128]{1,0:T(8,128)S(1)} %collective-permute-done.7.rest_2_), channel_id=1, source_target_pairs={{0,1},{1,0},{2,3},{3,2},{4,5},{5,4},{6,7},{7,6},{8,9},{9,8},{10,11... | collective-permute-start | bytes 589832 | tf_op jit(solution)/shard_map/ppermute | solution.py:219
  49.0 2.1 %collective-permute-start.17 = (f32[384,128]{1,0:T(8,128)S(1)}, f32[384,128]{1,0:T(8,128)S(1)}, u32[]{:S(2)}, u32[]{:S(2)}) collective-permute-start(f32[384,128]{1,0:T(8,128)S(1)} %collective-permute-done.13.rest_11_), channel_id=1, source_target_pairs={{0,1},{1,0},{2,3},{3,2},{4,5},{5,4},{6,7},{7,6},{8,9},{9,8},{10,11... | collective-permute-start | bytes 589832 | tf_op jit(solution)/shard_map/ppermute | solution.py:219
  49.0 2.5 %collective-permute-start.16 = (f32[384,128]{1,0:T(8,128)S(1)}, f32[384,128]{1,0:T(8,128)S(1)}, u32[]{:S(2)}, u32[]{:S(2)}) collective-permute-start(f32[384,128]{1,0:T(8,128)S(1)} %collective-permute-done.12.rest_10_), channel_id=1, source_target_pairs={{0,1},{1,0},{2,3},{3,2},{4,5},{5,4},{6,7},{7,6},{8,9},{9,8},{10,11... | collective-permute-start | bytes 589832 | tf_op jit(solution)/shard_map/ppermute | solution.py:219
  50.4 1.5 %collective-permute-start.8 = (f32[384,128]{1,0:T(8,128)S(1)}, f32[384,128]{1,0:T(8,128)S(1)}, u32[]{:S(2)}, u32[]{:S(2)}) collective-permute-start(f32[384,128]{1,0:T(8,128)S(1)} %bitcast.59), channel_id=1, source_target_pairs={{0,1},{1,0},{2,3},{3,2},{4,5},{5,4},{6,7},{7,6},{8,9},{9,8},{10,11... | collective-permute-start | bytes 589832 | tf_op jit(solution)/shard_map/ppermute | solution.py:219
  50.5 1.7 %collective-permute-start.9 = (f32[384,128]{1,0:T(8,128)S(1)}, f32[384,128]{1,0:T(8,128)S(1)}, u32[]{:S(2)}, u32[]{:S(2)}) collective-permute-start(f32[384,128]{1,0:T(8,128)S(1)} %collective-permute-done.1.rest_1_), channel_id=1, source_target_pairs={{0,1},{1,0},{2,3},{3,2},{4,5},{5,4},{6,7},{7,6},{8,9},{9,8},{10,11... | collective-permute-start | bytes 589832 | tf_op jit(solution)/shard_map/ppermute | solution.py:219
  51.0 1.5 %collective-permute-start.11 = (f32[384,128]{1,0:T(8,128)S(1)}, f32[384,128]{1,0:T(8,128)S(1)}, u32[]{:S(2)}, u32[]{:S(2)}) collective-permute-start(f32[384,128]{1,0:T(8,128)S(1)} %collective-permute-done.2.rest_3_), channel_id=1, source_target_pairs={{0,1},{1,0},{2,3},{3,2},{4,5},{5,4},{6,7},{7,6},{8,9},{9,8},{10,11... | collective-permute-start | bytes 589832 | tf_op jit(solution)/shard_map/ppermute | solution.py:219
  51.1 1.7 %collective-permute-start.14 = (f32[384,128]{1,0:T(8,128)S(1)}, f32[384,128]{1,0:T(8,128)S(1)}, u32[]{:S(2)}, u32[]{:S(2)}) collective-permute-start(f32[384,128]{1,0:T(8,128)S(1)} %collective-permute-done.rest_8_), channel_id=1, source_target_pairs={{0,1},{1,0},{2,3},{3,2},{4,5},{5,4},{6,7},{7,6},{8,9},{9,8},{10,11... | collective-permute-start | bytes 589832 | tf_op jit(solution)/shard_map/ppermute | solution.py:219
  51.5 1.5 %collective-permute-start.15 = (f32[384,128]{1,0:T(8,128)S(1)}, f32[384,128]{1,0:T(8,128)S(1)}, u32[]{:S(2)}, u32[]{:S(2)}) collective-permute-start(f32[384,128]{1,0:T(8,128)S(1)} %collective-permute-done.6.rest_9_), channel_id=1, source_target_pairs={{0,1},{1,0},{2,3},{3,2},{4,5},{5,4},{6,7},{7,6},{8,9},{9,8},{10,11... | collective-permute-start | bytes 589832 | tf_op jit(solution)/shard_map/ppermute | solution.py:219
  68.3 16.8 %all-to-all-start.1 = ((f32[16,3,8,128]{3,2,1,0:T(8,128)}), f32[16,3,8,128]{3,2,1,0:T(8,128)S(1)}, u32[]{:S(2)}, u32[]{:S(2)}) async-start(f32[16,3,8,128]{3,2,1,0:T(8,128)} %bitcast.21), calls=%async_computation.1 | async-start | bytes 393216 | tf_op jit(solution)/shard_map/all_to_all | solution.py:270

commit v10 on v6

--- a/solution.py
+++ b/solution.py
@@ -18,7 +18,7 @@
 NT = 3
 PART = NQ * NT * RA
 EPAD = 96
-CHUNK = 32
+BOUNDS = (0, 8, 48, EPAD)
 
 SMEM = pl.BlockSpec(memory_space=pltpu.SMEM)
 VMEM = pl.BlockSpec(memory_space=pltpu.VMEM)
@@ -94,11 +94,10 @@
     count = N_GRP * NS
     parts = rest[:count]
     o_ref, table, cidx, widx, idx_sem = rest[count:]
-    chunks = EPAD // CHUNK
-    length = CHUNK * LANES
+    chunks = len(BOUNDS) - 1
 
     def index_copies(k):
-        at = pl.ds(k * length, length)
+        at = pl.ds(BOUNDS[k] * LANES, (BOUNDS[k + 1] - BOUNDS[k]) * LANES)
         return (
             pltpu.make_async_copy(cidx_hbm.at[at], cidx.at[at], idx_sem.at[0, k]),
             pltpu.make_async_copy(widx_hbm.at[at], widx.at[at], idx_sem.at[1, k]),
@@ -120,7 +119,7 @@
             for a in range(RA):
                 rows = pl.ds(q * (NT * RA) + a, NT, stride=RA)
                 acc = None if k == 0 else o_ref[rows, :]
-                for e in range(k * CHUNK, min((k + 1) * CHUNK, n_exc)):
+                for e in range(BOUNDS[k], min(BOUNDS[k + 1], n_exc)):
                     base = e * LANES + a
                     ci = cidx.at[pl.ds(base, size)][start]
                     wi = widx.at[pl.ds(base, size)][start]
@@ -130,7 +129,7 @@
                     )
                     acc = term if acc is None else acc + term
                 o_ref[rows, :] = acc
-            if k == 0:
+            if k == 1:
                 mix = mix_ref[q, NT][:, : N_GRP * RA]
                 for t in range(NT):
                     at = q * (NT * RA) + t * RA
@@ -163,7 +162,7 @@
             pltpu.VMEM((count * PART, LANES), jnp.float32),
             index,
             index,
-            pltpu.SemaphoreType.DMA((2, EPAD // CHUNK)),
+            pltpu.SemaphoreType.DMA((2, len(BOUNDS) - 1)),
         ],
         compiler_params=pltpu.CompilerParams(vmem_limit_bytes=16 << 20),
         cost_estimate=pl.CostEstimate(
@@ -239,17 +238,20 @@
     own = arrived[:, :NT].reshape(PART, LANES)
     after, before = shift(own, 1), shift(own, N_GRP - 1)
     over = swap(own, "xl")
-    again, over, after, before = lax.optimization_barrier((own, over, after, before))
+    again, over, after, before, twin = lax.optimization_barrier(
+        (own, over, after, before, swap(own, "c"))
+    )
     over_after, over_before = swap(after, "xl"), swap(before, "xl")
     two, over_two = shift(again, 2), shift(over, 2)
-    (start, after, before, over), over_after = lax.optimization_barrier(
-        ((again, after, before, over), over_after)
-    )
-    near = [start, after, two, before]
+    (after, before, over), over_after = lax.optimization_barrier(
+        ((after, before, over), over_after)
+    )
+    near = [own, after, two, before]
     across = [over, over_after, over_two, over_before]
     parts = (
         near
-        + [swap(v, "c") for v in near]
+        + [twin]
+        + [swap(v, "c") for v in near[1:]]
         + across
         + [swap(v, "c") for v in across]
     )

time: 84.1 us -> 85.5 us (1.017)
  waiting for transfers between devices: 23.2 us -> 25.3 us
    ppermute x4, waiting for transfers between devices: 6.39 us -> 8.24 us  [shift(): lax.ppermute(value, 'grp', [(i, (i - k) % N_GRP) for i in range(N_GRP)])]
  transfers between devices with their start and end apart: 20 -> 20, of which waited for: 12 -> 10; matrix products, arithmetic and copies ran while one was open for 14% -> 14% of each run, Pallas kernels for 5% -> 5%
where the time goes in v10:
time: 85.5 us; the launch traced here: 85 us
  starting transfers between devices  28 us (33%)
  waiting for transfers between devices  25.3 us (30%)
  Pallas kernels  18.9 us (22%)
  matrix products  9.82 us (11%)
  local copies, waits for them, and re-layouts  1.53 us (2%)
  other arithmetic  1.35 us (2%)
    pallas_call x1, Pallas kernels, mixed_call(): pl.pallas_call(functools.partial(mixed_kernel, n_exc), out_shape=jax.Shap...  14.7 us
    all_to_all x1, starting transfers between devices, per_device(): lax.all_to_all(packed, ('z', 'xh'), split_axis=0, concat_axis=0, tiled=True)  9.88 us
    ppermute x4, waiting for transfers between devices, shift(): lax.ppermute(value, 'grp', [(i, (i - k) % N_GRP) for i in range(N_GRP)])  8.24 us
    dot_general x1, matrix products, per_device(): applied = jnp.einsum('rpk,pkl->rpl', picked, beta_blocks, precision=HIGH)  7.45 us
    ppermute x4, starting transfers between devices, shift(): lax.ppermute(value, 'grp', [(i, (i - k) % N_GRP) for i in range(N_GRP)])  6.84 us
    all_to_all x1, waiting for transfers between devices, per_device(): lax.all_to_all(packed, ('z', 'xh'), split_axis=0, concat_axis=0, tiled=True)  6.8 us
    all_to_all x1, waiting for transfers between devices, per_device(): lax.all_to_all(mixed_local.reshape(NQ, NT, RA, LANES), ('z', 'xh'), split...  5.8 us
    ppermute x11, starting transfers between devices, swap(): return lax.ppermute(value, axis, [(0, 1), (1, 0)])  5.36 us
  transfers between devices with their start and end apart: 20, of which 10 were waited for; matrix products, arithmetic and copies ran while one was open for 14% of the time, Pallas kernels for 5%

profile of v10, /device:TPU:2, one launch (start us, length us, event | category | flops | bytes accessed | tf_op | source)
XLA Modules:
  0.0 85.0 jit_solution(17304907644798389752)
XLA Ops:
  0.0 0.0 collective-permute-start
  0.0 2.4 %collective-permute-start.2 = (s32[18,96]{1,0:T(8,128)}, s32[18,96]{1,0:T(8,128)S(1)}, u32[]{:S(2)}, u32[]{:S(2)}) collective-permute-start(s32[18,96]{1,0:T(8,128)} %param.18), channel_id=1, source_target_pairs={{0,3},{1,2},{2,1},{3,0},{4,7},{5,6},{6,5},{7,4},{8,11},{9,10},{10,... | collective-permute-start | bytes 20744 | tf_op jit(solution)/shard_map/ppermute | solution.py:213
  2.4 0.0 collective-permute-start.1
  2.4 1.7 %pack.1 = f32[16,4,8,128]{3,2,1,0:T(8,128)} custom-call(s32[1]{0:T(128)} %bitcast.g_ref, s32[1,4]{1,0:T(1,128)} %mask_ref.1, f32[8,6144]{1,0:T(8,128)} %x_ref.1, f32[1,4,8,8]{3,2,1,0:T(8,128)} %alpha_ref.1), custom_call_target="tpu_custom_call" | custom-call | tf_op jit(solution)/shard_map/pack/pallas_call | solution.py:43
  4.1 9.9 %all-to-all-start = ((f32[16,4,8,128]{3,2,1,0:T(8,128)}), f32[16,4,8,128]{3,2,1,0:T(8,128)S(1)}, u32[]{:S(2)}, u32[]{:S(2)}) async-start(f32[16,4,8,128]{3,2,1,0:T(8,128)} %pack.1), calls=%async_computation | async-start | bytes 524288 | tf_op jit(solution)/shard_map/all_to_all | solution.py:205
  14.0 0.8 slice_bitcast_fusion
  14.8 1.3 %convolution_bitcast_fusion.1 = f32[8,96,128]{2,1,0:T(8,128)S(1)} fusion(f32[8,48,128]{2,0,1:T(8,128)} %bitcast.62, s32[96]{0:T(128)S(1)} %get-tuple-element.42), kind=kOutput, calls=%fused_computation.1 | convolution fusion | flops 56627712 | bytes 590208 | tf_op jit(solution)/shard_map/rnk,pn->rpk/dot_general | solution.py:234
  16.1 0.6 pad_add_fusion.1.place_ref
  16.6 2.5 %prep.1 = (s32[96,128]{1,0:T(8,128)}, s32[96,128]{1,0:T(8,128)}) custom-call(s32[2]{0:T(128)} %pad_add_fusion.1.place_ref, s32[90,512]{1,0:T(8,128)} %src_ref.1, s32[90,512]{1,0:T(8,128)} %pair_ref.1, s32[90,512]{1,0:T(8,128)} %par_ref.1), custom_call_target="tpu_custom_call" | custom-call | tf_op jit(solution)/shard_map/prep/pallas_call | solution.py:81
  19.2 0.0 collective-permute-done
  19.2 0.0 collective-permute-done.1
  19.2 0.7 pad_add_fusion
  19.9 0.8 fusion.24
  20.7 0.1 pad_maximum_fusion
  20.8 6.8 %all-to-all-done.mix_ref = f32[16,4,8,128]{3,2,1,0:T(8,128)S(1)} async-done(((f32[16,4,8,128]{3,2,1,0:T(8,128)}), f32[16,4,8,128]{3,2,1,0:T(8,128)S(1)}, u32[]{:S(2)}, u32[]{:S(2)}) %all-to-all-start) | async-done | bytes 262176 | tf_op jit(solution)/shard_map/all_to_all | solution.py:205
  27.6 0.1 collective-permute-start.6
  27.7 1.7 %collective-permute-start.5 = (f32[384,128]{1,0:T(8,128)S(1)}, f32[384,128]{1,0:T(8,128)S(1)}, u32[]{:S(2)}, u32[]{:S(2)}) collective-permute-start(f32[384,128]{1,0:T(8,128)S(1)} %bitcast.56), channel_id=1, source_target_pairs={{0,64},{64,128},{128,192},{192,0},{1,65},{65,129},{129,193},{193,1... | collective-permute-start | bytes 589832 | tf_op jit(solution)/shard_map/ppermute | solution.py:197
  29.3 1.7 %collective-permute-start.4 = (f32[384,128]{1,0:T(8,128)S(1)}, f32[384,128]{1,0:T(8,128)S(1)}, u32[]{:S(2)}, u32[]{:S(2)}) collective-permute-start(f32[384,128]{1,0:T(8,128)S(1)} %bitcast.57), channel_id=1, source_target_pairs={{0,192},{64,0},{128,64},{192,128},{1,193},{65,1},{129,65},{193,129... | collective-permute-start | bytes 589832 | tf_op jit(solution)/shard_map/ppermute | solution.py:197
  31.0 1.4 %collective-permute-start.3 = (f32[384,128]{1,0:T(8,128)S(1)}, f32[384,128]{1,0:T(8,128)S(1)}, u32[]{:S(2)}, u32[]{:S(2)}) collective-permute-start(f32[384,128]{1,0:T(8,128)S(1)} %bitcast.58), channel_id=1, source_target_pairs={{0,2},{2,0},{1,3},{3,1},{4,6},{6,4},{5,7},{7,5},{8,10},{10,8},{9,1... | collective-permute-start | bytes 589832 | tf_op jit(solution)/shard_map/ppermute | solution.py:202
  32.4 0.0 collective-permute-done.6.rest_4_
  32.4 3.8 %collective-permute-done.5.rest_3_ = f32[384,128]{1,0:T(8,128)S(1)} collective-permute-done((f32[384,128]{1,0:T(8,128)S(1)}, f32[384,128]{1,0:T(8,128)S(1)}, u32[]{:S(2)}, u32[]{:S(2)}) %collective-permute-start.5) | collective-permute-done | bytes 196640 | tf_op jit(solution)/shard_map/ppermute | solution.py:197
  36.3 0.0 collective-permute-done.4.rest_1_
  36.3 1.4 %collective-permute-done.3.rest_8_ = f32[384,128]{1,0:T(8,128)S(1)} collective-permute-done((f32[384,128]{1,0:T(8,128)S(1)}, f32[384,128]{1,0:T(8,128)S(1)}, u32[]{:S(2)}, u32[]{:S(2)}) %collective-permute-start.3) | collective-permute-done | bytes 196640 | tf_op jit(solution)/shard_map/ppermute | solution.py:202
  37.7 1.4 %collective-permute-start.7 = (f32[384,128]{1,0:T(8,128)S(1)}, f32[384,128]{1,0:T(8,128)S(1)}, u32[]{:S(2)}, u32[]{:S(2)}) collective-permute-start(f32[384,128]{1,0:T(8,128)S(1)} %collective-permute-done.4.rest_1_), channel_id=1, source_target_pairs={{0,2},{2,0},{1,3},{3,1},{4,6},{6,4},{5,7},{7,5},{8,10},{10,8},{9,1... | collective-permute-start | bytes 589832 | tf_op jit(solution)/shard_map/ppermute | solution.py:202
  39.2 1.9 %collective-permute-start.8 = (f32[384,128]{1,0:T(8,128)S(1)}, f32[384,128]{1,0:T(8,128)S(1)}, u32[]{:S(2)}, u32[]{:S(2)}) collective-permute-start(f32[384,128]{1,0:T(8,128)S(1)} %bitcast.59), channel_id=1, source_target_pairs={{0,128},{64,192},{128,0},{192,64},{1,129},{65,193},{129,1},{193,65... | collective-permute-start | bytes 589832 | tf_op jit(solution)/shard_map/ppermute | solution.py:197
  41.1 0.6 collective-permute-start.13
  41.7 1.6 %collective-permute-start.12 = (f32[384,128]{1,0:T(8,128)S(1)}, f32[384,128]{1,0:T(8,128)S(1)}, u32[]{:S(2)}, u32[]{:S(2)}) collective-permute-start(f32[384,128]{1,0:T(8,128)S(1)} %collective-permute-done.3.rest_8_), channel_id=1, source_target_pairs={{0,128},{64,192},{128,0},{192,64},{1,129},{65,193},{129,1},{193,65... | collective-permute-start | bytes 589832 | tf_op jit(solution)/shard_map/ppermute | solution.py:197
  43.3 1.8 %collective-permute-done.7.rest_9_ = f32[384,128]{1,0:T(8,128)S(1)} collective-permute-done((f32[384,128]{1,0:T(8,128)S(1)}, f32[384,128]{1,0:T(8,128)S(1)}, u32[]{:S(2)}, u32[]{:S(2)}) %collective-permute-start.7) | collective-permute-done | bytes 196640 | tf_op jit(solution)/shard_map/ppermute | solution.py:202
  45.1 3.3 %collective-permute-done.8.rest_2_ = f32[384,128]{1,0:T(8,128)S(1)} collective-permute-done((f32[384,128]{1,0:T(8,128)S(1)}, f32[384,128]{1,0:T(8,128)S(1)}, u32[]{:S(2)}, u32[]{:S(2)}) %collective-permute-start.8) | collective-permute-done | bytes 196640 | tf_op jit(solution)/shard_map/ppermute | solution.py:197
  48.4 0.0 collective-permute-start.10
  48.4 0.5 collective-permute-start.9
  48.9 0.0 collective-permute-start.11
  48.9 0.0 collective-permute-done.13.rest_11_
  48.9 0.5 collective-permute-start.14
  49.4 1.1 %collective-permute-done.12.rest_10_ = f32[384,128]{1,0:T(8,128)S(1)} collective-permute-done((f32[384,128]{1,0:T(8,128)S(1)}, f32[384,128]{1,0:T(8,128)S(1)}, u32[]{:S(2)}, u32[]{:S(2)}) %collective-permute-start.12) | collective-permute-done | bytes 196640 | tf_op jit(solution)/shard_map/ppermute | solution.py:197
  50.5 0.0 collective-permute-done.10.rest_6_
  50.5 0.5 collective-permute-start.17
  51.0 0.0 collective-permute-done.9.rest_5_
  51.0 0.3 collective-permute-start.16
  51.3 0.6 collective-permute-done.15.rest_13_
  51.9 0.3 collective-permute-done.17.rest_15_
  52.2 0.3 collective-permute-done.16.rest_14_
  52.5 14.7 %mixed.1 = f32[384,128]{1,0:T(8,128)} custom-call(s32[12288]{0:T(1024)} %bitcast.63, s32[12288]{0:T(1024)} %bitcast.64, f32[1944,128]{1,0:T(8,128)S(1)} %bitcast.54, f32[16,4,8,128]{3,2,1,0:T(8,128)S(1)} %all-to-all-done.mix_ref, f32[384,128]{1,0:T(8,128)S(1)} %bitcast.60, f32[384,128]{1,0:T(8,128)S(1)} %collective-permute-done.4.rest_1_, ...), custom_call_target="tpu_custom_call" | custom-call | flops 8847360 | bytes 8388608 | tf_op jit(solution)/shard_map/mixed/pallas_call | solution.py:156
  67.2 3.5 %all-to-all-start.1 = ((f32[16,3,8,128]{3,2,1,0:T(8,128)}), f32[16,3,8,128]{3,2,1,0:T(8,128)S(1)}, u32[]{:S(2)}, u32[]{:S(2)}) async-start(f32[16,3,8,128]{3,2,1,0:T(8,128)} %bitcast.21), calls=%async_computation.1 | async-start | bytes 393216 | tf_op jit(solution)/shard_map/all_to_all | solution.py:266
  70.7 7.5 %fusion.3 = f32[96,8,128]{2,1,0:T(8,128)S(1)} fusion(f32[96,128,128]{2,1,0:T(8,128)} %param.11, f32[8,96,128]{2,1,0:T(8,128)S(1)} %convolution_bitcast_fusion.1), kind=kOutput, calls=%fused_computation.6 | convolution fusion | flops 150994944 | bytes 7077888 | tf_op jit(solution)/shard_map/rpk,pkl->rpl/dot_general | solution.py:277
  78.1 5.8 %all-to-all-done.1 = f32[16,3,8,128]{3,2,1,0:T(8,128)S(1)} async-done(((f32[16,3,8,128]{3,2,1,0:T(8,128)}), f32[16,3,8,128]{3,2,1,0:T(8,128)S(1)}, u32[]{:S(2)}, u32[]{:S(2)}) %all-to-all-start.1) | async-done | bytes 196640 | tf_op jit(solution)/shard_map/all_to_all | solution.py:266
  83.9 0.3 fusion.5
  84.3 0.7 copy.32
  (8 shorter events, 0.0 us)
Async XLA Ops:
  0.0 19.9 %copy-start = (f32[324,18]{0,1:T(8,128)S(1)}, f32[324,18]{0,1:T(8,128)}, u32[]{:S(2)}) copy-start(f32[324,18]{0,1:T(8,128)} %param.19) | copy-start | bytes 69988
  0.0 19.2 %collective-permute-start = (s32[18,96]{1,0:T(8,128)}, s32[18,96]{1,0:T(8,128)S(1)}, u32[]{:S(2)}, u32[]{:S(2)}) collective-permute-start(s32[18,96]{1,0:T(8,128)} %param.18), channel_id=1, source_target_pairs={{0,1},{1,0},{2,3},{3,2},{4,5},{5,4},{6,7},{7,6},{8,9},{9,8},{10,11... | collective-permute-start | bytes 20744 | tf_op jit(solution)/shard_map/ppermute | solution.py:213
  0.0 19.2 %collective-permute-start.2 = (s32[18,96]{1,0:T(8,128)}, s32[18,96]{1,0:T(8,128)S(1)}, u32[]{:S(2)}, u32[]{:S(2)}) collective-permute-start(s32[18,96]{1,0:T(8,128)} %param.18), channel_id=1, source_target_pairs={{0,3},{1,2},{2,1},{3,0},{4,7},{5,6},{6,5},{7,4},{8,11},{9,10},{10,... | collective-permute-start | bytes 20744 | tf_op jit(solution)/shard_map/ppermute | solution.py:213
  2.4 16.8 %collective-permute-start.1 = (s32[18,96]{1,0:T(8,128)}, s32[18,96]{1,0:T(8,128)S(1)}, u32[]{:S(2)}, u32[]{:S(2)}) collective-permute-start(s32[18,96]{1,0:T(8,128)} %param.18), channel_id=1, source_target_pairs={{0,2},{1,3},{2,0},{3,1},{4,6},{5,7},{6,4},{7,5},{8,10},{9,11},{10,... | collective-permute-start | bytes 20744 | tf_op jit(solution)/shard_map/ppermute | solution.py:213
  4.1 23.4 %all-to-all-start = ((f32[16,4,8,128]{3,2,1,0:T(8,128)}), f32[16,4,8,128]{3,2,1,0:T(8,128)S(1)}, u32[]{:S(2)}, u32[]{:S(2)}) async-start(f32[16,4,8,128]{3,2,1,0:T(8,128)} %pack.1), calls=%async_computation | async-start | bytes 524288 | tf_op jit(solution)/shard_map/all_to_all | solution.py:205
  27.6 4.9 %collective-permute-start.6 = (f32[384,128]{1,0:T(8,128)S(1)}, f32[384,128]{1,0:T(8,128)S(1)}, u32[]{:S(2)}, u32[]{:S(2)}) collective-permute-start(f32[384,128]{1,0:T(8,128)S(1)} %bitcast.55), channel_id=1, source_target_pairs={{0,1},{1,0},{2,3},{3,2},{4,5},{5,4},{6,7},{7,6},{8,9},{9,8},{10,11... | collective-permute-start | bytes 589832 | tf_op jit(solution)/shard_map/ppermute | solution.py:202
  27.7 8.6 %collective-permute-start.5 = (f32[384,128]{1,0:T(8,128)S(1)}, f32[384,128]{1,0:T(8,128)S(1)}, u32[]{:S(2)}, u32[]{:S(2)}) collective-permute-start(f32[384,128]{1,0:T(8,128)S(1)} %bitcast.56), channel_id=1, source_target_pairs={{0,64},{64,128},{128,192},{192,0},{1,65},{65,129},{129,193},{193,1... | collective-permute-start | bytes 589832 | tf_op jit(solution)/shard_map/ppermute | solution.py:197
  29.3 7.0 %collective-permute-start.4 = (f32[384,128]{1,0:T(8,128)S(1)}, f32[384,128]{1,0:T(8,128)S(1)}, u32[]{:S(2)}, u32[]{:S(2)}) collective-permute-start(f32[384,128]{1,0:T(8,128)S(1)} %bitcast.57), channel_id=1, source_target_pairs={{0,192},{64,0},{128,64},{192,128},{1,193},{65,1},{129,65},{193,129... | collective-permute-start | bytes 589832 | tf_op jit(solution)/shard_map/ppermute | solution.py:197
  31.0 6.7 %collective-permute-start.3 = (f32[384,128]{1,0:T(8,128)S(1)}, f32[384,128]{1,0:T(8,128)S(1)}, u32[]{:S(2)}, u32[]{:S(2)}) collective-permute-start(f32[384,128]{1,0:T(8,128)S(1)} %bitcast.58), channel_id=1, source_target_pairs={{0,2},{2,0},{1,3},{3,1},{4,6},{6,4},{5,7},{7,5},{8,10},{10,8},{9,1... | collective-permute-start | bytes 589832 | tf_op jit(solution)/shard_map/ppermute | solution.py:202
  37.7 7.3 %collective-permute-start.7 = (f32[384,128]{1,0:T(8,128)S(1)}, f32[384,128]{1,0:T(8,128)S(1)}, u32[]{:S(2)}, u32[]{:S(2)}) collective-permute-start(f32[384,128]{1,0:T(8,128)S(1)} %collective-permute-done.4.rest_1_), channel_id=1, source_target_pairs={{0,2},{2,0},{1,3},{3,1},{4,6},{6,4},{5,7},{7,5},{8,10},{10,8},{9,1... | collective-permute-start | bytes 589832 | tf_op jit(solution)/shard_map/ppermute | solution.py:202
  39.2 9.2 %collective-permute-start.8 = (f32[384,128]{1,0:T(8,128)S(1)}, f32[384,128]{1,0:T(8,128)S(1)}, u32[]{:S(2)}, u32[]{:S(2)}) collective-permute-start(f32[384,128]{1,0:T(8,128)S(1)} %bitcast.59), channel_id=1, source_target_pairs={{0,128},{64,192},{128,0},{192,64},{1,129},{65,193},{129,1},{193,65... | collective-permute-start | bytes 589832 | tf_op jit(solution)/shard_map/ppermute | solution.py:197
  41.1 7.8 %collective-permute-start.13 = (f32[384,128]{1,0:T(8,128)S(1)}, f32[384,128]{1,0:T(8,128)S(1)}, u32[]{:S(2)}, u32[]{:S(2)}) collective-permute-start(f32[384,128]{1,0:T(8,128)S(1)} %collective-permute-done.5.rest_3_), channel_id=1, source_target_pairs={{0,2},{2,0},{1,3},{3,1},{4,6},{6,4},{5,7},{7,5},{8,10},{10,8},{9,1... | collective-permute-start | bytes 589832 | tf_op jit(solution)/shard_map/ppermute | solution.py:202
  41.7 8.8 %collective-permute-start.12 = (f32[384,128]{1,0:T(8,128)S(1)}, f32[384,128]{1,0:T(8,128)S(1)}, u32[]{:S(2)}, u32[]{:S(2)}) collective-permute-start(f32[384,128]{1,0:T(8,128)S(1)} %collective-permute-done.3.rest_8_), channel_id=1, source_target_pairs={{0,128},{64,192},{128,0},{192,64},{1,129},{65,193},{129,1},{193,65... | collective-permute-start | bytes 589832 | tf_op jit(solution)/shard_map/ppermute | solution.py:197
  48.4 2.1 %collective-permute-start.10 = (f32[384,128]{1,0:T(8,128)S(1)}, f32[384,128]{1,0:T(8,128)S(1)}, u32[]{:S(2)}, u32[]{:S(2)}) collective-permute-start(f32[384,128]{1,0:T(8,128)S(1)} %collective-permute-done.8.rest_2_), channel_id=1, source_target_pairs={{0,1},{1,0},{2,3},{3,2},{4,5},{5,4},{6,7},{7,6},{8,9},{9,8},{10,11... | collective-permute-start | bytes 589832 | tf_op jit(solution)/shard_map/ppermute | solution.py:202
  48.4 2.6 %collective-permute-start.9 = (f32[384,128]{1,0:T(8,128)S(1)}, f32[384,128]{1,0:T(8,128)S(1)}, u32[]{:S(2)}, u32[]{:S(2)}) collective-permute-start(f32[384,128]{1,0:T(8,128)S(1)} %collective-permute-done.4.rest_1_), channel_id=1, source_target_pairs={{0,1},{1,0},{2,3},{3,2},{4,5},{5,4},{6,7},{7,6},{8,9},{9,8},{10,11... | collective-permute-start | bytes 589832 | tf_op jit(solution)/shard_map/ppermute | solution.py:202
  48.9 2.4 %collective-permute-start.11 = (f32[384,128]{1,0:T(8,128)S(1)}, f32[384,128]{1,0:T(8,128)S(1)}, u32[]{:S(2)}, u32[]{:S(2)}) collective-permute-start(f32[384,128]{1,0:T(8,128)S(1)} %collective-permute-done.5.rest_3_), channel_id=1, source_target_pairs={{0,1},{1,0},{2,3},{3,2},{4,5},{5,4},{6,7},{7,6},{8,9},{9,8},{10,11... | collective-permute-start | bytes 589832 | tf_op jit(solution)/shard_map/ppermute | solution.py:202
  48.9 2.4 %collective-permute-start.14 = (f32[384,128]{1,0:T(8,128)S(1)}, f32[384,128]{1,0:T(8,128)S(1)}, u32[]{:S(2)}, u32[]{:S(2)}) collective-permute-start(f32[384,128]{1,0:T(8,128)S(1)} %collective-permute-done.3.rest_8_), channel_id=1, source_target_pairs={{0,1},{1,0},{2,3},{3,2},{4,5},{5,4},{6,7},{7,6},{8,9},{9,8},{10,11... | collective-permute-start | bytes 589832 | tf_op jit(solution)/shard_map/ppermute | solution.py:202
  50.5 1.4 %collective-permute-start.15 = (f32[384,128]{1,0:T(8,128)S(1)}, f32[384,128]{1,0:T(8,128)S(1)}, u32[]{:S(2)}, u32[]{:S(2)}) collective-permute-start(f32[384,128]{1,0:T(8,128)S(1)} %collective-permute-done.7.rest_9_), channel_id=1, source_target_pairs={{0,1},{1,0},{2,3},{3,2},{4,5},{5,4},{6,7},{7,6},{8,9},{9,8},{10,11... | collective-permute-start | bytes 589832 | tf_op jit(solution)/shard_map/ppermute | solution.py:202
  50.5 1.7 %collective-permute-start.17 = (f32[384,128]{1,0:T(8,128)S(1)}, f32[384,128]{1,0:T(8,128)S(1)}, u32[]{:S(2)}, u32[]{:S(2)}) collective-permute-start(f32[384,128]{1,0:T(8,128)S(1)} %collective-permute-done.13.rest_11_), channel_id=1, source_target_pairs={{0,1},{1,0},{2,3},{3,2},{4,5},{5,4},{6,7},{7,6},{8,9},{9,8},{10,11... | collective-permute-start | bytes 589832 | tf_op jit(solution)/shard_map/ppermute | solution.py:202
  51.0 1.5 %collective-permute-start.16 = (f32[384,128]{1,0:T(8,128)S(1)}, f32[384,128]{1,0:T(8,128)S(1)}, u32[]{:S(2)}, u32[]{:S(2)}) collective-permute-start(f32[384,128]{1,0:T(8,128)S(1)} %collective-permute-done.12.rest_10_), channel_id=1, source_target_pairs={{0,1},{1,0},{2,3},{3,2},{4,5},{5,4},{6,7},{7,6},{8,9},{9,8},{10,11... | collective-permute-start | bytes 589832 | tf_op jit(solution)/shard_map/ppermute | solution.py:202
  67.2 16.8 %all-to-all-start.1 = ((f32[16,3,8,128]{3,2,1,0:T(8,128)}), f32[16,3,8,128]{3,2,1,0:T(8,128)S(1)}, u32[]{:S(2)}, u32[]{:S(2)}) async-start(f32[16,3,8,128]{3,2,1,0:T(8,128)} %bitcast.21), calls=%async_computation.1 | async-start | bytes 393216 | tf_op jit(solution)/shard_map/all_to_all | solution.py:266

commit v11 on v10

--- a/solution.py
+++ b/solution.py
@@ -238,20 +238,17 @@
     own = arrived[:, :NT].reshape(PART, LANES)
     after, before = shift(own, 1), shift(own, N_GRP - 1)
     over = swap(own, "xl")
-    again, over, after, before, twin = lax.optimization_barrier(
-        (own, over, after, before, swap(own, "c"))
-    )
+    again, over, after, before = lax.optimization_barrier((own, over, after, before))
     over_after, over_before = swap(after, "xl"), swap(before, "xl")
     two, over_two = shift(again, 2), shift(over, 2)
-    (after, before, over), over_after = lax.optimization_barrier(
-        ((after, before, over), over_after)
-    )
-    near = [own, after, two, before]
+    (start, after, before, over), over_after = lax.optimization_barrier(
+        ((again, after, before, over), over_after)
+    )
+    near = [start, after, two, before]
     across = [over, over_after, over_two, over_before]
     parts = (
         near
-        + [twin]
-        + [swap(v, "c") for v in near[1:]]
+        + [swap(v, "c") for v in near]
         + across
         + [swap(v, "c") for v in across]
     )

time: 85.5 us -> 83.5 us (0.977)
  waiting for transfers between devices: 25.3 us -> 23.2 us
    ppermute x4, waiting for transfers between devices: 8.24 us -> 6.39 us  [shift(): lax.ppermute(value, 'grp', [(i, (i - k) % N_GRP) for i in range(N_GRP)])]
  transfers between devices with their start and end apart: 20 -> 20, of which waited for: 10 -> 12; matrix products, arithmetic and copies ran while one was open for 14% -> 14% of each run, Pallas kernels for 5% -> 5%
where the time goes in v11:
time: 83.5 us; the launch traced here: 82.6 us
  starting transfers between devices  27.7 us (33%)
  waiting for transfers between devices  23.2 us (28%)
  Pallas kernels  18.9 us (23%)
  matrix products  9.82 us (12%)
  local copies, waits for them, and re-layouts  1.53 us (2%)
  other arithmetic  1.35 us (2%)
    pallas_call x1, Pallas kernels, mixed_call(): pl.pallas_call(functools.partial(mixed_kernel, n_exc), out_shape=jax.Shap...  14.7 us
    all_to_all x1, starting transfers between devices, per_device(): lax.all_to_all(packed, ('z', 'xh'), split_axis=0, concat_axis=0, tiled=True)  9.88 us
    dot_general x1, matrix products, per_device(): applied = jnp.einsum('rpk,pkl->rpl', picked, beta_blocks, precision=HIGH)  7.45 us
    ppermute x4, starting transfers between devices, shift(): lax.ppermute(value, 'grp', [(i, (i - k) % N_GRP) for i in range(N_GRP)])  6.84 us
    all_to_all x1, waiting for transfers between devices, per_device(): lax.all_to_all(packed, ('z', 'xh'), split_axis=0, concat_axis=0, tiled=True)  6.8 us
    ppermute x4, waiting for transfers between devices, shift(): lax.ppermute(value, 'grp', [(i, (i - k) % N_GRP) for i in range(N_GRP)])  6.39 us
    all_to_all x1, waiting for transfers between devices, per_device(): lax.all_to_all(mixed_local.reshape(NQ, NT, RA, LANES), ('z', 'xh'), split...  5.81 us
    ppermute x11, starting transfers between devices, swap(): return lax.ppermute(value, axis, [(0, 1), (1, 0)])  5 us
  transfers between devices with their start and end apart: 20, of which 12 were waited for; matrix products, arithmetic and copies ran while one was open for 14% of the time, Pallas kernels for 5%

profile of v11, /device:TPU:2, one launch (start us, length us, event | category | flops | bytes accessed | tf_op | source)
XLA Modules:
  0.0 82.6 jit_solution(10354161356544895143)
XLA Ops:
  0.0 0.0 collective-permute-start
  0.0 2.4 %collective-permute-start.2 = (s32[18,96]{1,0:T(8,128)}, s32[18,96]{1,0:T(8,128)S(1)}, u32[]{:S(2)}, u32[]{:S(2)}) collective-permute-start(s32[18,96]{1,0:T(8,128)} %param.18), channel_id=1, source_target_pairs={{0,3},{1,2},{2,1},{3,0},{4,7},{5,6},{6,5},{7,4},{8,11},{9,10},{10,... | collective-permute-start | bytes 20744 | tf_op jit(solution)/shard_map/ppermute | solution.py:213
  2.4 0.0 collective-permute-start.1
  2.4 1.7 %pack.1 = f32[16,4,8,128]{3,2,1,0:T(8,128)} custom-call(s32[1]{0:T(128)} %bitcast.g_ref, s32[1,4]{1,0:T(1,128)} %mask_ref.1, f32[8,6144]{1,0:T(8,128)} %x_ref.1, f32[1,4,8,8]{3,2,1,0:T(8,128)} %alpha_ref.1), custom_call_target="tpu_custom_call" | custom-call | tf_op jit(solution)/shard_map/pack/pallas_call | solution.py:43
  4.1 9.9 %all-to-all-start = ((f32[16,4,8,128]{3,2,1,0:T(8,128)}), f32[16,4,8,128]{3,2,1,0:T(8,128)S(1)}, u32[]{:S(2)}, u32[]{:S(2)}) async-start(f32[16,4,8,128]{3,2,1,0:T(8,128)} %pack.1), calls=%async_computation | async-start | bytes 524288 | tf_op jit(solution)/shard_map/all_to_all | solution.py:205
  14.0 0.8 slice_bitcast_fusion
  14.8 1.3 %convolution_bitcast_fusion.1 = f32[8,96,128]{2,1,0:T(8,128)S(1)} fusion(f32[8,48,128]{2,0,1:T(8,128)} %bitcast.62, s32[96]{0:T(128)S(1)} %get-tuple-element.42), kind=kOutput, calls=%fused_computation.1 | convolution fusion | flops 56627712 | bytes 590208 | tf_op jit(solution)/shard_map/rnk,pn->rpk/dot_general | solution.py:234
  16.1 0.6 pad_add_fusion.1.place_ref
  16.6 2.5 %prep.1 = (s32[96,128]{1,0:T(8,128)}, s32[96,128]{1,0:T(8,128)}) custom-call(s32[2]{0:T(128)} %pad_add_fusion.1.place_ref, s32[90,512]{1,0:T(8,128)} %src_ref.1, s32[90,512]{1,0:T(8,128)} %pair_ref.1, s32[90,512]{1,0:T(8,128)} %par_ref.1), custom_call_target="tpu_custom_call" | custom-call | tf_op jit(solution)/shard_map/prep/pallas_call | solution.py:81
  19.2 0.0 collective-permute-done
  19.2 0.0 collective-permute-done.1
  19.2 0.7 pad_add_fusion
  19.9 0.8 fusion.24
  20.7 0.1 pad_maximum_fusion
  20.8 6.8 %all-to-all-done.mix_ref = f32[16,4,8,128]{3,2,1,0:T(8,128)S(1)} async-done(((f32[16,4,8,128]{3,2,1,0:T(8,128)}), f32[16,4,8,128]{3,2,1,0:T(8,128)S(1)}, u32[]{:S(2)}, u32[]{:S(2)}) %all-to-all-start) | async-done | bytes 262176 | tf_op jit(solution)/shard_map/all_to_all | solution.py:205
  27.6 1.7 %collective-permute-start.5 = (f32[384,128]{1,0:T(8,128)S(1)}, f32[384,128]{1,0:T(8,128)S(1)}, u32[]{:S(2)}, u32[]{:S(2)}) collective-permute-start(f32[384,128]{1,0:T(8,128)S(1)} %bitcast.55), channel_id=1, source_target_pairs={{0,64},{64,128},{128,192},{192,0},{1,65},{65,129},{129,193},{193,1... | collective-permute-start | bytes 589832 | tf_op jit(solution)/shard_map/ppermute | solution.py:197
  29.2 1.7 %collective-permute-start.4 = (f32[384,128]{1,0:T(8,128)S(1)}, f32[384,128]{1,0:T(8,128)S(1)}, u32[]{:S(2)}, u32[]{:S(2)}) collective-permute-start(f32[384,128]{1,0:T(8,128)S(1)} %bitcast.56), channel_id=1, source_target_pairs={{0,192},{64,0},{128,64},{192,128},{1,193},{65,1},{129,65},{193,129... | collective-permute-start | bytes 589832 | tf_op jit(solution)/shard_map/ppermute | solution.py:197
  30.9 1.4 %collective-permute-start.3 = (f32[384,128]{1,0:T(8,128)S(1)}, f32[384,128]{1,0:T(8,128)S(1)}, u32[]{:S(2)}, u32[]{:S(2)}) collective-permute-start(f32[384,128]{1,0:T(8,128)S(1)} %bitcast.57), channel_id=1, source_target_pairs={{0,2},{2,0},{1,3},{3,1},{4,6},{6,4},{5,7},{7,5},{8,10},{10,8},{9,1... | collective-permute-start | bytes 589832 | tf_op jit(solution)/shard_map/ppermute | solution.py:202
  32.3 2.2 %collective-permute-done.5.rest_3_ = f32[384,128]{1,0:T(8,128)S(1)} collective-permute-done((f32[384,128]{1,0:T(8,128)S(1)}, f32[384,128]{1,0:T(8,128)S(1)}, u32[]{:S(2)}, u32[]{:S(2)}) %collective-permute-start.5) | collective-permute-done | bytes 196640 | tf_op jit(solution)/shard_map/ppermute | solution.py:197
  34.6 0.4 collective-permute-done.4.rest_1_
  34.9 1.7 %collective-permute-done.3.rest_8_ = f32[384,128]{1,0:T(8,128)S(1)} collective-permute-done((f32[384,128]{1,0:T(8,128)S(1)}, f32[384,128]{1,0:T(8,128)S(1)}, u32[]{:S(2)}, u32[]{:S(2)}) %collective-permute-start.3) | collective-permute-done | bytes 196640 | tf_op jit(solution)/shard_map/ppermute | solution.py:202
  36.6 2.0 %collective-permute-start.7 = (f32[384,128]{1,0:T(8,128)S(1)}, f32[384,128]{1,0:T(8,128)S(1)}, u32[]{:S(2)}, u32[]{:S(2)}) collective-permute-start(f32[384,128]{1,0:T(8,128)S(1)} %bitcast.58), channel_id=1, source_target_pairs={{0,128},{64,192},{128,0},{192,64},{1,129},{65,193},{129,1},{193,65... | collective-permute-start | bytes 589832 | tf_op jit(solution)/shard_map/ppermute | solution.py:197
  38.6 1.4 %collective-permute-start.6 = (f32[384,128]{1,0:T(8,128)S(1)}, f32[384,128]{1,0:T(8,128)S(1)}, u32[]{:S(2)}, u32[]{:S(2)}) collective-permute-start(f32[384,128]{1,0:T(8,128)S(1)} %collective-permute-done.4.rest_1_), channel_id=1, source_target_pairs={{0,2},{2,0},{1,3},{3,1},{4,6},{6,4},{5,7},{7,5},{8,10},{10,8},{9,1... | collective-permute-start | bytes 589832 | tf_op jit(solution)/shard_map/ppermute | solution.py:202
  40.0 0.6 collective-permute-start.13
  40.6 1.5 %collective-permute-start.12 = (f32[384,128]{1,0:T(8,128)S(1)}, f32[384,128]{1,0:T(8,128)S(1)}, u32[]{:S(2)}, u32[]{:S(2)}) collective-permute-start(f32[384,128]{1,0:T(8,128)S(1)} %collective-permute-done.3.rest_8_), channel_id=1, source_target_pairs={{0,128},{64,192},{128,0},{192,64},{1,129},{65,193},{129,1},{193,65... | collective-permute-start | bytes 589832 | tf_op jit(solution)/shard_map/ppermute | solution.py:197
  42.1 2.4 %collective-permute-done.7.rest_2_ = f32[384,128]{1,0:T(8,128)S(1)} collective-permute-done((f32[384,128]{1,0:T(8,128)S(1)}, f32[384,128]{1,0:T(8,128)S(1)}, u32[]{:S(2)}, u32[]{:S(2)}) %collective-permute-start.7) | collective-permute-done | bytes 196640 | tf_op jit(solution)/shard_map/ppermute | solution.py:197
  44.5 0.5 collective-permute-start.8
  45.0 0.0 collective-permute-start.9
  45.1 1.3 %collective-permute-done.13.rest_11_ = f32[384,128]{1,0:T(8,128)S(1)} collective-permute-done((f32[384,128]{1,0:T(8,128)S(1)}, f32[384,128]{1,0:T(8,128)S(1)}, u32[]{:S(2)}, u32[]{:S(2)}) %collective-permute-start.13) | collective-permute-done | bytes 196640 | tf_op jit(solution)/shard_map/ppermute | solution.py:202
  46.3 1.4 %collective-permute-done.12.rest_10_ = f32[384,128]{1,0:T(8,128)S(1)} collective-permute-done((f32[384,128]{1,0:T(8,128)S(1)}, f32[384,128]{1,0:T(8,128)S(1)}, u32[]{:S(2)}, u32[]{:S(2)}) %collective-permute-start.12) | collective-permute-done | bytes 196640 | tf_op jit(solution)/shard_map/ppermute | solution.py:197
  47.8 0.0 collective-permute-start.14
  47.8 0.0 collective-permute-done.10.rest_6_
  47.8 0.5 collective-permute-start.15
  48.3 0.0 collective-permute-done.8.rest_4_
  48.3 0.1 collective-permute-start.17
  48.4 0.0 collective-permute-done.9.rest_5_
  48.4 0.4 collective-permute-start.16
  48.8 0.0 collective-permute-done.11.rest_7_
  48.8 0.4 collective-permute-done.14.rest_12_
  49.2 0.3 collective-permute-done.15.rest_13_
  49.5 0.3 collective-permute-done.17.rest_15_
  49.8 0.3 collective-permute-done.16.rest_14_
  50.1 14.7 %mixed.1 = f32[384,128]{1,0:T(8,128)} custom-call(s32[12288]{0:T(1024)} %bitcast.63, s32[12288]{0:T(1024)} %bitcast.64, f32[1944,128]{1,0:T(8,128)S(1)} %bitcast.54, f32[16,4,8,128]{3,2,1,0:T(8,128)S(1)} %all-to-all-done.mix_ref, f32[384,128]{1,0:T(8,128)S(1)} %bitcast.60, f32[384,128]{1,0:T(8,128)S(1)} %collective-permute-done.4.rest_1_, ...), custom_call_target="tpu_custom_call" | custom-call | flops 8847360 | bytes 8388608 | tf_op jit(solution)/shard_map/mixed/pallas_call | solution.py:156
  64.7 3.5 %all-to-all-start.1 = ((f32[16,3,8,128]{3,2,1,0:T(8,128)}), f32[16,3,8,128]{3,2,1,0:T(8,128)S(1)}, u32[]{:S(2)}, u32[]{:S(2)}) async-start(f32[16,3,8,128]{3,2,1,0:T(8,128)} %bitcast.21), calls=%async_computation.1 | async-start | bytes 393216 | tf_op jit(solution)/shard_map/all_to_all | solution.py:263
  68.3 7.5 %fusion.3 = f32[96,8,128]{2,1,0:T(8,128)S(1)} fusion(f32[96,128,128]{2,1,0:T(8,128)} %param.11, f32[8,96,128]{2,1,0:T(8,128)S(1)} %convolution_bitcast_fusion.1), kind=kOutput, calls=%fused_computation.6 | convolution fusion | flops 150994944 | bytes 7077888 | tf_op jit(solution)/shard_map/rpk,pkl->rpl/dot_general | solution.py:274
  75.7 5.8 %all-to-all-done.1 = f32[16,3,8,128]{3,2,1,0:T(8,128)S(1)} async-done(((f32[16,3,8,128]{3,2,1,0:T(8,128)}), f32[16,3,8,128]{3,2,1,0:T(8,128)S(1)}, u32[]{:S(2)}, u32[]{:S(2)}) %all-to-all-start.1) | async-done | bytes 196640 | tf_op jit(solution)/shard_map/all_to_all | solution.py:263
  81.5 0.3 fusion.5
  81.8 0.7 copy.32
  (8 shorter events, 0.0 us)
Async XLA Ops:
  0.0 19.9 %copy-start = (f32[324,18]{0,1:T(8,128)S(1)}, f32[324,18]{0,1:T(8,128)}, u32[]{:S(2)}) copy-start(f32[324,18]{0,1:T(8,128)} %param.19) | copy-start | bytes 69988
  0.0 19.2 %collective-permute-start = (s32[18,96]{1,0:T(8,128)}, s32[18,96]{1,0:T(8,128)S(1)}, u32[]{:S(2)}, u32[]{:S(2)}) collective-permute-start(s32[18,96]{1,0:T(8,128)} %param.18), channel_id=1, source_target_pairs={{0,1},{1,0},{2,3},{3,2},{4,5},{5,4},{6,7},{7,6},{8,9},{9,8},{10,11... | collective-permute-start | bytes 20744 | tf_op jit(solution)/shard_map/ppermute | solution.py:213
  0.0 19.2 %collective-permute-start.2 = (s32[18,96]{1,0:T(8,128)}, s32[18,96]{1,0:T(8,128)S(1)}, u32[]{:S(2)}, u32[]{:S(2)}) collective-permute-start(s32[18,96]{1,0:T(8,128)} %param.18), channel_id=1, source_target_pairs={{0,3},{1,2},{2,1},{3,0},{4,7},{5,6},{6,5},{7,4},{8,11},{9,10},{10,... | collective-permute-start | bytes 20744 | tf_op jit(solution)/shard_map/ppermute | solution.py:213
  2.4 16.8 %collective-permute-start.1 = (s32[18,96]{1,0:T(8,128)}, s32[18,96]{1,0:T(8,128)S(1)}, u32[]{:S(2)}, u32[]{:S(2)}) collective-permute-start(s32[18,96]{1,0:T(8,128)} %param.18), channel_id=1, source_target_pairs={{0,2},{1,3},{2,0},{3,1},{4,6},{5,7},{6,4},{7,5},{8,10},{9,11},{10,... | collective-permute-start | bytes 20744 | tf_op jit(solution)/shard_map/ppermute | solution.py:213
  4.1 23.4 %all-to-all-start = ((f32[16,4,8,128]{3,2,1,0:T(8,128)}), f32[16,4,8,128]{3,2,1,0:T(8,128)S(1)}, u32[]{:S(2)}, u32[]{:S(2)}) async-start(f32[16,4,8,128]{3,2,1,0:T(8,128)} %pack.1), calls=%async_computation | async-start | bytes 524288 | tf_op jit(solution)/shard_map/all_to_all | solution.py:205
  27.6 7.0 %collective-permute-start.5 = (f32[384,128]{1,0:T(8,128)S(1)}, f32[384,128]{1,0:T(8,128)S(1)}, u32[]{:S(2)}, u32[]{:S(2)}) collective-permute-start(f32[384,128]{1,0:T(8,128)S(1)} %bitcast.55), channel_id=1, source_target_pairs={{0,64},{64,128},{128,192},{192,0},{1,65},{65,129},{129,193},{193,1... | collective-permute-start | bytes 589832 | tf_op jit(solution)/shard_map/ppermute | solution.py:197
  29.2 5.7 %collective-permute-start.4 = (f32[384,128]{1,0:T(8,128)S(1)}, f32[384,128]{1,0:T(8,128)S(1)}, u32[]{:S(2)}, u32[]{:S(2)}) collective-permute-start(f32[384,128]{1,0:T(8,128)S(1)} %bitcast.56), channel_id=1, source_target_pairs={{0,192},{64,0},{128,64},{192,128},{1,193},{65,1},{129,65},{193,129... | collective-permute-start | bytes 589832 | tf_op jit(solution)/shard_map/ppermute | solution.py:197
  30.9 5.7 %collective-permute-start.3 = (f32[384,128]{1,0:T(8,128)S(1)}, f32[384,128]{1,0:T(8,128)S(1)}, u32[]{:S(2)}, u32[]{:S(2)}) collective-permute-start(f32[384,128]{1,0:T(8,128)S(1)} %bitcast.57), channel_id=1, source_target_pairs={{0,2},{2,0},{1,3},{3,1},{4,6},{6,4},{5,7},{7,5},{8,10},{10,8},{9,1... | collective-permute-start | bytes 589832 | tf_op jit(solution)/shard_map/ppermute | solution.py:202
  36.6 8.0 %collective-permute-start.7 = (f32[384,128]{1,0:T(8,128)S(1)}, f32[384,128]{1,0:T(8,128)S(1)}, u32[]{:S(2)}, u32[]{:S(2)}) collective-permute-start(f32[384,128]{1,0:T(8,128)S(1)} %bitcast.58), channel_id=1, source_target_pairs={{0,128},{64,192},{128,0},{192,64},{1,129},{65,193},{129,1},{193,65... | collective-permute-start | bytes 589832 | tf_op jit(solution)/shard_map/ppermute | solution.py:197
  38.6 6.0 %collective-permute-start.6 = (f32[384,128]{1,0:T(8,128)S(1)}, f32[384,128]{1,0:T(8,128)S(1)}, u32[]{:S(2)}, u32[]{:S(2)}) collective-permute-start(f32[384,128]{1,0:T(8,128)S(1)} %collective-permute-done.4.rest_1_), channel_id=1, source_target_pairs={{0,2},{2,0},{1,3},{3,1},{4,6},{6,4},{5,7},{7,5},{8,10},{10,8},{9,1... | collective-permute-start | bytes 589832 | tf_op jit(solution)/shard_map/ppermute | solution.py:202
  40.0 6.3 %collective-permute-start.13 = (f32[384,128]{1,0:T(8,128)S(1)}, f32[384,128]{1,0:T(8,128)S(1)}, u32[]{:S(2)}, u32[]{:S(2)}) collective-permute-start(f32[384,128]{1,0:T(8,128)S(1)} %collective-permute-done.5.rest_3_), channel_id=1, source_target_pairs={{0,2},{2,0},{1,3},{3,1},{4,6},{6,4},{5,7},{7,5},{8,10},{10,8},{9,1... | collective-permute-start | bytes 589832 | tf_op jit(solution)/shard_map/ppermute | solution.py:202
  40.6 7.2 %collective-permute-start.12 = (f32[384,128]{1,0:T(8,128)S(1)}, f32[384,128]{1,0:T(8,128)S(1)}, u32[]{:S(2)}, u32[]{:S(2)}) collective-permute-start(f32[384,128]{1,0:T(8,128)S(1)} %collective-permute-done.3.rest_8_), channel_id=1, source_target_pairs={{0,128},{64,192},{128,0},{192,64},{1,129},{65,193},{129,1},{193,65... | collective-permute-start | bytes 589832 | tf_op jit(solution)/shard_map/ppermute | solution.py:197
  44.5 3.2 %collective-permute-start.10 = (f32[384,128]{1,0:T(8,128)S(1)}, f32[384,128]{1,0:T(8,128)S(1)}, u32[]{:S(2)}, u32[]{:S(2)}) collective-permute-start(f32[384,128]{1,0:T(8,128)S(1)} %collective-permute-done.7.rest_2_), channel_id=1, source_target_pairs={{0,1},{1,0},{2,3},{3,2},{4,5},{5,4},{6,7},{7,6},{8,9},{9,8},{10,11... | collective-permute-start | bytes 589832 | tf_op jit(solution)/shard_map/ppermute | solution.py:202
  44.5 3.7 %collective-permute-start.8 = (f32[384,128]{1,0:T(8,128)S(1)}, f32[384,128]{1,0:T(8,128)S(1)}, u32[]{:S(2)}, u32[]{:S(2)}) collective-permute-start(f32[384,128]{1,0:T(8,128)S(1)} %bitcast.59), channel_id=1, source_target_pairs={{0,1},{1,0},{2,3},{3,2},{4,5},{5,4},{6,7},{7,6},{8,9},{9,8},{10,11... | collective-permute-start | bytes 589832 | tf_op jit(solution)/shard_map/ppermute | solution.py:202
  45.0 3.3 %collective-permute-start.9 = (f32[384,128]{1,0:T(8,128)S(1)}, f32[384,128]{1,0:T(8,128)S(1)}, u32[]{:S(2)}, u32[]{:S(2)}) collective-permute-start(f32[384,128]{1,0:T(8,128)S(1)} %collective-permute-done.4.rest_1_), channel_id=1, source_target_pairs={{0,1},{1,0},{2,3},{3,2},{4,5},{5,4},{6,7},{7,6},{8,9},{9,8},{10,11... | collective-permute-start | bytes 589832 | tf_op jit(solution)/shard_map/ppermute | solution.py:202
  46.3 2.5 %collective-permute-start.11 = (f32[384,128]{1,0:T(8,128)S(1)}, f32[384,128]{1,0:T(8,128)S(1)}, u32[]{:S(2)}, u32[]{:S(2)}) collective-permute-start(f32[384,128]{1,0:T(8,128)S(1)} %collective-permute-done.5.rest_3_), channel_id=1, source_target_pairs={{0,1},{1,0},{2,3},{3,2},{4,5},{5,4},{6,7},{7,6},{8,9},{9,8},{10,11... | collective-permute-start | bytes 589832 | tf_op jit(solution)/shard_map/ppermute | solution.py:202
  47.8 1.4 %collective-permute-start.14 = (f32[384,128]{1,0:T(8,128)S(1)}, f32[384,128]{1,0:T(8,128)S(1)}, u32[]{:S(2)}, u32[]{:S(2)}) collective-permute-start(f32[384,128]{1,0:T(8,128)S(1)} %collective-permute-done.3.rest_8_), channel_id=1, source_target_pairs={{0,1},{1,0},{2,3},{3,2},{4,5},{5,4},{6,7},{7,6},{8,9},{9,8},{10,11... | collective-permute-start | bytes 589832 | tf_op jit(solution)/shard_map/ppermute | solution.py:202
  47.8 1.7 %collective-permute-start.15 = (f32[384,128]{1,0:T(8,128)S(1)}, f32[384,128]{1,0:T(8,128)S(1)}, u32[]{:S(2)}, u32[]{:S(2)}) collective-permute-start(f32[384,128]{1,0:T(8,128)S(1)} %collective-permute-done.6.rest_9_), channel_id=1, source_target_pairs={{0,1},{1,0},{2,3},{3,2},{4,5},{5,4},{6,7},{7,6},{8,9},{9,8},{10,11... | collective-permute-start | bytes 589832 | tf_op jit(solution)/shard_map/ppermute | solution.py:202
  48.3 1.5 %collective-permute-start.17 = (f32[384,128]{1,0:T(8,128)S(1)}, f32[384,128]{1,0:T(8,128)S(1)}, u32[]{:S(2)}, u32[]{:S(2)}) collective-permute-start(f32[384,128]{1,0:T(8,128)S(1)} %collective-permute-done.13.rest_11_), channel_id=1, source_target_pairs={{0,1},{1,0},{2,3},{3,2},{4,5},{5,4},{6,7},{7,6},{8,9},{9,8},{10,11... | collective-permute-start | bytes 589832 | tf_op jit(solution)/shard_map/ppermute | solution.py:202
  48.4 1.7 %collective-permute-start.16 = (f32[384,128]{1,0:T(8,128)S(1)}, f32[384,128]{1,0:T(8,128)S(1)}, u32[]{:S(2)}, u32[]{:S(2)}) collective-permute-start(f32[384,128]{1,0:T(8,128)S(1)} %collective-permute-done.12.rest_10_), channel_id=1, source_target_pairs={{0,1},{1,0},{2,3},{3,2},{4,5},{5,4},{6,7},{7,6},{8,9},{9,8},{10,11... | collective-permute-start | bytes 589832 | tf_op jit(solution)/shard_map/ppermute | solution.py:202
  64.7 16.8 %all-to-all-start.1 = ((f32[16,3,8,128]{3,2,1,0:T(8,128)}), f32[16,3,8,128]{3,2,1,0:T(8,128)S(1)}, u32[]{:S(2)}, u32[]{:S(2)}) async-start(f32[16,3,8,128]{3,2,1,0:T(8,128)} %bitcast.21), calls=%async_computation.1 | async-start | bytes 393216 | tf_op jit(solution)/shard_map/all_to_all | solution.py:263

commit v12 on v11

--- a/solution.py
+++ b/solution.py
@@ -240,7 +240,7 @@
     over = swap(own, "xl")
     again, over, after, before = lax.optimization_barrier((own, over, after, before))
     over_after, over_before = swap(after, "xl"), swap(before, "xl")
-    two, over_two = shift(again, 2), shift(over, 2)
+    two, over_two = shift(after, 1), shift(over, 2)
     (start, after, before, over), over_after = lax.optimization_barrier(
         ((again, after, before, over), over_after)
     )

time: 83.5 us -> 83.2 us (level)
  transfers between devices with their start and end apart: 20 -> 20, of which waited for: 12 -> 15; matrix products, arithmetic and copies ran while one was open for 14% -> 14% of each run, Pallas kernels for 5% -> 5%
where the time goes in v12:
time: 83.2 us; the launch traced here: 82.7 us
  starting transfers between devices  27 us (32%)
  waiting for transfers between devices  24 us (29%)
  Pallas kernels  18.9 us (23%)
  matrix products  9.82 us (12%)
  local copies, waits for them, and re-layouts  1.53 us (2%)
  other arithmetic  1.35 us (2%)
    pallas_call x1, Pallas kernels, mixed_call(): pl.pallas_call(functools.partial(mixed_kernel, n_exc), out_shape=jax.Shap...  14.7 us
    all_to_all x1, starting transfers between devices, per_device(): lax.all_to_all(packed, ('z', 'xh'), split_axis=0, concat_axis=0, tiled=True)  9.88 us
    dot_general x1, matrix products, per_device(): applied = jnp.einsum('rpk,pkl->rpl', picked, beta_blocks, precision=HIGH)  7.45 us
    all_to_all x1, waiting for transfers between devices, per_device(): lax.all_to_all(packed, ('z', 'xh'), split_axis=0, concat_axis=0, tiled=True)  6.8 us
    ppermute x4, starting transfers between devices, shift(): lax.ppermute(value, 'grp', [(i, (i - k) % N_GRP) for i in range(N_GRP)])  6.52 us
    ppermute x4, waiting for transfers between devices, shift(): lax.ppermute(value, 'grp', [(i, (i - k) % N_GRP) for i in range(N_GRP)])  6.41 us
    all_to_all x1, waiting for transfers between devices, per_device(): lax.all_to_all(mixed_local.reshape(NQ, NT, RA, LANES), ('z', 'xh'), split...  5.78 us
    ppermute x11, waiting for transfers between devices, swap(): return lax.ppermute(value, axis, [(0, 1), (1, 0)])  5.03 us
  transfers between devices with their start and end apart: 20, of which 15 were waited for; matrix products, arithmetic and copies ran while one was open for 14% of the time, Pallas kernels for 5%

profile of v12, /device:TPU:2, one launch (start us, length us, event | category | flops | bytes accessed | tf_op | source)
XLA Modules:
  0.0 82.7 jit_solution(1718724718724571246)
XLA Ops:
  0.0 2.4 %collective-permute-start.2 = (s32[18,96]{1,0:T(8,128)}, s32[18,96]{1,0:T(8,128)S(1)}, u32[]{:S(2)}, u32[]{:S(2)}) collective-permute-start(s32[18,96]{1,0:T(8,128)} %param.18), channel_id=1, source_target_pairs={{0,3},{1,2},{2,1},{3,0},{4,7},{5,6},{6,5},{7,4},{8,11},{9,10},{10,... | collective-permute-start | bytes 20744 | tf_op jit(solution)/shard_map/ppermute | solution.py:213
  2.4 0.0 collective-permute-start.1
  2.4 1.7 %pack.1 = f32[16,4,8,128]{3,2,1,0:T(8,128)} custom-call(s32[1]{0:T(128)} %bitcast.g_ref, s32[1,4]{1,0:T(1,128)} %mask_ref.1, f32[8,6144]{1,0:T(8,128)} %x_ref.1, f32[1,4,8,8]{3,2,1,0:T(8,128)} %alpha_ref.1), custom_call_target="tpu_custom_call" | custom-call | tf_op jit(solution)/shard_map/pack/pallas_call | solution.py:43
  4.1 9.9 %all-to-all-start = ((f32[16,4,8,128]{3,2,1,0:T(8,128)}), f32[16,4,8,128]{3,2,1,0:T(8,128)S(1)}, u32[]{:S(2)}, u32[]{:S(2)}) async-start(f32[16,4,8,128]{3,2,1,0:T(8,128)} %pack.1), calls=%async_computation | async-start | bytes 524288 | tf_op jit(solution)/shard_map/all_to_all | solution.py:205
  14.0 0.8 slice_bitcast_fusion
  14.8 1.3 %convolution_bitcast_fusion.1 = f32[8,96,128]{2,1,0:T(8,128)S(1)} fusion(f32[8,48,128]{2,0,1:T(8,128)} %bitcast.61, s32[96]{0:T(128)S(1)} %get-tuple-element.42), kind=kOutput, calls=%fused_computation.1 | convolution fusion | flops 56627712 | bytes 590208 | tf_op jit(solution)/shard_map/rnk,pn->rpk/dot_general | solution.py:234
  16.1 0.6 pad_add_fusion.1.place_ref
  16.6 2.5 %prep.1 = (s32[96,128]{1,0:T(8,128)}, s32[96,128]{1,0:T(8,128)}) custom-call(s32[2]{0:T(128)} %pad_add_fusion.1.place_ref, s32[90,512]{1,0:T(8,128)} %src_ref.1, s32[90,512]{1,0:T(8,128)} %pair_ref.1, s32[90,512]{1,0:T(8,128)} %par_ref.1), custom_call_target="tpu_custom_call" | custom-call | tf_op jit(solution)/shard_map/prep/pallas_call | solution.py:81
  19.2 0.0 collective-permute-done.2
  19.2 0.0 collective-permute-done.1
  19.2 0.7 pad_add_fusion
  19.9 0.8 fusion.24
  20.7 0.1 pad_maximum_fusion
  20.8 6.8 %all-to-all-done.mix_ref = f32[16,4,8,128]{3,2,1,0:T(8,128)S(1)} async-done(((f32[16,4,8,128]{3,2,1,0:T(8,128)}), f32[16,4,8,128]{3,2,1,0:T(8,128)S(1)}, u32[]{:S(2)}, u32[]{:S(2)}) %all-to-all-start) | async-done | bytes 262176 | tf_op jit(solution)/shard_map/all_to_all | solution.py:205
  27.6 1.7 %collective-permute-start.5 = (f32[384,128]{1,0:T(8,128)S(1)}, f32[384,128]{1,0:T(8,128)S(1)}, u32[]{:S(2)}, u32[]{:S(2)}) collective-permute-start(f32[384,128]{1,0:T(8,128)S(1)} %bitcast.55), channel_id=1, source_target_pairs={{0,64},{64,128},{128,192},{192,0},{1,65},{65,129},{129,193},{193,1... | collective-permute-start | bytes 589832 | tf_op jit(solution)/shard_map/ppermute | solution.py:197
  29.2 1.7 %collective-permute-start.4 = (f32[384,128]{1,0:T(8,128)S(1)}, f32[384,128]{1,0:T(8,128)S(1)}, u32[]{:S(2)}, u32[]{:S(2)}) collective-permute-start(f32[384,128]{1,0:T(8,128)S(1)} %bitcast.56), channel_id=1, source_target_pairs={{0,192},{64,0},{128,64},{192,128},{1,193},{65,1},{129,65},{193,129... | collective-permute-start | bytes 589832 | tf_op jit(solution)/shard_map/ppermute | solution.py:197
  30.9 1.4 %collective-permute-start.3 = (f32[384,128]{1,0:T(8,128)S(1)}, f32[384,128]{1,0:T(8,128)S(1)}, u32[]{:S(2)}, u32[]{:S(2)}) collective-permute-start(f32[384,128]{1,0:T(8,128)S(1)} %bitcast.57), channel_id=1, source_target_pairs={{0,2},{2,0},{1,3},{3,1},{4,6},{6,4},{5,7},{7,5},{8,10},{10,8},{9,1... | collective-permute-start | bytes 589832 | tf_op jit(solution)/shard_map/ppermute | solution.py:202
  32.3 2.2 %collective-permute-done.5.rest_3_ = f32[384,128]{1,0:T(8,128)S(1)} collective-permute-done((f32[384,128]{1,0:T(8,128)S(1)}, f32[384,128]{1,0:T(8,128)S(1)}, u32[]{:S(2)}, u32[]{:S(2)}) %collective-permute-start.5) | collective-permute-done | bytes 196640 | tf_op jit(solution)/shard_map/ppermute | solution.py:197
  34.6 0.4 collective-permute-done.4.rest_1_
  34.9 2.4 %collective-permute-done.3.rest_8_ = f32[384,128]{1,0:T(8,128)S(1)} collective-permute-done((f32[384,128]{1,0:T(8,128)S(1)}, f32[384,128]{1,0:T(8,128)S(1)}, u32[]{:S(2)}, u32[]{:S(2)}) %collective-permute-start.3) | collective-permute-done | bytes 196640 | tf_op jit(solution)/shard_map/ppermute | solution.py:202
  37.3 1.4 %collective-permute-start.13 = (f32[384,128]{1,0:T(8,128)S(1)}, f32[384,128]{1,0:T(8,128)S(1)}, u32[]{:S(2)}, u32[]{:S(2)}) collective-permute-start(f32[384,128]{1,0:T(8,128)S(1)} %collective-permute-done.5.rest_3_), channel_id=1, source_target_pairs={{0,2},{2,0},{1,3},{3,1},{4,6},{6,4},{5,7},{7,5},{8,10},{10,8},{9,1... | collective-permute-start | bytes 589832 | tf_op jit(solution)/shard_map/ppermute | solution.py:202
  38.8 2.2 %collective-permute-start.12 = (f32[384,128]{1,0:T(8,128)S(1)}, f32[384,128]{1,0:T(8,128)S(1)}, u32[]{:S(2)}, u32[]{:S(2)}) collective-permute-start(f32[384,128]{1,0:T(8,128)S(1)} %collective-permute-done.3.rest_8_), channel_id=1, source_target_pairs={{0,128},{64,192},{128,0},{192,64},{1,129},{65,193},{129,1},{193,65... | collective-permute-start | bytes 589832 | tf_op jit(solution)/shard_map/ppermute | solution.py:197
  40.9 1.1 %collective-permute-start.7 = (f32[384,128]{1,0:T(8,128)S(1)}, f32[384,128]{1,0:T(8,128)S(1)}, u32[]{:S(2)}, u32[]{:S(2)}) collective-permute-start(f32[384,128]{1,0:T(8,128)S(1)} %collective-permute-done.4.rest_1_), channel_id=1, source_target_pairs={{0,192},{64,0},{128,64},{192,128},{1,193},{65,1},{129,65},{193,129... | collective-permute-start | bytes 589832 | tf_op jit(solution)/shard_map/ppermute | solution.py:197
  42.0 0.6 collective-permute-start.6
  42.6 0.9 %collective-permute-done.13.rest_11_ = f32[384,128]{1,0:T(8,128)S(1)} collective-permute-done((f32[384,128]{1,0:T(8,128)S(1)}, f32[384,128]{1,0:T(8,128)S(1)}, u32[]{:S(2)}, u32[]{:S(2)}) %collective-permute-start.13) | collective-permute-done | bytes 196640 | tf_op jit(solution)/shard_map/ppermute | solution.py:202
  43.5 0.0 collective-permute-start.17
  43.5 2.4 %collective-permute-done.12.rest_10_ = f32[384,128]{1,0:T(8,128)S(1)} collective-permute-done((f32[384,128]{1,0:T(8,128)S(1)}, f32[384,128]{1,0:T(8,128)S(1)}, u32[]{:S(2)}, u32[]{:S(2)}) %collective-permute-start.12) | collective-permute-done | bytes 196640 | tf_op jit(solution)/shard_map/ppermute | solution.py:197
  45.9 0.0 collective-permute-start.16
  45.9 1.4 %collective-permute-done.7.rest_2_ = f32[384,128]{1,0:T(8,128)S(1)} collective-permute-done((f32[384,128]{1,0:T(8,128)S(1)}, f32[384,128]{1,0:T(8,128)S(1)}, u32[]{:S(2)}, u32[]{:S(2)}) %collective-permute-start.7) | collective-permute-done | bytes 196640 | tf_op jit(solution)/shard_map/ppermute | solution.py:197
  47.3 0.0 collective-permute-start.10
  47.3 0.3 collective-permute-done.6.rest_9_
  47.6 0.2 collective-permute-start.8
  47.9 0.3 collective-permute-start.9
  48.1 0.2 collective-permute-start.11
  48.4 0.3 collective-permute-start.14
  48.7 0.1 collective-permute-done.10.rest_6_
  48.8 0.2 collective-permute-start.15
  48.9 0.1 collective-permute-done.8.rest_4_
  49.1 0.3 collective-permute-done.9.rest_5_
  49.4 0.3 collective-permute-done.11.rest_7_
  49.6 0.3 collective-permute-done.14.rest_12_
  49.9 0.3 collective-permute-done.15.rest_13_
  50.2 14.7 %mixed.1 = f32[384,128]{1,0:T(8,128)} custom-call(s32[12288]{0:T(1024)} %bitcast.62, s32[12288]{0:T(1024)} %bitcast.63, f32[1944,128]{1,0:T(8,128)S(1)} %bitcast.54, f32[16,4,8,128]{3,2,1,0:T(8,128)S(1)} %all-to-all-done.mix_ref, f32[384,128]{1,0:T(8,128)S(1)} %bitcast.59, f32[384,128]{1,0:T(8,128)S(1)} %collective-permute-done.4.rest_1_, ...), custom_call_target="tpu_custom_call" | custom-call | flops 8847360 | bytes 8388608 | tf_op jit(solution)/shard_map/mixed/pallas_call | solution.py:156
  64.9 3.5 %all-to-all-start.1 = ((f32[16,3,8,128]{3,2,1,0:T(8,128)}), f32[16,3,8,128]{3,2,1,0:T(8,128)S(1)}, u32[]{:S(2)}, u32[]{:S(2)}) async-start(f32[16,3,8,128]{3,2,1,0:T(8,128)} %bitcast.21), calls=%async_computation.1 | async-start | bytes 393216 | tf_op jit(solution)/shard_map/all_to_all | solution.py:263
  68.4 7.5 %fusion.3 = f32[96,8,128]{2,1,0:T(8,128)S(1)} fusion(f32[96,128,128]{2,1,0:T(8,128)} %param.11, f32[8,96,128]{2,1,0:T(8,128)S(1)} %convolution_bitcast_fusion.1), kind=kOutput, calls=%fused_computation.6 | convolution fusion | flops 150994944 | bytes 7077888 | tf_op jit(solution)/shard_map/rpk,pkl->rpl/dot_general | solution.py:274
  75.9 5.8 %all-to-all-done.1 = f32[16,3,8,128]{3,2,1,0:T(8,128)S(1)} async-done(((f32[16,3,8,128]{3,2,1,0:T(8,128)}), f32[16,3,8,128]{3,2,1,0:T(8,128)S(1)}, u32[]{:S(2)}, u32[]{:S(2)}) %all-to-all-start.1) | async-done | bytes 196640 | tf_op jit(solution)/shard_map/all_to_all | solution.py:263
  81.7 0.3 fusion.5
  82.0 0.7 copy.32
  (8 shorter events, 0.0 us)
Async XLA Ops:
  0.0 19.9 %copy-start = (f32[324,18]{0,1:T(8,128)S(1)}, f32[324,18]{0,1:T(8,128)}, u32[]{:S(2)}) copy-start(f32[324,18]{0,1:T(8,128)} %param.19) | copy-start | bytes 69988
  0.0 19.2 %collective-permute-start = (s32[18,96]{1,0:T(8,128)}, s32[18,96]{1,0:T(8,128)S(1)}, u32[]{:S(2)}, u32[]{:S(2)}) collective-permute-start(s32[18,96]{1,0:T(8,128)} %param.18), channel_id=1, source_target_pairs={{0,1},{1,0},{2,3},{3,2},{4,5},{5,4},{6,7},{7,6},{8,9},{9,8},{10,11... | collective-permute-start | bytes 20744 | tf_op jit(solution)/shard_map/ppermute | solution.py:213
  0.0 19.2 %collective-permute-start.2 = (s32[18,96]{1,0:T(8,128)}, s32[18,96]{1,0:T(8,128)S(1)}, u32[]{:S(2)}, u32[]{:S(2)}) collective-permute-start(s32[18,96]{1,0:T(8,128)} %param.18), channel_id=1, source_target_pairs={{0,3},{1,2},{2,1},{3,0},{4,7},{5,6},{6,5},{7,4},{8,11},{9,10},{10,... | collective-permute-start | bytes 20744 | tf_op jit(solution)/shard_map/ppermute | solution.py:213
  2.4 16.8 %collective-permute-start.1 = (s32[18,96]{1,0:T(8,128)}, s32[18,96]{1,0:T(8,128)S(1)}, u32[]{:S(2)}, u32[]{:S(2)}) collective-permute-start(s32[18,96]{1,0:T(8,128)} %param.18), channel_id=1, source_target_pairs={{0,2},{1,3},{2,0},{3,1},{4,6},{5,7},{6,4},{7,5},{8,10},{9,11},{10,... | collective-permute-start | bytes 20744 | tf_op jit(solution)/shard_map/ppermute | solution.py:213
  4.1 23.4 %all-to-all-start = ((f32[16,4,8,128]{3,2,1,0:T(8,128)}), f32[16,4,8,128]{3,2,1,0:T(8,128)S(1)}, u32[]{:S(2)}, u32[]{:S(2)}) async-start(f32[16,4,8,128]{3,2,1,0:T(8,128)} %pack.1), calls=%async_computation | async-start | bytes 524288 | tf_op jit(solution)/shard_map/all_to_all | solution.py:205
  27.6 7.0 %collective-permute-start.5 = (f32[384,128]{1,0:T(8,128)S(1)}, f32[384,128]{1,0:T(8,128)S(1)}, u32[]{:S(2)}, u32[]{:S(2)}) collective-permute-start(f32[384,128]{1,0:T(8,128)S(1)} %bitcast.55), channel_id=1, source_target_pairs={{0,64},{64,128},{128,192},{192,0},{1,65},{65,129},{129,193},{193,1... | collective-permute-start | bytes 589832 | tf_op jit(solution)/shard_map/ppermute | solution.py:197
  29.2 5.7 %collective-permute-start.4 = (f32[384,128]{1,0:T(8,128)S(1)}, f32[384,128]{1,0:T(8,128)S(1)}, u32[]{:S(2)}, u32[]{:S(2)}) collective-permute-start(f32[384,128]{1,0:T(8,128)S(1)} %bitcast.56), channel_id=1, source_target_pairs={{0,192},{64,0},{128,64},{192,128},{1,193},{65,1},{129,65},{193,129... | collective-permute-start | bytes 589832 | tf_op jit(solution)/shard_map/ppermute | solution.py:197
  30.9 6.4 %collective-permute-start.3 = (f32[384,128]{1,0:T(8,128)S(1)}, f32[384,128]{1,0:T(8,128)S(1)}, u32[]{:S(2)}, u32[]{:S(2)}) collective-permute-start(f32[384,128]{1,0:T(8,128)S(1)} %bitcast.57), channel_id=1, source_target_pairs={{0,2},{2,0},{1,3},{3,1},{4,6},{6,4},{5,7},{7,5},{8,10},{10,8},{9,1... | collective-permute-start | bytes 589832 | tf_op jit(solution)/shard_map/ppermute | solution.py:202
  37.3 6.2 %collective-permute-start.13 = (f32[384,128]{1,0:T(8,128)S(1)}, f32[384,128]{1,0:T(8,128)S(1)}, u32[]{:S(2)}, u32[]{:S(2)}) collective-permute-start(f32[384,128]{1,0:T(8,128)S(1)} %collective-permute-done.5.rest_3_), channel_id=1, source_target_pairs={{0,2},{2,0},{1,3},{3,1},{4,6},{6,4},{5,7},{7,5},{8,10},{10,8},{9,1... | collective-permute-start | bytes 589832 | tf_op jit(solution)/shard_map/ppermute | solution.py:202
  38.8 7.2 %collective-permute-start.12 = (f32[384,128]{1,0:T(8,128)S(1)}, f32[384,128]{1,0:T(8,128)S(1)}, u32[]{:S(2)}, u32[]{:S(2)}) collective-permute-start(f32[384,128]{1,0:T(8,128)S(1)} %collective-permute-done.3.rest_8_), channel_id=1, source_target_pairs={{0,128},{64,192},{128,0},{192,64},{1,129},{65,193},{129,1},{193,65... | collective-permute-start | bytes 589832 | tf_op jit(solution)/shard_map/ppermute | solution.py:197
  40.9 6.4 %collective-permute-start.7 = (f32[384,128]{1,0:T(8,128)S(1)}, f32[384,128]{1,0:T(8,128)S(1)}, u32[]{:S(2)}, u32[]{:S(2)}) collective-permute-start(f32[384,128]{1,0:T(8,128)S(1)} %collective-permute-done.4.rest_1_), channel_id=1, source_target_pairs={{0,192},{64,0},{128,64},{192,128},{1,193},{65,1},{129,65},{193,129... | collective-permute-start | bytes 589832 | tf_op jit(solution)/shard_map/ppermute | solution.py:197
  42.0 5.7 %collective-permute-start.6 = (f32[384,128]{1,0:T(8,128)S(1)}, f32[384,128]{1,0:T(8,128)S(1)}, u32[]{:S(2)}, u32[]{:S(2)}) collective-permute-start(f32[384,128]{1,0:T(8,128)S(1)} %collective-permute-done.4.rest_1_), channel_id=1, source_target_pairs={{0,2},{2,0},{1,3},{3,1},{4,6},{6,4},{5,7},{7,5},{8,10},{10,8},{9,1... | collective-permute-start | bytes 589832 | tf_op jit(solution)/shard_map/ppermute | solution.py:202
  43.5 4.7 %collective-permute-start.17 = (f32[384,128]{1,0:T(8,128)S(1)}, f32[384,128]{1,0:T(8,128)S(1)}, u32[]{:S(2)}, u32[]{:S(2)}) collective-permute-start(f32[384,128]{1,0:T(8,128)S(1)} %collective-permute-done.13.rest_11_), channel_id=1, source_target_pairs={{0,1},{1,0},{2,3},{3,2},{4,5},{5,4},{6,7},{7,6},{8,9},{9,8},{10,11... | collective-permute-start | bytes 589832 | tf_op jit(solution)/shard_map/ppermute | solution.py:202
  45.9 2.4 %collective-permute-start.16 = (f32[384,128]{1,0:T(8,128)S(1)}, f32[384,128]{1,0:T(8,128)S(1)}, u32[]{:S(2)}, u32[]{:S(2)}) collective-permute-start(f32[384,128]{1,0:T(8,128)S(1)} %collective-permute-done.12.rest_10_), channel_id=1, source_target_pairs={{0,1},{1,0},{2,3},{3,2},{4,5},{5,4},{6,7},{7,6},{8,9},{9,8},{10,11... | collective-permute-start | bytes 589832 | tf_op jit(solution)/shard_map/ppermute | solution.py:202
  47.3 1.4 %collective-permute-start.10 = (f32[384,128]{1,0:T(8,128)S(1)}, f32[384,128]{1,0:T(8,128)S(1)}, u32[]{:S(2)}, u32[]{:S(2)}) collective-permute-start(f32[384,128]{1,0:T(8,128)S(1)} %collective-permute-done.7.rest_2_), channel_id=1, source_target_pairs={{0,1},{1,0},{2,3},{3,2},{4,5},{5,4},{6,7},{7,6},{8,9},{9,8},{10,11... | collective-permute-start | bytes 589832 | tf_op jit(solution)/shard_map/ppermute | solution.py:202
  47.6 1.4 %collective-permute-start.8 = (f32[384,128]{1,0:T(8,128)S(1)}, f32[384,128]{1,0:T(8,128)S(1)}, u32[]{:S(2)}, u32[]{:S(2)}) collective-permute-start(f32[384,128]{1,0:T(8,128)S(1)} %bitcast.58), channel_id=1, source_target_pairs={{0,1},{1,0},{2,3},{3,2},{4,5},{5,4},{6,7},{7,6},{8,9},{9,8},{10,11... | collective-permute-start | bytes 589832 | tf_op jit(solution)/shard_map/ppermute | solution.py:202
  47.9 1.5 %collective-permute-start.9 = (f32[384,128]{1,0:T(8,128)S(1)}, f32[384,128]{1,0:T(8,128)S(1)}, u32[]{:S(2)}, u32[]{:S(2)}) collective-permute-start(f32[384,128]{1,0:T(8,128)S(1)} %collective-permute-done.4.rest_1_), channel_id=1, source_target_pairs={{0,1},{1,0},{2,3},{3,2},{4,5},{5,4},{6,7},{7,6},{8,9},{9,8},{10,11... | collective-permute-start | bytes 589832 | tf_op jit(solution)/shard_map/ppermute | solution.py:202
  48.1 1.5 %collective-permute-start.11 = (f32[384,128]{1,0:T(8,128)S(1)}, f32[384,128]{1,0:T(8,128)S(1)}, u32[]{:S(2)}, u32[]{:S(2)}) collective-permute-start(f32[384,128]{1,0:T(8,128)S(1)} %collective-permute-done.5.rest_3_), channel_id=1, source_target_pairs={{0,1},{1,0},{2,3},{3,2},{4,5},{5,4},{6,7},{7,6},{8,9},{9,8},{10,11... | collective-permute-start | bytes 589832 | tf_op jit(solution)/shard_map/ppermute | solution.py:202
  48.4 1.5 %collective-permute-start.14 = (f32[384,128]{1,0:T(8,128)S(1)}, f32[384,128]{1,0:T(8,128)S(1)}, u32[]{:S(2)}, u32[]{:S(2)}) collective-permute-start(f32[384,128]{1,0:T(8,128)S(1)} %collective-permute-done.3.rest_8_), channel_id=1, source_target_pairs={{0,1},{1,0},{2,3},{3,2},{4,5},{5,4},{6,7},{7,6},{8,9},{9,8},{10,11... | collective-permute-start | bytes 589832 | tf_op jit(solution)/shard_map/ppermute | solution.py:202
  48.8 1.4 %collective-permute-start.15 = (f32[384,128]{1,0:T(8,128)S(1)}, f32[384,128]{1,0:T(8,128)S(1)}, u32[]{:S(2)}, u32[]{:S(2)}) collective-permute-start(f32[384,128]{1,0:T(8,128)S(1)} %collective-permute-done.6.rest_9_), channel_id=1, source_target_pairs={{0,1},{1,0},{2,3},{3,2},{4,5},{5,4},{6,7},{7,6},{8,9},{9,8},{10,11... | collective-permute-start | bytes 589832 | tf_op jit(solution)/shard_map/ppermute | solution.py:202
  64.9 16.8 %all-to-all-start.1 = ((f32[16,3,8,128]{3,2,1,0:T(8,128)}), f32[16,3,8,128]{3,2,1,0:T(8,128)S(1)}, u32[]{:S(2)}, u32[]{:S(2)}) async-start(f32[16,3,8,128]{3,2,1,0:T(8,128)} %bitcast.21), calls=%async_computation.1 | async-start | bytes 393216 | tf_op jit(solution)/shard_map/all_to_all | solution.py:263
